TPU v7x, 32 devices: a whole 2x2x4 slice. The times are simulated.
32 devices in a mesh: obs: 8 (over z, y), cell: 4 (over x, core).
Axes of the slice: x: 2, y: 2, z: 4, core: 2. Of those that a mesh axis runs over, the one named last changes fastest.
Arguments:
- footprint: bfloat16 [512, 16, 4096], P('obs', None, 'cell'), may hold values from -0.75 to 0.75
- block_mask: int32 [512, 32], P('obs', 'cell'), may hold values 0 or 1
- cell_coords: int32 [2, 4096], P(None, 'cell'), may hold values from 0 to 63, as said below
- cell_sigma: float32 [4096], P('cell'), may hold values from 0.3 to 3
- time_cov: float32 [16, 16], replicated, as said below
- error_var: float32 [512], P('obs'), may hold values from 0.3 to 300
- panel_index: int32 [128], replicated, may hold values from 0 to 511, as said below
Outputs:
- cov_product: bfloat16 [512, 16, 4096], P('obs', None, 'cell')
- innovation_panel: float32 [512, 128], P('obs')
Inputs may be any that keep to these rules, and one draw needn't show every extreme that they name: `cell_coords`: each cell holds a distinct point of the 64 by 64 grid, and every point is held by some cell. `time_cov`: Symmetric. `panel_index`: entries are distinct; entries k * 16 to (k + 1) * 16 - 1 name observations among rows k * 64 to (k + 1) * 64 - 1.
All inputs are finite; a program needn't handle non-finite values. No bound on the sum of `block_mask` on one device may be relied on, other than what follows from the above.
Results may differ from a plain program's by a relative error of at most 0.0049.
Values may be sent and summed in bfloat16 or wider, within the bound.
No kernel may reach another device: no remote copies, remote signals or barrier semaphores. Data moves between devices by JAX's collectives and lax.ppermute only.
A program may use at most 64 MiB of HBM per device.

v0:
```python
import functools
import math

import jax
import jax.numpy as jnp
from jax import lax
from jax.experimental import pallas as pl
from jax.experimental.pallas import tpu as pltpu
from jax.sharding import PartitionSpec as P


GRID = 64
LENGTH = GRID / 16.0
F32, BF16, I32 = jnp.float32, jnp.bfloat16, jnp.int32
SHIFT = 4
INFO = 8


VMEM = pl.BlockSpec(memory_space=pltpu.VMEM)
SMEM = pl.BlockSpec(memory_space=pltpu.SMEM)
ANY = pl.BlockSpec(memory_space=pl.ANY)
HBM = pl.BlockSpec(memory_space=pltpu.HBM)


def shape_of(shape, dtype):
    return jax.ShapeDtypeStruct(shape, dtype)


def params(mib):
    return pltpu.CompilerParams(vmem_limit_bytes=mib * 2**20)


def cost(micros):
    return pl.CostEstimate(flops=int(micros * 9e8), bytes_accessed=1_000_000, transcendentals=0)


def aligned(start, size):
    return pl.ds(pl.multiple_of(start, size), size)


def slot_count(tiles, extra):
    room = tiles / 2 + 4.1 * math.sqrt(tiles / 4)
    return extra + min(tiles + 1, 2 * math.ceil(room / 2) + 1)


def pack_rows(mask_at, feet_at, begin, end, blocks, buf, carry):
    slots, _, lanes = buf.shape
    row_of = lax.broadcasted_iota(I32, (8, lanes), 0)
    lane_of = lax.broadcasted_iota(I32, (8, lanes), 1)
    flat = row_of * lanes + lane_of
    batch = math.gcd(2, end - begin)

    def some(i, carry):
        pos, head, ends = carry
        first = begin + i * batch
        tiles = [[feet_at(first + j, b) for b in range(blocks)] for j in range(batch)]
        kept = [[mask_at(first + j, b) for b in range(blocks)] for j in range(batch)]
        for j in range(batch):
            for b in range(blocks):
                buf[jnp.minimum(pos, slots - 1)] = tiles[j][b]
                head = jnp.where(flat == (first + j) * blocks + b, kept[j][b] * pos, head)
                pos = pos + kept[j][b]
            ends = jnp.where(lane_of == first + j, pos, ends)
        return pos, head, ends

    return lax.fori_loop(0, (end - begin) // batch, some, carry)


def no_rows(first, lanes):
    zeros = jnp.zeros((8, lanes), I32)
    return jnp.int32(first), zeros, zeros


def write_head(carry, rows, blocks, buf, head_v, flag=None):
    lanes = buf.shape[2]
    deep = -(-rows * blocks // lanes)
    _, head, ends = carry
    low = (1 << SHIFT) - 1
    head_v[...] = jnp.zeros_like(head_v)
    head_v[0:deep, :] = (head >> SHIFT)[0:deep].astype(F32)
    head_v[deep : 2 * deep, :] = (head & low)[0:deep].astype(F32)
    head_v[2 * deep : 2 * deep + 1, :] = (ends >> SHIFT)[0:1].astype(F32)
    head_v[2 * deep + 1 : 2 * deep + 2, :] = (ends & low)[0:1].astype(F32)
    if flag is not None:
        head_v[2 * deep + 2 : 2 * deep + 3, :] = jnp.broadcast_to(flag, (1, lanes)).astype(F32)
    buf[0] = head_v[...].astype(BF16)


def pack_feet_kernel(chunks, mask_ref, coords_hbm, sigma_hbm, feet_ref, *rest):
    outs, (coords_ref, sigma_ref, feet, buf, head_v, small_sem, in_sem, sem) = (
        rest[: len(chunks)],
        rest[len(chunks) :],
    )
    blocks, rows = mask_ref.shape
    small = [
        pltpu.make_async_copy(src, dst, small_sem.at[k])
        for k, (src, dst) in enumerate(((coords_hbm, coords_ref), (sigma_hbm, sigma_ref)))
    ]
    for copy in small:
        copy.start()
    times, lanes = buf.shape[1:]
    groups = in_sem.shape[0]
    each = rows // groups
    loads = [
        pltpu.make_async_copy(feet_ref.at[pl.ds(g * each, each)], feet.at[pl.ds(g * each, each)], in_sem.at[g])
        for g in range(groups)
    ]
    for load in loads:
        load.start()
    for copy in small:
        copy.wait()
    sigma = sigma_ref[...]
    high = sigma.astype(BF16).astype(F32)
    middle = (sigma - high).astype(BF16).astype(F32)
    lowest = sigma - high - middle
    at = lax.broadcasted_iota(I32, (times, sigma.shape[1]), 0)
    info = jnp.zeros(at.shape, F32)
    for k, row in enumerate((coords_ref[0:1, :].astype(F32), coords_ref[1:2, :].astype(F32), high, middle, lowest)):
        info = jnp.where(at == k, row, info)
    info = info.astype(BF16)
    for b in range(blocks):
        buf[1 + b] = info[:, b * lanes : (b + 1) * lanes]
    carry = no_rows(1 + blocks, lanes)
    for g in range(groups):
        loads[g].wait()
        carry = pack_rows(
            lambda o, b: mask_ref[b, o],
            lambda o, b: feet[o, :, b * lanes : (b + 1) * lanes],
            g * each,
            (g + 1) * each,
            blocks,
            buf,
            carry,
        )
    write_head(carry, rows, blocks, buf, head_v)
    copies, first = [], 0
    for k, size in enumerate(chunks):
        copies.append(pltpu.make_async_copy(buf.at[pl.ds(first, size)], outs[k], sem.at[k]))
        first += size
    for copy in copies:
        copy.start()
    for copy in copies:
        copy.wait()


def pack_feet(mask, coords, sigma, feet, chunks):
    rows, times, cells = feet.shape
    lanes = cells // mask.shape[0]
    groups = math.gcd(4, rows)
    return pl.pallas_call(
        functools.partial(pack_feet_kernel, chunks),
        out_shape=tuple(shape_of((size, times, lanes), BF16) for size in chunks),
        in_specs=[SMEM, HBM, HBM, HBM],
        out_specs=(ANY,) * len(chunks),
        scratch_shapes=[
            pltpu.VMEM(coords.shape, I32),
            pltpu.VMEM(sigma.shape, F32),
            pltpu.VMEM((rows, times, cells), BF16),
            pltpu.VMEM((sum(chunks), times, lanes), BF16),
            pltpu.VMEM((times, lanes), F32),
            pltpu.SemaphoreType.DMA((2,)),
            pltpu.SemaphoreType.DMA((groups,)),
            pltpu.SemaphoreType.DMA((len(chunks),)),
        ],
        compiler_params=params(12),
        cost_estimate=cost(3),
        name="pack_feet",
    )(mask, coords, sigma, feet)


def pack_panel_kernel(room, mask_ref, mask_hbm, index_hbm, group_ref, feet_ref, out_ref, mask_v, index_ref, rows_buf, head_v, small_sem, sem):
    count = rows_buf.shape[0]
    blocks, obs = mask_ref.shape
    lanes = out_ref.shape[2]
    small = [
        pltpu.make_async_copy(src, dst, small_sem.at[k])
        for k, (src, dst) in enumerate(((index_hbm, index_ref), (mask_hbm, mask_v)))
    ]
    for copy in small:
        copy.start()
    base = group_ref[0]
    small[0].wait()
    rows = [jnp.clip(index_ref[base * count + j] - base * obs, 0, obs - 1) for j in range(count)]
    copies = [pltpu.make_async_copy(feet_ref.at[rows[j]], rows_buf.at[j], sem.at[j]) for j in range(count)]
    for copy in copies:
        copy.start()
    for copy in small[1:]:
        copy.wait()
    flag = (jnp.sum(mask_v[...].astype(F32), axis=(0, 1), keepdims=True) > room).astype(I32)
    for copy in copies:
        copy.wait()

    def mask_at(o, b):
        return mask_ref[b, jnp.clip(index_ref[base * count + o] - base * obs, 0, obs - 1)]

    carry = pack_rows(
        mask_at, lambda o, b: rows_buf[o, :, b * lanes : (b + 1) * lanes], 0, count, blocks, out_ref, no_rows(1, lanes)
    )
    write_head(carry, count, blocks, out_ref, head_v, flag)


def pack_panel(mask, panel_index, group, feet, count, slots, room):
    _, times, cells = feet.shape
    lanes = cells // mask.shape[0]
    return pl.pallas_call(
        functools.partial(pack_panel_kernel, room),
        out_shape=shape_of((slots, times, lanes), BF16),
        in_specs=[SMEM, HBM, HBM, SMEM, HBM],
        out_specs=VMEM,
        scratch_shapes=[
            pltpu.VMEM(mask.shape, I32),
            pltpu.SMEM(panel_index.shape, I32),
            pltpu.VMEM((count, times, cells), BF16),
            pltpu.VMEM((times, lanes), F32),
            pltpu.SemaphoreType.DMA((2,)),
            pltpu.SemaphoreType.DMA((count,)),
        ],
        compiler_params=params(8),
        cost_estimate=cost(2),
        name="pack_panel",
    )(mask, mask, panel_index, group[None], feet)


def fetch(chunks, buf, sem):
    copies, first = [], 0
    for k, chunk in enumerate(chunks):
        copies.append(pltpu.make_async_copy(chunk, buf.at[pl.ds(first, chunk.shape[0])], sem.at[k]))
        copies[-1].start()
        first += chunk.shape[0]
    return copies


def read_head(buf, rows, blocks, bits_v, flagged=False):
    slots, _, lanes = buf.shape
    deep = -(-rows * blocks // lanes)
    head = buf[0].astype(F32)
    scale = float(1 << SHIFT)
    bits_v[0:deep, :] = jnp.minimum(head[0:deep] * scale + head[deep : 2 * deep], slots - 1.0).astype(I32)
    bits_v[deep : deep + 1, :] = (head[2 * deep : 2 * deep + 1] * scale + head[2 * deep + 1 : 2 * deep + 2]).astype(I32)
    if flagged:
        bits_v[deep + 1 : deep + 2, :] = head[2 * deep + 2 : 2 * deep + 3].astype(I32)
    buf[0] = jnp.zeros(buf.shape[1:], buf.dtype)


def copy_in(src, dst, sem):
    copy = pltpu.make_async_copy(src, dst, sem)
    copy.start()
    copy.wait()


def expand(buf, bits, first, count, blocks, store, unrolled=False):
    lanes = buf.shape[2]
    batch = math.gcd(2, count)

    def some(i, _):
        tiles = []
        for j in range(batch):
            base = (first + i * batch + j) * blocks
            row, col = lax.div(base, lanes), lax.rem(base, lanes)
            tiles += [buf[bits[row, col + b]] for b in range(blocks)]
        for j in range(batch):
            for b in range(blocks):
                store(i * batch + j, b, tiles[j * blocks + b])
        return 0

    if unrolled:
        for i in range(count // batch):
            some(i, 0)
    else:
        lax.fori_loop(0, count // batch, some, 0)


def into(dense, times, lanes, offset, first=0):
    def store(i, b, tile):
        at = aligned((first + i) * times, times)
        dense[at, offset + b * lanes : offset + (b + 1) * lanes] = tile.astype(dense.dtype)

    return store


def read_info(buf, blocks, row_v, turned):
    _, lanes = buf.shape[1:]
    for b in range(blocks):
        tile = buf[1 + b].astype(F32)[0:INFO]
        sigma = tile[2:3] + tile[3:4] + tile[4:5]
        tile = jnp.where(lax.broadcasted_iota(I32, tile.shape, 0) == 2, sigma, tile)
        at = slice(b * lanes, (b + 1) * lanes)
        if row_v is not None:
            row_v[:, at] = tile
        if turned is not None:
            turned[at, :] = tile.T


def fill_covariance(dst, dst_first, src_first, rows, turned, own):
    x, y, s = own[0:1, :], own[1:2, :], own[2:3, :]
    step = min(32, rows)
    for i in range(rows // step):
        at = aligned(src_first + i * step, step)
        dx = turned[at, 0:1] - x
        dy = turned[at, 1:2] - y
        square = dx * dx + dy * dy + 1.0
        decay = jnp.exp(square * lax.rsqrt(square) * (-1.0 / LENGTH))
        dst[aligned(dst_first + i * step, step), :] = (decay * (turned[at, 2:3] * s)).astype(BF16)


def own_kernel(chunks, *refs):
    msgs = refs[:chunks], refs[chunks : 2 * chunks]
    out_ref, mate_dense, next_ref, info_ref = refs[2 * chunks : 2 * chunks + 4]
    bufs, bits_v, bits_s, dense, cov, turned, sem = refs[2 * chunks + 4 :]
    times, lanes = bufs.shape[2:]
    cells = cov.shape[1]
    blocks = cells // lanes
    rows = dense.shape[0] // times
    tall = min(256, rows * times)
    steps = rows * times // tall
    part = cells // steps
    copies = [fetch(msg, bufs.at[k], sem.at[k]) for k, msg in enumerate(msgs)]
    for k in range(2):
        for copy in copies[k]:
            copy.wait()
        read_info(bufs.at[k], blocks, None if k else info_ref, turned.at[k])
        read_head(bufs.at[k], rows, blocks, bits_v.at[k])
    copy_in(bits_v, bits_s, sem.at[2, 0])
    fine = math.gcd(8, rows // 2)
    piece = cells // fine

    @pl.loop(0, fine)
    def _(i):
        fill_covariance(cov, i * piece, i * piece, piece, turned.at[0], info_ref)
        some = rows // fine
        expand(bufs.at[0], bits_s.at[0], i * some, some, blocks, into(dense, times, lanes, 0, i * some), unrolled=True)

    @pl.loop(0, steps)
    def _(u):
        here = aligned(u * tall, tall)
        fill_covariance(next_ref, u * part, u * part, part, turned.at[1], info_ref)
        out_ref[here, :] = jnp.dot(dense[here, :], cov[...], preferred_element_type=F32)
        some = rows // steps
        expand(bufs.at[1], bits_s.at[1], u * some, some, blocks, into(mate_dense, times, lanes, 0, u * some), unrolled=True)


def own_call(own_msg, mate_msg, rows, cells):
    times, lanes = own_msg[0].shape[1:]
    slots = sum(chunk.shape[0] for chunk in own_msg)
    chunks = len(own_msg)
    return pl.pallas_call(
        functools.partial(own_kernel, chunks),
        out_shape=(
            shape_of((rows * times, cells), F32),
            shape_of((rows * times, cells), BF16),
            shape_of((cells, cells), BF16),
            shape_of((INFO, cells), F32),
        ),
        in_specs=[ANY] * (2 * chunks),
        out_specs=(VMEM,) * 4,
        scratch_shapes=[
            pltpu.VMEM((2, slots, times, lanes), BF16),
            pltpu.VMEM((2, 8, lanes), I32),
            pltpu.SMEM((2, 8, lanes), I32),
            pltpu.VMEM((rows * times, cells), BF16),
            pltpu.VMEM((cells, cells), BF16),
            pltpu.VMEM((2, cells, INFO), F32),
            pltpu.SemaphoreType.DMA((3, chunks)),
        ],
        compiler_params=params(24),
        cost_estimate=cost(9),
        name="own_product",
    )(*own_msg, *mate_msg)


def mate_kernel(count, *refs):
    firsts = refs[:count]
    near_ref, dense, cov_ref, info_ref, out_ref, far_ref, info_buf, turned, sem = refs[count:]
    _, lanes = info_buf.shape[2:]
    cells = cov_ref.shape[1]
    blocks = cells // lanes
    tall = min(256, dense.shape[0])
    steps = dense.shape[0] // tall
    part = count * cells // steps
    copies = []
    for k in range(count):
        copies.append(pltpu.make_async_copy(firsts[k].at[pl.ds(0, 1 + blocks)], info_buf.at[k], sem.at[k]))
        copies[-1].start()
    for k in range(count):
        copies[k].wait()
        read_info(info_buf.at[k], blocks, None, turned.at[pl.ds(k * cells, cells)])

    @pl.loop(0, steps)
    def _(u):
        here = aligned(u * tall, tall)
        fill_covariance(far_ref, u * part, u * part, part, turned, info_ref)
        out_ref[here, :] = near_ref[here, :] + jnp.dot(dense[here, :], cov_ref[...], preferred_element_type=F32)


def mate_call(firsts, near, mate_dense, cov, info):
    times, lanes = firsts[0].shape[1:]
    cells = cov.shape[1]
    blocks = cells // lanes
    count = len(firsts)
    return pl.pallas_call(
        functools.partial(mate_kernel, count),
        out_shape=(shape_of(near.shape, F32), shape_of((count * cells, cells), BF16)),
        in_specs=[ANY] * count + [VMEM] * 4,
        out_specs=(VMEM, VMEM),
        scratch_shapes=[
            pltpu.VMEM((count, 1 + blocks, times, lanes), BF16),
            pltpu.VMEM((count * cells, INFO), F32),
            pltpu.SemaphoreType.DMA((count,)),
        ],
        input_output_aliases={count: 0},
        compiler_params=params(24),
        cost_estimate=cost(8),
        name="mate_product",
    )(*firsts, near, mate_dense, cov, info)


def mixed_unit(mix_ref, value):
    high = value.astype(BF16)
    low = (value - high.astype(F32)).astype(BF16)
    stacked = jnp.concatenate([high, low, high], axis=0)
    return jnp.dot(mix_ref[...], stacked, preferred_element_type=F32).astype(BF16)


def turn(value, rows, times):
    return jnp.swapaxes(value.reshape(rows, times, value.shape[1]), 0, 1)


def first_kernel(count, chunks, unit, *refs):
    msgs = [refs[k * chunks : (k + 1) * chunks] for k in range(count)]
    cov_ref, near_ref, mix_ref, out_ref, next_ref, bufs, bits_v, bits_s, dense, sem = refs[count * chunks :]
    times, lanes = bufs.shape[2:]
    cells = near_ref.shape[1]
    blocks = cells // lanes
    rows = out_ref.shape[0]
    deep = -(-rows * blocks // lanes)
    limit = sum(chunk.shape[0] for chunk in msgs[0])
    copies = [fetch(msgs[k], bufs.at[k], sem.at[k]) for k in range(count)]
    for k in range(count):
        for copy in copies[k]:
            copy.wait()
        read_head(bufs.at[k], rows, blocks, bits_v.at[k])
    copy_in(bits_v, bits_s, sem.at[count, 0])
    ready = jnp.int32(0)
    for u in range(rows // unit):
        whole = jnp.int32(1)
        for k in range(count):
            whole = whole * (bits_s[k, deep, (u + 1) * unit - 1] <= limit).astype(I32)
        ready = ready + whole
    next_ref[0] = ready

    def step(u, _):
        for k in range(count):
            expand(bufs.at[k], bits_s.at[k], u * unit, unit, blocks, into(dense, times, lanes, k * cells))
        here = aligned(u * unit * times, unit * times)
        value = near_ref[here, :] + jnp.dot(dense[...], cov_ref[...], preferred_element_type=F32)
        out_ref[aligned(u * unit, unit)] = mixed_unit(mix_ref, value).reshape(unit, times, cells)
        return 0

    lax.fori_loop(0, ready, step, 0)


def first_rows(msgs, cov, near, mix, rows, unit, slots):
    times, lanes = msgs[0][0].shape[1:]
    cells = near.shape[1]
    count, chunks = len(msgs), len(msgs[0])
    flat = [chunk for msg in msgs for chunk in msg]
    return pl.pallas_call(
        functools.partial(first_kernel, count, chunks, unit),
        out_shape=(shape_of((rows, times, cells), BF16), shape_of((1,), I32)),
        in_specs=[ANY] * len(flat) + [VMEM] * 3,
        out_specs=(VMEM, SMEM),
        scratch_shapes=[
            pltpu.VMEM((count, slots, times, lanes), BF16),
            pltpu.VMEM((count, 8, lanes), I32),
            pltpu.SMEM((count, 8, lanes), I32),
            pltpu.VMEM((unit * times, count * cells), BF16),
            pltpu.SemaphoreType.DMA((count + 1, chunks)),
        ],
        compiler_params=params(20),
        cost_estimate=cost(6),
        name="first_rows",
    )(*flat, cov, near, mix)


def last_kernel(count, chunks, pieces, unit, each, *refs):
    msgs = [refs[k * chunks : (k + 1) * chunks] for k in range(count)]
    panel_msgs = refs[count * chunks : count * chunks + pieces]
    refs = refs[count * chunks + pieces :]
    start_ref, sources_ref, cov_ref, near_ref, mix_ref, done_ref, out_ref, part_ref = refs[:8]
    bufs, panel_bufs, bits_v, bits_s, dense, turned, panel, sem, panel_sem = refs[8:]
    times, lanes = bufs.shape[2:]
    cells = near_ref.shape[1]
    blocks = cells // lanes
    rows = out_ref.shape[0]
    copies = [fetch(msgs[k], bufs.at[k], sem.at[k]) for k in range(count)]
    panel_copies = [
        pltpu.make_async_copy(panel_msgs[k], panel_bufs.at[k], panel_sem.at[k]) for k in range(pieces)
    ]
    for copy in panel_copies:
        copy.start()
    for k in range(count):
        for copy in copies[k]:
            copy.wait()
        read_head(bufs.at[k], rows, blocks, bits_v.at[k])
    for k in range(pieces):
        panel_copies[k].wait()
        read_head(panel_bufs.at[k], each, blocks, bits_v.at[count + k], flagged=True)
    copy_in(bits_v, bits_s, sem.at[count, 0])
    first = start_ref[0]

    def step(u, _):
        for k in range(count):
            expand(bufs.at[k], bits_s.at[k], u * unit, unit, blocks, into(dense, times, lanes, k * cells))
        here = aligned(u * unit * times, unit * times)
        value = near_ref[here, :] + jnp.dot(dense[...], cov_ref[...], preferred_element_type=F32)
        mixed = mixed_unit(mix_ref, value)
        out_ref[aligned(u * unit, unit)] = mixed.reshape(unit, times, cells)
        turned[:, aligned(u * unit, unit), :] = turn(mixed, unit, times)
        return 0

    lax.fori_loop(first, rows // unit, step, 0)

    def earlier(u, _):
        at = aligned(u * unit, unit)
        value = done_ref[at]
        out_ref[at] = value
        value = value.reshape(unit * times, cells)
        turned[:, aligned(u * unit, unit), :] = turn(value, unit, times)
        return 0

    lax.fori_loop(0, first, earlier, 0)

    deep = -(-each * blocks // lanes)
    over = jnp.int32(0)
    for k in range(pieces):
        over = over + (bits_s[count + k, deep, each - 1] > panel_bufs.shape[1] - 1).astype(I32)
        over = over + bits_s[count + k, deep + 1, 0]

    group = max(1, 16 // each)
    placed = each % 16 == 0

    @pl.loop(0, pieces // group)
    def _(g):
        at = pl.multiple_of((sources_ref[g] if placed else g) * each * group, 16)
        for b in range(blocks):
            tiles = []
            for i in range(group * each):
                k, place = g * group + i // each, i % each * blocks + b
                tiles.append(panel_bufs[k, bits_s[count + k, place // lanes, place % lanes]])
            value = turn(jnp.concatenate(tiles, axis=0), group * each, times)
            panel[:, pl.ds(at, group * each), b * lanes : (b + 1) * lanes] = value

    total = None
    for t in range(times):
        value = lax.dot_general(
            turned[t], panel[t], (((1,), (1,)), ((), ())), preferred_element_type=F32
        )
        total = value if total is None else total + value
    if not placed:
        size = pieces * each
        row = lax.broadcasted_iota(I32, (size, size), 0)
        target = row
        for k in range(pieces):
            target = jnp.where(row // each == k, sources_ref[k] * each + row % each, target)
        select = (lax.broadcasted_iota(I32, (size, size), 1) == target).astype(F32).astype(BF16)
        value, total = total, jnp.zeros(total.shape, F32)
        for _ in range(3):
            high = value.astype(BF16)
            total = total + jnp.dot(high, select, preferred_element_type=F32)
            value = value - high.astype(F32)
    part_ref[0:rows, :] = total
    part_ref[rows:, :] = jnp.broadcast_to(over, (8, pieces * each)).astype(F32)


def last_rows(msgs, panel_msgs, start, sources, cov, near, mix, done, unit, each):
    times, lanes = panel_msgs[0].shape[1:]
    rows, _, cells = done.shape
    count, chunks, pieces = len(msgs), len(msgs[0]), len(panel_msgs)
    slots = sum(chunk.shape[0] for chunk in msgs[0])
    flat = [chunk for msg in msgs for chunk in msg] + list(panel_msgs)
    return pl.pallas_call(
        functools.partial(last_kernel, count, chunks, pieces, unit, each),
        out_shape=(shape_of(done.shape, BF16), shape_of((rows + 8, pieces * each), F32)),
        in_specs=[ANY] * len(flat) + [SMEM, SMEM] + [VMEM] * 4,
        out_specs=(VMEM, VMEM),
        scratch_shapes=[
            pltpu.VMEM((count, slots, times, lanes), BF16),
            pltpu.VMEM((pieces, panel_msgs[0].shape[0], times, lanes), BF16),
            pltpu.VMEM((count + pieces, 8, lanes), I32),
            pltpu.SMEM((count + pieces, 8, lanes), I32),
            pltpu.VMEM((unit * times, count * cells), BF16),
            pltpu.VMEM((times, rows, cells), BF16),
            pltpu.VMEM((times, pieces * each, cells), BF16),
            pltpu.SemaphoreType.DMA((count + 1, chunks)),
            pltpu.SemaphoreType.DMA((pieces,)),
        ],
        compiler_params=params(36),
        cost_estimate=cost(10),
        name="last_rows",
    )(*flat, start, sources, cov, near, mix, done)


def mix_kernel(unit, time_ref, out_ref):
    times = time_ref.shape[0]
    size = unit * times
    value = time_ref[...]
    high = value.astype(BF16)
    low = (value - high.astype(F32)).astype(BF16)

    def same(shape, dim):
        index = lax.broadcasted_iota(I32, shape, 1 - dim) % times
        return (index == lax.broadcasted_iota(I32, shape, dim)).astype(F32).astype(BF16)

    row = lax.broadcasted_iota(I32, (size, size), 0)
    col = lax.broadcasted_iota(I32, (size, size), 1)
    for j, part in enumerate((high, high, low)):
        spread = jnp.dot(same((size, times), 1), part, preferred_element_type=F32).astype(BF16)
        spread = jnp.dot(spread, same((times, size), 0), preferred_element_type=F32)
        out_ref[:, j * size : (j + 1) * size] = jnp.where(row // times == col // times, spread, 0.0).astype(BF16)


def mixing(time_cov, unit):
    size = unit * time_cov.shape[0]
    return pl.pallas_call(
        functools.partial(mix_kernel, unit),
        out_shape=shape_of((size, 3 * size), BF16),
        in_specs=[VMEM],
        out_specs=VMEM,
        compiler_params=params(8),
        cost_estimate=cost(1),
        name="mixing",
    )(time_cov)


def partner(value, axis, count):
    return lax.ppermute(value, axis, [(i, i ^ 1) for i in range(count)])


def shifted(value, axis, count, shift, flip=0):
    return lax.ppermute(value, axis, [(i, ((i + 2 * shift) % count) ^ flip) for i in range(count)])


def add_cells(part, cells):
    total = part
    for shift in range(cells // 2):
        for flip in range(2):
            if shift or flip:
                total = total + shifted(part, "cell", cells, shift, flip)
    return total


def dense_way(cells, observers, footprint, block_mask, own, time_cov, mine, sources):
    obs_rows, times, cell_local = footprint.shape
    blocks = block_mask.shape[1]
    keep = block_mask.astype(BF16)[:, None, :, None]
    feet = (footprint.reshape(obs_rows, times, blocks, cell_local // blocks) * keep).reshape(footprint.shape)

    def add(carry, _):
        total, feet, info = carry
        dx = info[0][:, None] - own[0][None, :]
        dy = info[1][:, None] - own[1][None, :]
        decay = jnp.exp(-jnp.sqrt(dx * dx + dy * dy + 1.0) / LENGTH)
        cov = (decay * (info[2][:, None] * own[2][None, :])).astype(BF16)
        total = total + jnp.dot(feet.reshape(-1, cell_local), cov, preferred_element_type=F32)
        ring = [(i, (i + 1) % cells) for i in range(cells)]
        return (total, lax.ppermute(feet, "cell", ring), lax.ppermute(info, "cell", ring)), None

    zero = jnp.zeros((obs_rows * times, cell_local), F32)
    (total, _, _), _ = lax.scan(add, (zero, feet, own), None, length=cells)
    cov_product = jnp.einsum(
        "ts,ksc->ktc", time_cov, total.reshape(obs_rows, times, cell_local), precision=lax.Precision.HIGHEST
    ).astype(BF16)
    flat = cov_product.reshape(obs_rows, times * cell_local)

    def meet(held, _):
        both = jnp.concatenate([held, partner(held, "obs", observers)], axis=0)
        part = lax.dot_general(
            flat, both.reshape(both.shape[0], -1), (((1,), (1,)), ((), ())), preferred_element_type=F32
        )
        return shifted(held, "obs", observers, 1), part

    _, parts = lax.scan(meet, jnp.take(feet, mine, axis=0), None, length=observers // 2)
    parts = parts.transpose(1, 0, 2).reshape(obs_rows, observers, -1)
    ordered = jnp.zeros_like(parts).at[:, sources].set(parts)
    return cov_product, add_cells(ordered.reshape(obs_rows, -1), cells)


def body(cells, observers, footprint, block_mask, cell_coords, cell_sigma, time_cov, error_var, panel_index):
    obs_rows, _, cell_local = footprint.shape
    blocks = block_mask.shape[1]
    group = lax.axis_index("obs")
    each = panel_index.shape[0] // observers
    half = observers // 2
    unit = math.gcd(16, obs_rows)
    slots = slot_count(obs_rows * blocks, 1 + blocks)
    chunks = (slots - slots // 2, slots // 2)
    mask = block_mask.T
    order = jnp.arange(observers, dtype=I32)
    sources = (group // 2 - order // 2) % half * 2 + (group % 2 ^ (order % 2))

    room = slots - 2 - blocks - 1
    own_panel = pack_panel(mask, panel_index, group, footprint, each, slot_count(each * blocks, 1), room)
    ring = [own_panel]
    for _ in range(1, half):
        ring.append(shifted(ring[-1], "obs", observers, 1))
    messages = []
    for held in ring:
        messages += [held, partner(held, "obs", observers)]
    own_msg = pack_feet(mask, cell_coords, cell_sigma[None, :], footprint, chunks)
    far_msgs = []
    for shift in range(1, cells // 2):
        far_msgs.append([shifted(c, "cell", cells, shift) for c in own_msg])
    mate_msg = [partner(c, "cell", cells) for c in own_msg]
    for shift in range(1, cells // 2):
        far_msgs.append([partner(c, "cell", cells) for c in far_msgs[shift - 1]])

    near, mate_dense, mate_cov, info = own_call(own_msg, mate_msg, obs_rows, cell_local)
    near, far_cov = mate_call([msg[0] for msg in far_msgs], near, mate_dense, mate_cov, info)
    mix = mixing(time_cov, unit)
    cov_product, start = first_rows([msg[:1] for msg in far_msgs], far_cov, near, mix, obs_rows, unit, slots)
    cov_product, part = last_rows(far_msgs, messages, start, sources, far_cov, near, mix, cov_product, unit, each)
    total = add_cells(part, cells)

    def again(carry):
        wanted = carry[1][obs_rows, 0] > 0
        mask, cell_info, place, from_group = (
            jnp.where(wanted, value, 0) for value in (block_mask, info, group, sources)
        )
        mine = lax.dynamic_slice_in_dim(panel_index, place * each, each) - place * obs_rows
        cov_product, total = dense_way(
            cells, observers, footprint, mask, cell_info, time_cov, mine, from_group
        )
        return cov_product, jnp.pad(total, ((0, 8), (0, 0)))

    cov_product, total = lax.while_loop(lambda carry: carry[1][obs_rows, 0] > 0, again, (cov_product, total))
    total = total[:obs_rows]
    positions = jnp.arange(obs_rows, dtype=I32)
    on_diagonal = ((group * obs_rows + positions)[:, None] == panel_index[None, :]).astype(F32)
    return cov_product, total + error_var[:, None] * on_diagonal


def solution(mesh):
    in_specs = (
        P("obs", None, "cell"),
        P("obs", "cell"),
        P(None, "cell"),
        P("cell"),
        P(),
        P("obs"),
        P(),
    )
    out_specs = (P("obs", None, "cell"), P("obs", None))
    cells, observers = mesh.shape["cell"], mesh.shape["obs"]

    def per_device(*args):
        return body(cells, observers, *args)

    return jax.shard_map(per_device, mesh=mesh, in_specs=in_specs, out_specs=out_specs, check_vma=False)
```

profile of v0, /device:TPU:0, one launch (start us, length us, event | category | flops | bytes accessed | tf_op | source)
XLA Modules:
  0.0 91.1 jit_solution(12812277071254315461)
XLA Ops:
  2.7 3.8 %pack_feet.1 = (bf16[157,16,128]{2,1,0:T(8,128)(2,1)S(1)}, bf16[157,16,128]{2,1,0:T(8,128)(2,1)S(1)}) custom-call(s32[8,64]{1,0:T(8,128)S(1)} %bitcast.109, s32[2,1024]{1,0:T(2,128)S(1)} %copy-done.2, f32[1,1024]{1,0:T(1,128)S(1)} %bitcast.112, bf16[64,16,1024]{2,1,0:T(8,128)(2,1)} %feet_ref.3), custom_call_target="tpu_custom_call" | custom-call | flops 2700000000 | bytes 1000000 | tf_op jit(solution)/shard_map/pack_feet/pallas_call | solution.py:150
  7.1 2.6 %collective-permute-start.7 = (bf16[157,16,128]{2,1,0:T(8,128)(2,1)S(1)}, bf16[157,16,128]{2,1,0:T(8,128)(2,1)S(1)}, u32[]{:S(2)}, u32[]{:S(2)}) collective-permute-start(bf16[157,16,128]{2,1,0:T(8,128)(2,1)S(1)} %get-tuple-element.173.refs_0_), channel_id=1, source_target_pairs={{0,2},{1,3},{2,0},{3,1},{4,6},{5,7},{6,4},{7,5},{8,10},{9,11},{10,... | collective-permute-start | bytes 1929224 | tf_op jit(solution)/shard_map/ppermute | solution.py:640
  9.8 3.5 %pack_panel.1.refs_4_ = bf16[90,16,128]{2,1,0:T(8,128)(2,1)} custom-call(s32[8,64]{1,0:T(8,128)S(1)} %bitcast.110, s32[8,64]{1,0:T(8,128)S(1)} %bitcast.111, s32[128]{0:T(128)S(1)} %copy-done.7, s32[1]{0:T(128)} %bitcast.4.group_ref, bf16[64,16,1024]{2,1,0:T(8,128)(2,1)} %feet_ref.3), custom_call_target="tpu_custom_call" | custom-call | flops 1800000000 | bytes 1000000 | tf_op jit(solution)/shard_map/pack_panel/pallas_call | solution.py:205
  13.3 1.6 %collective-permute-start.12 = (bf16[90,16,128]{2,1,0:T(8,128)(2,1)}, bf16[90,16,128]{2,1,0:T(8,128)(2,1)}, u32[]{:S(2)}, u32[]{:S(2)}) collective-permute-start(bf16[90,16,128]{2,1,0:T(8,128)(2,1)} %pack_panel.1.refs_4_), channel_id=1, source_target_pairs={{0,8},{4,12},{8,16},{12,20},{16,24},{20,28},{24,0},{28,4},{1,9},{5... | collective-permute-start | bytes 1105928 | tf_op jit(solution)/shard_map/ppermute | solution.py:640
  15.3 1.6 %collective-permute-start.11 = (bf16[90,16,128]{2,1,0:T(8,128)(2,1)}, bf16[90,16,128]{2,1,0:T(8,128)(2,1)S(1)}, u32[]{:S(2)}, u32[]{:S(2)}) collective-permute-start(bf16[90,16,128]{2,1,0:T(8,128)(2,1)} %pack_panel.1.refs_4_), channel_id=1, source_target_pairs={{0,4},{4,0},{8,12},{12,8},{16,20},{20,16},{24,28},{28,24},{1,5},{5... | collective-permute-start | bytes 1105928 | tf_op jit(solution)/shard_map/ppermute | solution.py:636
  16.9 9.5 %collective-permute-done.12.refs_6_ = bf16[90,16,128]{2,1,0:T(8,128)(2,1)} collective-permute-done((bf16[90,16,128]{2,1,0:T(8,128)(2,1)}, bf16[90,16,128]{2,1,0:T(8,128)(2,1)}, u32[]{:S(2)}, u32[]{:S(2)}) %collective-permute-start.12) | collective-permute-done | bytes 368672 | tf_op jit(solution)/shard_map/ppermute | solution.py:640
  27.0 9.4 %own_product.1 = (f32[1024,1024]{1,0:T(8,128)S(1)}, bf16[1024,1024]{1,0:T(8,128)(2,1)S(1)}, bf16[1024,1024]{1,0:T(8,128)(2,1)S(1)}, f32[8,1024]{1,0:T(8,128)S(1)}) custom-call(bf16[157,16,128]{2,1,0:T(8,128)(2,1)S(1)} %get-tuple-element.173.refs_0_, bf16[157,16,128]{2,1,0:T(8,128)(2,1)S(1)} %get-tuple-element.174.refs_1_, ...), custom_call_target="tpu_custom_call" | custom-call | flops 8099999744 | bytes 1000000 | tf_op jit(solution)/shard_map/own_product/pallas_call | solution.py:346
  36.4 1.6 %collective-permute-start.13 = (bf16[90,16,128]{2,1,0:T(8,128)(2,1)}, bf16[90,16,128]{2,1,0:T(8,128)(2,1)S(1)}, u32[]{:S(2)}, u32[]{:S(2)}) collective-permute-start(bf16[90,16,128]{2,1,0:T(8,128)(2,1)} %collective-permute-done.12.refs_6_), channel_id=1, source_target_pairs={{0,4},{4,0},{8,12},{12,8},{16,20},{20,16},{24,28},{28,24},{1,5},{5... | collective-permute-start | bytes 1105928 | tf_op jit(solution)/shard_map/ppermute | solution.py:636
  38.0 4.3 %collective-permute-done.8.refs_1_ = bf16[157,16,128]{2,1,0:T(8,128)(2,1)S(1)} collective-permute-done((bf16[157,16,128]{2,1,0:T(8,128)(2,1)S(1)}, bf16[157,16,128]{2,1,0:T(8,128)(2,1)S(1)}, u32[]{:S(2)}, u32[]{:S(2)}) %collective-permute-start.8) | collective-permute-done | bytes 643104 | tf_op jit(solution)/shard_map/ppermute | solution.py:640
  42.4 6.7 %mate_product.1 = (f32[1024,1024]{1,0:T(8,128)S(1)}, bf16[2048,1024]{1,0:T(8,128)(2,1)S(1)}) custom-call(bf16[157,16,128]{2,1,0:T(8,128)(2,1)S(1)} %collective-permute-done.7.refs_0_, bf16[157,16,128]{2,1,0:T(8,128)(2,1)S(1)} %collective-permute-done.9.refs_1_.refs_2_, f32[1024,1024]{1,0:T(8,128)S(1)} %get-tuple-element.175.refs_2_, ...), custom_call_target="tpu_custom_call", output_to_operand_aliasing={{0}: (2, {})} | custom-call | flops 7200000000 | bytes 1000000 | tf_op jit(solution)/shard_map/mate_product/pallas_call | solution.py:400
  49.1 1.6 %collective-permute-start.15 = (bf16[90,16,128]{2,1,0:T(8,128)(2,1)S(1)}, bf16[90,16,128]{2,1,0:T(8,128)(2,1)S(1)}, u32[]{:S(2)}, u32[]{:S(2)}) collective-permute-start(bf16[90,16,128]{2,1,0:T(8,128)(2,1)S(1)} %collective-permute-done.14.refs_8_), channel_id=1, source_target_pairs={{0,4},{4,0},{8,12},{12,8},{16,20},{20,16},{24,28},{28,24},{1,5},{5... | collective-permute-start | bytes 1105928 | tf_op jit(solution)/shard_map/ppermute | solution.py:636
  50.7 4.5 %collective-permute-done.16.refs_10_ = bf16[90,16,128]{2,1,0:T(8,128)(2,1)S(1)} collective-permute-done((bf16[90,16,128]{2,1,0:T(8,128)(2,1)S(1)}, bf16[90,16,128]{2,1,0:T(8,128)(2,1)S(1)}, u32[]{:S(2)}, u32[]{:S(2)}) %collective-permute-start.16) | collective-permute-done | bytes 368672 | tf_op jit(solution)/shard_map/ppermute | solution.py:640
  55.1 1.5 %collective-permute-start.17 = (bf16[90,16,128]{2,1,0:T(8,128)(2,1)S(1)}, bf16[90,16,128]{2,1,0:T(8,128)(2,1)S(1)}, u32[]{:S(2)}, u32[]{:S(2)}) collective-permute-start(bf16[90,16,128]{2,1,0:T(8,128)(2,1)S(1)} %collective-permute-done.16.refs_10_), channel_id=1, source_target_pairs={{0,4},{4,0},{8,12},{12,8},{16,20},{20,16},{24,28},{28,24},{1,5},{5... | collective-permute-start | bytes 1105928 | tf_op jit(solution)/shard_map/ppermute | solution.py:636
  56.7 6.6 %first_rows.1 = (bf16[64,16,1024]{2,1,0:T(8,128)(2,1)S(1)}, s32[1]{0:T(128)}) custom-call(bf16[157,16,128]{2,1,0:T(8,128)(2,1)S(1)} %collective-permute-done.7.refs_0_, bf16[157,16,128]{2,1,0:T(8,128)(2,1)S(1)} %collective-permute-done.9.refs_1_.refs_2_, bf16[2048,1024]{1,0:T(8,128)(2,1)S(1)} %get-tuple-element.179.refs_2_.refs_14_, ...), custom_call_target="tpu_custom_call" | custom-call | flops 5400000000 | bytes 1000000 | tf_op jit(solution)/shard_map/first_rows/pallas_call | solution.py:467
  63.3 4.8 %collective-permute-done.17.refs_11_ = bf16[90,16,128]{2,1,0:T(8,128)(2,1)S(1)} collective-permute-done((bf16[90,16,128]{2,1,0:T(8,128)(2,1)S(1)}, bf16[90,16,128]{2,1,0:T(8,128)(2,1)S(1)}, u32[]{:S(2)}, u32[]{:S(2)}) %collective-permute-start.17) | collective-permute-done | bytes 368672 | tf_op jit(solution)/shard_map/ppermute | solution.py:636
  68.0 13.8 %last_rows.1 = (bf16[64,16,1024]{2,1,0:T(8,128)(2,1)}, f32[72,128]{1,0:T(8,128)S(1)}) custom-call(bf16[157,16,128]{2,1,0:T(8,128)(2,1)S(1)} %collective-permute-done.7.refs_0_, bf16[157,16,128]{2,1,0:T(8,128)(2,1)S(1)} %collective-permute-done.8.refs_1_, bf16[157,16,128]{2,1,0:T(8,128)(2,1)S(1)} %collective-permute-done.9.refs_1_.refs_2_, ...), custom_call_target="tpu_custom_call" | custom-call | flops 8999999488 | bytes 1000000 | tf_op jit(solution)/shard_map/last_rows/pallas_call | solution.py:581
  82.0 0.8 collective-permute-start.21
  82.8 1.0 %collective-permute-start.22 = (f32[72,128]{1,0:T(8,128)S(1)}, f32[72,128]{1,0:T(8,128)S(1)}, u32[]{:S(2)}, u32[]{:S(2)}) collective-permute-start(f32[72,128]{1,0:T(8,128)S(1)} %get-tuple-element.184), channel_id=1, source_target_pairs={{0,3},{1,2},{2,1},{3,0},{4,7},{5,6},{6,5},{7,4},{8,11},{9,10},{10,... | collective-permute-start | bytes 110600 | tf_op jit(solution)/shard_map/ppermute | solution.py:640
  84.5 1.7 %collective-permute-done.21 = f32[72,128]{1,0:T(8,128)S(1)} collective-permute-done((f32[72,128]{1,0:T(8,128)S(1)}, f32[72,128]{1,0:T(8,128)S(1)}, u32[]{:S(2)}, u32[]{:S(2)}) %collective-permute-start.21) | collective-permute-done | bytes 36896 | tf_op jit(solution)/shard_map/ppermute | solution.py:640
  86.6 0.7 copy.15
  87.3 2.2 %while.62 = (bf16[64,16,1024]{2,1,0:T(8,128)(2,1)}, f32[72,128]{0,1:T(8,128)}, s32[64,8]{1,0:T(8,128)S(1)}, bf16[64,16,1024]{2,1,0:T(8,128)(2,1)}, f32[8,1024]{1...) while((bf16[64,16,1024]{2,1,0:T(8,128)(2,1)}, ...), condition=%wide.region_6.7_spmd.clone, body=%wide.region_0.6_spmd.clone.sunk | while | flops 2432469248 | bytes 70916280 | solution.py:735
  87.3 1.3 %slice.54 = f32[1,1]{0,1:T(1,128)} slice(f32[72,128]{0,1:T(8,128)} %get-tuple-element.367), slice={[64:65], [0:1]} | slice | bytes 8 | tf_op jit(solution)/shard_map/while/cond/slice | solution.py:735
  89.5 0.9 %copy.17 = f32[72,128]{1,0:T(8,128)S(1)} copy(f32[72,128]{0,1:T(8,128)} %get-tuple-element.186) | data formatting | bytes 73728 | tf_op jit(solution)/shard_map/while | solution.py:735
  90.4 0.7 slice_add_fusion
  (42 shorter events, 4.9 us)
Async XLA Ops:
  0.6 0.7 copy-start
  1.3 0.7 copy-start.2
  2.7 7.1 %copy-start.1 = (s32[64,8]{0,1:T(8,128)S(1)}, s32[64,8]{0,1:T(8,128)}, u32[]{:S(2)}) copy-start(s32[64,8]{0,1:T(8,128)} %param.14) | copy-start | bytes 6148
  2.7 7.1 %copy-start.7 = (s32[128]{0:T(128)S(1)}, s32[128]{0:T(128)}, u32[]{:S(2)}) copy-start(s32[128]{0:T(128)} %index_hbm.1) | copy-start | bytes 1540
  6.5 8.4 %copy-start.5 = (f32[16,16]{1,0:T(8,128)S(1)}, f32[16,16]{1,0:T(8,128)}, u32[]{:S(2)}) copy-start(f32[16,16]{1,0:T(8,128)} %time_ref.1) | copy-start | bytes 3076
  6.5 20.4 %collective-permute-start.18 = (bf16[157,16,128]{2,1,0:T(8,128)(2,1)S(1)}, bf16[157,16,128]{2,1,0:T(8,128)(2,1)S(1)}, u32[]{:S(2)}, u32[]{:S(2)}) collective-permute-start(bf16[157,16,128]{2,1,0:T(8,128)(2,1)S(1)} %get-tuple-element.173.refs_0_), channel_id=1, source_target_pairs={{0,1},{1,0},{2,3},{3,2},{4,5},{5,4},{6,7},{7,6},{8,9},{9,8},{10,11... | collective-permute-start | bytes 1929224 | tf_op jit(solution)/shard_map/ppermute | solution.py:636
  7.1 19.8 %collective-permute-start.7 = (bf16[157,16,128]{2,1,0:T(8,128)(2,1)S(1)}, bf16[157,16,128]{2,1,0:T(8,128)(2,1)S(1)}, u32[]{:S(2)}, u32[]{:S(2)}) collective-permute-start(bf16[157,16,128]{2,1,0:T(8,128)(2,1)S(1)} %get-tuple-element.173.refs_0_), channel_id=1, source_target_pairs={{0,2},{1,3},{2,0},{3,1},{4,6},{5,7},{6,4},{7,5},{8,10},{9,11},{10,... | collective-permute-start | bytes 1929224 | tf_op jit(solution)/shard_map/ppermute | solution.py:640
  9.6 17.4 %collective-permute-start.19 = (bf16[157,16,128]{2,1,0:T(8,128)(2,1)S(1)}, bf16[157,16,128]{2,1,0:T(8,128)(2,1)S(1)}, u32[]{:S(2)}, u32[]{:S(2)}) collective-permute-start(bf16[157,16,128]{2,1,0:T(8,128)(2,1)S(1)} %get-tuple-element.174.refs_1_), channel_id=1, source_target_pairs={{0,1},{1,0},{2,3},{3,2},{4,5},{5,4},{6,7},{7,6},{8,9},{9,8},{10,11... | collective-permute-start | bytes 1929224 | tf_op jit(solution)/shard_map/ppermute | solution.py:636
  13.3 13.1 %collective-permute-start.12 = (bf16[90,16,128]{2,1,0:T(8,128)(2,1)}, bf16[90,16,128]{2,1,0:T(8,128)(2,1)}, u32[]{:S(2)}, u32[]{:S(2)}) collective-permute-start(bf16[90,16,128]{2,1,0:T(8,128)(2,1)} %pack_panel.1.refs_4_), channel_id=1, source_target_pairs={{0,8},{4,12},{8,16},{12,20},{16,24},{20,28},{24,0},{28,4},{1,9},{5... | collective-permute-start | bytes 1105928 | tf_op jit(solution)/shard_map/ppermute | solution.py:640
  15.3 47.9 %collective-permute-start.11 = (bf16[90,16,128]{2,1,0:T(8,128)(2,1)}, bf16[90,16,128]{2,1,0:T(8,128)(2,1)S(1)}, u32[]{:S(2)}, u32[]{:S(2)}) collective-permute-start(bf16[90,16,128]{2,1,0:T(8,128)(2,1)} %pack_panel.1.refs_4_), channel_id=1, source_target_pairs={{0,4},{4,0},{8,12},{12,8},{16,20},{20,16},{24,28},{28,24},{1,5},{5... | collective-permute-start | bytes 1105928 | tf_op jit(solution)/shard_map/ppermute | solution.py:636
  26.4 15.9 %collective-permute-start.8 = (bf16[157,16,128]{2,1,0:T(8,128)(2,1)S(1)}, bf16[157,16,128]{2,1,0:T(8,128)(2,1)S(1)}, u32[]{:S(2)}, u32[]{:S(2)}) collective-permute-start(bf16[157,16,128]{2,1,0:T(8,128)(2,1)S(1)} %get-tuple-element.174.refs_1_), channel_id=1, source_target_pairs={{0,2},{1,3},{2,0},{3,1},{4,6},{5,7},{6,4},{7,5},{8,10},{9,11},{10,... | collective-permute-start | bytes 1929224 | tf_op jit(solution)/shard_map/ppermute | solution.py:640
  26.9 15.4 %collective-permute-start.14 = (bf16[90,16,128]{2,1,0:T(8,128)(2,1)}, bf16[90,16,128]{2,1,0:T(8,128)(2,1)S(1)}, u32[]{:S(2)}, u32[]{:S(2)}) collective-permute-start(bf16[90,16,128]{2,1,0:T(8,128)(2,1)} %collective-permute-done.12.refs_6_), channel_id=1, source_target_pairs={{0,8},{4,12},{8,16},{12,20},{16,24},{20,28},{24,0},{28,4},{1,9},{5... | collective-permute-start | bytes 1105928 | tf_op jit(solution)/shard_map/ppermute | solution.py:640
  26.9 15.4 %collective-permute-start.9 = (bf16[157,16,128]{2,1,0:T(8,128)(2,1)S(1)}, bf16[157,16,128]{2,1,0:T(8,128)(2,1)S(1)}, u32[]{:S(2)}, u32[]{:S(2)}) collective-permute-start(bf16[157,16,128]{2,1,0:T(8,128)(2,1)S(1)} %collective-permute-done.7.refs_0_), channel_id=1, source_target_pairs={{0,1},{1,0},{2,3},{3,2},{4,5},{5,4},{6,7},{7,6},{8,9},{9,8},{10,11... | collective-permute-start | bytes 1929224 | tf_op jit(solution)/shard_map/ppermute | solution.py:636
  36.4 26.8 %collective-permute-start.13 = (bf16[90,16,128]{2,1,0:T(8,128)(2,1)}, bf16[90,16,128]{2,1,0:T(8,128)(2,1)S(1)}, u32[]{:S(2)}, u32[]{:S(2)}) collective-permute-start(bf16[90,16,128]{2,1,0:T(8,128)(2,1)} %collective-permute-done.12.refs_6_), channel_id=1, source_target_pairs={{0,4},{4,0},{8,12},{12,8},{16,20},{20,16},{24,28},{28,24},{1,5},{5... | collective-permute-start | bytes 1105928 | tf_op jit(solution)/shard_map/ppermute | solution.py:636
  42.3 20.9 %collective-permute-start.10 = (bf16[157,16,128]{2,1,0:T(8,128)(2,1)S(1)}, bf16[157,16,128]{2,1,0:T(8,128)(2,1)S(1)}, u32[]{:S(2)}, u32[]{:S(2)}) collective-permute-start(bf16[157,16,128]{2,1,0:T(8,128)(2,1)S(1)} %collective-permute-done.8.refs_1_), channel_id=1, source_target_pairs={{0,1},{1,0},{2,3},{3,2},{4,5},{5,4},{6,7},{7,6},{8,9},{9,8},{10,11... | collective-permute-start | bytes 1929224 | tf_op jit(solution)/shard_map/ppermute | solution.py:636
  42.3 12.8 %collective-permute-start.16 = (bf16[90,16,128]{2,1,0:T(8,128)(2,1)S(1)}, bf16[90,16,128]{2,1,0:T(8,128)(2,1)S(1)}, u32[]{:S(2)}, u32[]{:S(2)}) collective-permute-start(bf16[90,16,128]{2,1,0:T(8,128)(2,1)S(1)} %collective-permute-done.14.refs_8_), channel_id=1, source_target_pairs={{0,8},{4,12},{8,16},{12,20},{16,24},{20,28},{24,0},{28,4},{1,9},{5... | collective-permute-start | bytes 1105928 | tf_op jit(solution)/shard_map/ppermute | solution.py:640
  49.1 14.2 %collective-permute-start.15 = (bf16[90,16,128]{2,1,0:T(8,128)(2,1)S(1)}, bf16[90,16,128]{2,1,0:T(8,128)(2,1)S(1)}, u32[]{:S(2)}, u32[]{:S(2)}) collective-permute-start(bf16[90,16,128]{2,1,0:T(8,128)(2,1)S(1)} %collective-permute-done.14.refs_8_), channel_id=1, source_target_pairs={{0,4},{4,0},{8,12},{12,8},{16,20},{20,16},{24,28},{28,24},{1,5},{5... | collective-permute-start | bytes 1105928 | tf_op jit(solution)/shard_map/ppermute | solution.py:636
  55.1 12.9 %collective-permute-start.17 = (bf16[90,16,128]{2,1,0:T(8,128)(2,1)S(1)}, bf16[90,16,128]{2,1,0:T(8,128)(2,1)S(1)}, u32[]{:S(2)}, u32[]{:S(2)}) collective-permute-start(bf16[90,16,128]{2,1,0:T(8,128)(2,1)S(1)} %collective-permute-done.16.refs_10_), channel_id=1, source_target_pairs={{0,4},{4,0},{8,12},{12,8},{16,20},{20,16},{24,28},{28,24},{1,5},{5... | collective-permute-start | bytes 1105928 | tf_op jit(solution)/shard_map/ppermute | solution.py:636
  68.0 19.2 %copy-start.6 = (f32[16,16]{1,0:T(8,128)S(1)}, f32[16,16]{1,0:T(8,128)}, u32[]{:S(2)}) copy-start(f32[16,16]{1,0:T(8,128)} %time_ref.1) | copy-start | bytes 3076
  81.9 2.6 %collective-permute-start.20 = (f32[72,128]{1,0:T(8,128)S(1)}, f32[72,128]{1,0:T(8,128)S(1)}, u32[]{:S(2)}, u32[]{:S(2)}) collective-permute-start(f32[72,128]{1,0:T(8,128)S(1)} %get-tuple-element.184), channel_id=1, source_target_pairs={{0,1},{1,0},{2,3},{3,2},{4,5},{5,4},{6,7},{7,6},{8,9},{9,8},{10,11... | collective-permute-start | bytes 110600 | tf_op jit(solution)/shard_map/ppermute | solution.py:640
  82.0 4.2 %collective-permute-start.21 = (f32[72,128]{1,0:T(8,128)S(1)}, f32[72,128]{1,0:T(8,128)S(1)}, u32[]{:S(2)}, u32[]{:S(2)}) collective-permute-start(f32[72,128]{1,0:T(8,128)S(1)} %get-tuple-element.184), channel_id=1, source_target_pairs={{0,2},{1,3},{2,0},{3,1},{4,6},{5,7},{6,4},{7,5},{8,10},{9,11},{10,... | collective-permute-start | bytes 110600 | tf_op jit(solution)/shard_map/ppermute | solution.py:640
  82.8 3.8 %collective-permute-start.22 = (f32[72,128]{1,0:T(8,128)S(1)}, f32[72,128]{1,0:T(8,128)S(1)}, u32[]{:S(2)}, u32[]{:S(2)}) collective-permute-start(f32[72,128]{1,0:T(8,128)S(1)} %get-tuple-element.184), channel_id=1, source_target_pairs={{0,3},{1,2},{2,1},{3,0},{4,7},{5,6},{6,5},{7,4},{8,11},{9,10},{10,... | collective-permute-start | bytes 110600 | tf_op jit(solution)/shard_map/ppermute | solution.py:640
  87.3 3.1 %copy-start.8 = (f32[64]{0:T(128)S(1)}, f32[64]{0:T(128)}, u32[]{:S(2)}) copy-start(f32[64]{0:T(128)} %param.18) | copy-start | bytes 772
  87.3 3.1 %copy-start.9 = (s32[64]{0:T(128)S(1)}, s32[64]{0:T(128)}, u32[]{:S(2)}) copy-start(s32[64]{0:T(128)} %iota_add_fusion) | copy-start | bytes 772
  (1 other events, 0.7 us)
where the time goes:
time: 91.6 us; the launch traced here: 91.1 us
  Pallas kernels  44.1 us (48%)
  waiting for transfers between devices  25.2 us (28%)
  starting transfers between devices  13.7 us (15%)
  local copies, waits for them, and re-layouts  5.14 us (6%)
  other arithmetic  1.31 us (1%)
    ppermute x8, waiting for transfers between devices, shifted(): lax.ppermute(value, axis, [(i, (i + 2 * shift) % count ^ flip) for i in r...  20.4 us
    pallas_call x1, Pallas kernels, last_rows(): pl.pallas_call(functools.partial(last_kernel, count, chunks, pieces, unit...  13.8 us
    pallas_call x1, Pallas kernels, own_call(): pl.pallas_call(functools.partial(own_kernel, chunks), out_shape=(shape_of...  9.39 us
    ppermute x8, starting transfers between devices, partner(): return lax.ppermute(value, axis, [(i, i ^ 1) for i in range(count)])  7.07 us
    pallas_call x1, Pallas kernels, mate_call(): pl.pallas_call(functools.partial(mate_kernel, count), out_shape=(shape_of...  6.72 us
    ppermute x8, starting transfers between devices, shifted(): lax.ppermute(value, axis, [(i, (i + 2 * shift) % count ^ flip) for i in r...  6.64 us
    pallas_call x1, Pallas kernels, first_rows(): pl.pallas_call(functools.partial(first_kernel, count, chunks, unit), out_...  6.55 us
    ppermute x8, waiting for transfers between devices, partner(): return lax.ppermute(value, axis, [(i, i ^ 1) for i in range(count)])  4.8 us
  transfers between devices with their start and end apart: 16, of which 6 were waited for; matrix products, arithmetic and copies ran while one was open for 1% of the time, Pallas kernels for 29%

commit v1 on v0

--- a/solution.py
+++ b/solution.py
@@ -168,24 +168,18 @@
     )(mask, coords, sigma, feet)
 
 
-def pack_panel_kernel(room, mask_ref, mask_hbm, index_hbm, group_ref, feet_ref, out_ref, mask_v, index_ref, rows_buf, head_v, small_sem, sem):
+def pack_panel_kernel(room, mask_ref, mask_hbm, index_ref, group_ref, feet_ref, out_ref, mask_v, rows_buf, head_v, small_sem, sem):
     count = rows_buf.shape[0]
     blocks, obs = mask_ref.shape
     lanes = out_ref.shape[2]
-    small = [
-        pltpu.make_async_copy(src, dst, small_sem.at[k])
-        for k, (src, dst) in enumerate(((index_hbm, index_ref), (mask_hbm, mask_v)))
-    ]
-    for copy in small:
-        copy.start()
+    mask_copy = pltpu.make_async_copy(mask_hbm, mask_v, small_sem.at[0])
+    mask_copy.start()
     base = group_ref[0]
-    small[0].wait()
     rows = [jnp.clip(index_ref[base * count + j] - base * obs, 0, obs - 1) for j in range(count)]
     copies = [pltpu.make_async_copy(feet_ref.at[rows[j]], rows_buf.at[j], sem.at[j]) for j in range(count)]
     for copy in copies:
         copy.start()
-    for copy in small[1:]:
-        copy.wait()
+    mask_copy.wait()
     flag = (jnp.sum(mask_v[...].astype(F32), axis=(0, 1), keepdims=True) > room).astype(I32)
     for copy in copies:
         copy.wait()
@@ -205,14 +199,13 @@
     return pl.pallas_call(
         functools.partial(pack_panel_kernel, room),
         out_shape=shape_of((slots, times, lanes), BF16),
-        in_specs=[SMEM, HBM, HBM, SMEM, HBM],
+        in_specs=[SMEM, HBM, SMEM, SMEM, HBM],
         out_specs=VMEM,
         scratch_shapes=[
             pltpu.VMEM(mask.shape, I32),
-            pltpu.SMEM(panel_index.shape, I32),
             pltpu.VMEM((count, times, cells), BF16),
             pltpu.VMEM((times, lanes), F32),
-            pltpu.SemaphoreType.DMA((2,)),
+            pltpu.SemaphoreType.DMA((1,)),
             pltpu.SemaphoreType.DMA((count,)),
         ],
         compiler_params=params(8),
@@ -362,7 +355,7 @@
             pltpu.VMEM((2, cells, INFO), F32),
             pltpu.SemaphoreType.DMA((3, chunks)),
         ],
-        compiler_params=params(24),
+        compiler_params=params(16),
         cost_estimate=cost(9),
         name="own_product",
     )(*own_msg, *mate_msg)
@@ -408,7 +401,7 @@
             pltpu.SemaphoreType.DMA((count,)),
         ],
         input_output_aliases={count: 0},
-        compiler_params=params(24),
+        compiler_params=params(16),
         cost_estimate=cost(8),
         name="mate_product",
     )(*firsts, near, mate_dense, cov, info)
@@ -425,50 +418,77 @@
     return jnp.swapaxes(value.reshape(rows, times, value.shape[1]), 0, 1)
 
 
-def first_kernel(count, chunks, unit, *refs):
+def rows_kernel(count, chunks, unit, late, *refs):
     msgs = [refs[k * chunks : (k + 1) * chunks] for k in range(count)]
-    cov_ref, near_ref, mix_ref, out_ref, next_ref, bufs, bits_v, bits_s, dense, sem = refs[count * chunks :]
+    refs = refs[count * chunks :]
+    cov_ref, near_ref, mix_ref = refs[:3]
+    if late:
+        start_ref, done_ref, out_ref, turned_ref = refs[3:7]
+    else:
+        out_ref, next_ref = refs[3:5]
+    bufs, bits_v, bits_s, dense, sem = refs[-5:]
     times, lanes = bufs.shape[2:]
     cells = near_ref.shape[1]
     blocks = cells // lanes
     rows = out_ref.shape[0]
     deep = -(-rows * blocks // lanes)
-    limit = sum(chunk.shape[0] for chunk in msgs[0])
     copies = [fetch(msgs[k], bufs.at[k], sem.at[k]) for k in range(count)]
     for k in range(count):
         for copy in copies[k]:
             copy.wait()
         read_head(bufs.at[k], rows, blocks, bits_v.at[k])
-    copy_in(bits_v, bits_s, sem.at[count, 0])
-    ready = jnp.int32(0)
-    for u in range(rows // unit):
-        whole = jnp.int32(1)
-        for k in range(count):
-            whole = whole * (bits_s[k, deep, (u + 1) * unit - 1] <= limit).astype(I32)
-        ready = ready + whole
-    next_ref[0] = ready
+    copy = pltpu.make_async_copy(bits_v, bits_s, sem.at[count, 0])
+    copy.start()
 
     def step(u, _):
         for k in range(count):
             expand(bufs.at[k], bits_s.at[k], u * unit, unit, blocks, into(dense, times, lanes, k * cells))
         here = aligned(u * unit * times, unit * times)
         value = near_ref[here, :] + jnp.dot(dense[...], cov_ref[...], preferred_element_type=F32)
-        out_ref[aligned(u * unit, unit)] = mixed_unit(mix_ref, value).reshape(unit, times, cells)
+        mixed = mixed_unit(mix_ref, value)
+        at = aligned(u * unit, unit)
+        out_ref[at] = mixed.reshape(unit, times, cells)
+        if late:
+            turned_ref[:, at, :] = turn(mixed, unit, times)
         return 0
 
-    lax.fori_loop(0, ready, step, 0)
-
-
-def first_rows(msgs, cov, near, mix, rows, unit, slots):
+    def carry_over(u, _):
+        at = aligned(u * unit, unit)
+        value = done_ref[at]
+        out_ref[at] = value
+        turned_ref[:, at, :] = turn(value.reshape(unit * times, cells), unit, times)
+        return 0
+
+    if late:
+        first = start_ref[0]
+        lax.fori_loop(0, first, carry_over, 0)
+        copy.wait()
+        lax.fori_loop(first, rows // unit, step, 0)
+    else:
+        copy.wait()
+        limit = sum(chunk.shape[0] for chunk in msgs[0])
+        ready = jnp.int32(0)
+        for u in range(rows // unit):
+            whole = jnp.int32(1)
+            for k in range(count):
+                whole = whole * (bits_s[k, deep, (u + 1) * unit - 1] <= limit).astype(I32)
+            ready = ready + whole
+        next_ref[0] = ready
+        lax.fori_loop(0, ready, step, 0)
+
+
+def some_rows(msgs, cov, near, mix, rows, unit, slots, carried=None):
     times, lanes = msgs[0][0].shape[1:]
     cells = near.shape[1]
     count, chunks = len(msgs), len(msgs[0])
+    late = carried is not None
     flat = [chunk for msg in msgs for chunk in msg]
+    out = shape_of((rows, times, cells), BF16)
     return pl.pallas_call(
-        functools.partial(first_kernel, count, chunks, unit),
-        out_shape=(shape_of((rows, times, cells), BF16), shape_of((1,), I32)),
-        in_specs=[ANY] * len(flat) + [VMEM] * 3,
-        out_specs=(VMEM, SMEM),
+        functools.partial(rows_kernel, count, chunks, unit, late),
+        out_shape=(out, shape_of((times, rows, cells), BF16) if late else shape_of((1,), I32)),
+        in_specs=[ANY] * len(flat) + [VMEM] * 3 + ([SMEM, VMEM] if late else []),
+        out_specs=(VMEM, VMEM if late else SMEM),
         scratch_shapes=[
             pltpu.VMEM((count, slots, times, lanes), BF16),
             pltpu.VMEM((count, 8, lanes), I32),
@@ -476,128 +496,10 @@
             pltpu.VMEM((unit * times, count * cells), BF16),
             pltpu.SemaphoreType.DMA((count + 1, chunks)),
         ],
-        compiler_params=params(20),
+        compiler_params=params(16),
         cost_estimate=cost(6),
-        name="first_rows",
-    )(*flat, cov, near, mix)
-
-
-def last_kernel(count, chunks, pieces, unit, each, *refs):
-    msgs = [refs[k * chunks : (k + 1) * chunks] for k in range(count)]
-    panel_msgs = refs[count * chunks : count * chunks + pieces]
-    refs = refs[count * chunks + pieces :]
-    start_ref, sources_ref, cov_ref, near_ref, mix_ref, done_ref, out_ref, part_ref = refs[:8]
-    bufs, panel_bufs, bits_v, bits_s, dense, turned, panel, sem, panel_sem = refs[8:]
-    times, lanes = bufs.shape[2:]
-    cells = near_ref.shape[1]
-    blocks = cells // lanes
-    rows = out_ref.shape[0]
-    copies = [fetch(msgs[k], bufs.at[k], sem.at[k]) for k in range(count)]
-    panel_copies = [
-        pltpu.make_async_copy(panel_msgs[k], panel_bufs.at[k], panel_sem.at[k]) for k in range(pieces)
-    ]
-    for copy in panel_copies:
-        copy.start()
-    for k in range(count):
-        for copy in copies[k]:
-            copy.wait()
-        read_head(bufs.at[k], rows, blocks, bits_v.at[k])
-    for k in range(pieces):
-        panel_copies[k].wait()
-        read_head(panel_bufs.at[k], each, blocks, bits_v.at[count + k], flagged=True)
-    copy_in(bits_v, bits_s, sem.at[count, 0])
-    first = start_ref[0]
-
-    def step(u, _):
-        for k in range(count):
-            expand(bufs.at[k], bits_s.at[k], u * unit, unit, blocks, into(dense, times, lanes, k * cells))
-        here = aligned(u * unit * times, unit * times)
-        value = near_ref[here, :] + jnp.dot(dense[...], cov_ref[...], preferred_element_type=F32)
-        mixed = mixed_unit(mix_ref, value)
-        out_ref[aligned(u * unit, unit)] = mixed.reshape(unit, times, cells)
-        turned[:, aligned(u * unit, unit), :] = turn(mixed, unit, times)
-        return 0
-
-    lax.fori_loop(first, rows // unit, step, 0)
-
-    def earlier(u, _):
-        at = aligned(u * unit, unit)
-        value = done_ref[at]
-        out_ref[at] = value
-        value = value.reshape(unit * times, cells)
-        turned[:, aligned(u * unit, unit), :] = turn(value, unit, times)
-        return 0
-
-    lax.fori_loop(0, first, earlier, 0)
-
-    deep = -(-each * blocks // lanes)
-    over = jnp.int32(0)
-    for k in range(pieces):
-        over = over + (bits_s[count + k, deep, each - 1] > panel_bufs.shape[1] - 1).astype(I32)
-        over = over + bits_s[count + k, deep + 1, 0]
-
-    group = max(1, 16 // each)
-    placed = each % 16 == 0
-
-    @pl.loop(0, pieces // group)
-    def _(g):
-        at = pl.multiple_of((sources_ref[g] if placed else g) * each * group, 16)
-        for b in range(blocks):
-            tiles = []
-            for i in range(group * each):
-                k, place = g * group + i // each, i % each * blocks + b
-                tiles.append(panel_bufs[k, bits_s[count + k, place // lanes, place % lanes]])
-            value = turn(jnp.concatenate(tiles, axis=0), group * each, times)
-            panel[:, pl.ds(at, group * each), b * lanes : (b + 1) * lanes] = value
-
-    total = None
-    for t in range(times):
-        value = lax.dot_general(
-            turned[t], panel[t], (((1,), (1,)), ((), ())), preferred_element_type=F32
-        )
-        total = value if total is None else total + value
-    if not placed:
-        size = pieces * each
-        row = lax.broadcasted_iota(I32, (size, size), 0)
-        target = row
-        for k in range(pieces):
-            target = jnp.where(row // each == k, sources_ref[k] * each + row % each, target)
-        select = (lax.broadcasted_iota(I32, (size, size), 1) == target).astype(F32).astype(BF16)
-        value, total = total, jnp.zeros(total.shape, F32)
-        for _ in range(3):
-            high = value.astype(BF16)
-            total = total + jnp.dot(high, select, preferred_element_type=F32)
-            value = value - high.astype(F32)
-    part_ref[0:rows, :] = total
-    part_ref[rows:, :] = jnp.broadcast_to(over, (8, pieces * each)).astype(F32)
-
-
-def last_rows(msgs, panel_msgs, start, sources, cov, near, mix, done, unit, each):
-    times, lanes = panel_msgs[0].shape[1:]
-    rows, _, cells = done.shape
-    count, chunks, pieces = len(msgs), len(msgs[0]), len(panel_msgs)
-    slots = sum(chunk.shape[0] for chunk in msgs[0])
-    flat = [chunk for msg in msgs for chunk in msg] + list(panel_msgs)
-    return pl.pallas_call(
-        functools.partial(last_kernel, count, chunks, pieces, unit, each),
-        out_shape=(shape_of(done.shape, BF16), shape_of((rows + 8, pieces * each), F32)),
-        in_specs=[ANY] * len(flat) + [SMEM, SMEM] + [VMEM] * 4,
-        out_specs=(VMEM, VMEM),
-        scratch_shapes=[
-            pltpu.VMEM((count, slots, times, lanes), BF16),
-            pltpu.VMEM((pieces, panel_msgs[0].shape[0], times, lanes), BF16),
-            pltpu.VMEM((count + pieces, 8, lanes), I32),
-            pltpu.SMEM((count + pieces, 8, lanes), I32),
-            pltpu.VMEM((unit * times, count * cells), BF16),
-            pltpu.VMEM((times, rows, cells), BF16),
-            pltpu.VMEM((times, pieces * each, cells), BF16),
-            pltpu.SemaphoreType.DMA((count + 1, chunks)),
-            pltpu.SemaphoreType.DMA((pieces,)),
-        ],
-        compiler_params=params(36),
-        cost_estimate=cost(10),
-        name="last_rows",
-    )(*flat, start, sources, cov, near, mix, done)
+        name="late_rows" if late else "first_rows",
+    )(*flat, cov, near, mix, *(carried or ()))
 
 
 def mix_kernel(unit, time_ref, out_ref):
@@ -630,6 +532,95 @@
         cost_estimate=cost(1),
         name="mixing",
     )(time_cov)
+
+
+def panel_kernel(pieces, each, final, *refs):
+    msgs = refs[:pieces]
+    refs = refs[pieces:]
+    if final:
+        sources_ref, turned, before_ref, over_ref, out_ref = refs[:5]
+    else:
+        turned, out_ref, over_ref = refs[:3]
+    bufs, bits_v, bits_s, panel, sem = refs[-5:]
+    slots, times, lanes = bufs.shape[1:]
+    rows, cells = turned.shape[1:]
+    blocks = cells // lanes
+    deep = -(-each * blocks // lanes)
+    copies = [pltpu.make_async_copy(msg, bufs.at[k], sem.at[k]) for k, msg in enumerate(msgs)]
+    for copy in copies:
+        copy.start()
+    for k, copy in enumerate(copies):
+        copy.wait()
+        read_head(bufs.at[k], each, blocks, bits_v.at[k], flagged=True)
+    copy_in(bits_v, bits_s, sem.at[pieces])
+    over = over_ref[0] if final else jnp.int32(0)
+    for k in range(pieces):
+        over = over + (bits_s[k, deep, each - 1] > slots - 1).astype(I32) + bits_s[k, deep + 1, 0]
+    group = max(1, 16 // each)
+
+    @pl.loop(0, pieces // group)
+    def _(g):
+        for b in range(blocks):
+            tiles = []
+            for i in range(group * each):
+                k, place = g * group + i // each, i % each * blocks + b
+                tiles.append(bufs[k, bits_s[k, place // lanes, place % lanes]])
+            value = turn(jnp.concatenate(tiles, axis=0), group * each, times)
+            panel[:, aligned(g * group * each, group * each), b * lanes : (b + 1) * lanes] = value
+
+    total = None
+    for t in range(times):
+        value = lax.dot_general(turned[t], panel[t], (((1,), (1,)), ((), ())), preferred_element_type=F32)
+        total = value if total is None else total + value
+    if not final:
+        out_ref[...] = total
+        over_ref[0] = over
+        return
+    value = jnp.concatenate([before_ref[...], total], axis=1)
+    size = value.shape[1]
+    row = lax.broadcasted_iota(I32, (size, size), 0)
+    target = row
+    for k in range(size // each):
+        target = jnp.where(row // each == k, sources_ref[k] * each + row % each, target)
+    select = (lax.broadcasted_iota(I32, (size, size), 1) == target).astype(F32).astype(BF16)
+    total = jnp.zeros(value.shape, F32)
+    for _ in range(3):
+        high = value.astype(BF16)
+        total = total + jnp.dot(high, select, preferred_element_type=F32)
+        value = value - high.astype(F32)
+    out_ref[0:rows, :] = total
+    out_ref[rows:, :] = jnp.broadcast_to(over, (8, size)).astype(F32)
+
+
+def panel_part(msgs, turned, each, final=None):
+    slots, times, lanes = msgs[0].shape
+    rows, cells = turned.shape[1:]
+    pieces = len(msgs)
+    width = pieces * each
+    if final:
+        sources, before, over = final
+        operands, in_specs = (sources, turned, before, over), [SMEM, VMEM, VMEM, SMEM]
+        out_shape = shape_of((rows + 8, before.shape[1] + width), F32)
+        out_specs = VMEM
+    else:
+        operands, in_specs = (turned,), [VMEM]
+        out_shape, out_specs = (shape_of((rows, width), F32), shape_of((1,), I32)), (VMEM, SMEM)
+    return pl.pallas_call(
+        functools.partial(panel_kernel, pieces, each, bool(final)),
+        out_shape=out_shape,
+        in_specs=[ANY] * pieces + in_specs,
+        out_specs=out_specs,
+        scratch_shapes=[
+            pltpu.VMEM((pieces, slots, times, lanes), BF16),
+            pltpu.VMEM((pieces, 8, lanes), I32),
+            pltpu.SMEM((pieces, 8, lanes), I32),
+            pltpu.VMEM((times, width, cells), BF16),
+            pltpu.SemaphoreType.DMA((pieces + 1,)),
+        ],
+        compiler_params=params(14),
+        cost_estimate=cost(3 if final else 5),
+        name="panel_last" if final else "panel_first",
+    )(*msgs, *operands)
 
 
 def partner(value, axis, count):
@@ -717,12 +708,21 @@
     near, mate_dense, mate_cov, info = own_call(own_msg, mate_msg, obs_rows, cell_local)
     near, far_cov = mate_call([msg[0] for msg in far_msgs], near, mate_dense, mate_cov, info)
     mix = mixing(time_cov, unit)
-    cov_product, start = first_rows([msg[:1] for msg in far_msgs], far_cov, near, mix, obs_rows, unit, slots)
-    cov_product, part = last_rows(far_msgs, messages, start, sources, far_cov, near, mix, cov_product, unit, each)
+    first_cov, start = some_rows([msg[:1] for msg in far_msgs], far_cov, near, mix, obs_rows, unit, slots)
+    cov_product, turned = some_rows(far_msgs, far_cov, near, mix, obs_rows, unit, slots, (start, first_cov))
+    cut = len(messages) * 3 // 4
+    before, over = panel_part(messages[:cut], turned, each)
+    part = panel_part(messages[cut:], turned, each, (sources, before, over))
+
+    def innovation_of(total):
+        positions = jnp.arange(obs_rows, dtype=I32)
+        on_diagonal = ((group * obs_rows + positions)[:, None] == panel_index[None, :]).astype(F32)
+        return total + error_var[:, None] * on_diagonal
+
     total = add_cells(part, cells)
 
     def again(carry):
-        wanted = carry[1][obs_rows, 0] > 0
+        wanted = carry[0]
         mask, cell_info, place, from_group = (
             jnp.where(wanted, value, 0) for value in (block_mask, info, group, sources)
         )
@@ -730,13 +730,10 @@
         cov_product, total = dense_way(
             cells, observers, footprint, mask, cell_info, time_cov, mine, from_group
         )
-        return cov_product, jnp.pad(total, ((0, 8), (0, 0)))
-
-    cov_product, total = lax.while_loop(lambda carry: carry[1][obs_rows, 0] > 0, again, (cov_product, total))
-    total = total[:obs_rows]
-    positions = jnp.arange(obs_rows, dtype=I32)
-    on_diagonal = ((group * obs_rows + positions)[:, None] == panel_index[None, :]).astype(F32)
-    return cov_product, total + error_var[:, None] * on_diagonal
+        return jnp.bool_(False), cov_product, innovation_of(total)
+
+    carry = (total[obs_rows, 0] > 0, cov_product, innovation_of(total[:obs_rows]))
+    return lax.while_loop(lambda carry: carry[0], again, carry)[1:]
 
 
 def solution(mesh):

time: 91.6 us -> 86.1 us (0.940)
  waiting for transfers between devices: 25.2 us -> 18.1 us
  Pallas kernels: 44.1 us -> 47.2 us
    ppermute x8, waiting for transfers between devices: 20.4 us -> 15.3 us  [shifted(): lax.ppermute(value, axis, [(i, (i + 2 * shift) % count ^ flip) for i in r...]
    pallas_call x2 -> x4, Pallas kernels: 20.4 us -> 24 us  [the longest x2 15.2 us: some_rows(): pl.pallas_call(functools.partial(rows_kernel, count, chunks, unit, late),...]
    ppermute x8, starting transfers between devices: 7.07 us -> 4.96 us  [partner(): return lax.ppermute(value, axis, [(i, i ^ 1) for i in range(count)])]
    ppermute x8, waiting for transfers between devices: 4.8 us -> 2.83 us  [partner(): return lax.ppermute(value, axis, [(i, i ^ 1) for i in range(count)])]
    unnamed x20 -> x17, local copies, waits for them, and re-layouts: 2.89 us -> 4.42 us
    ppermute x8, starting transfers between devices: 6.64 us -> 7.86 us  [shifted(): lax.ppermute(value, axis, [(i, (i + 2 * shift) % count ^ flip) for i in r...]
  transfers between devices with their start and end apart: 16 -> 16, of which waited for: 6 -> 7; matrix products, arithmetic and copies ran while one was open for 1% -> 0% of each run, Pallas kernels for 29% -> 46%
where the time goes in v1:
time: 86.1 us; the launch traced here: 85.6 us
  Pallas kernels  47.2 us (55%)
  waiting for transfers between devices  18.1 us (21%)
  starting transfers between devices  12.8 us (15%)
  local copies, waits for them, and re-layouts  5 us (6%)
  between operations  1.45 us (2%)
    ppermute x8, waiting for transfers between devices, shifted(): lax.ppermute(value, axis, [(i, (i + 2 * shift) % count ^ flip) for i in r...  15.3 us
    pallas_call x2, Pallas kernels, some_rows(): pl.pallas_call(functools.partial(rows_kernel, count, chunks, unit, late),...  15.2 us
    pallas_call x1, Pallas kernels, own_call(): pl.pallas_call(functools.partial(own_kernel, chunks), out_shape=(shape_of...  9.39 us
    pallas_call x2, Pallas kernels, panel_part(): pl.pallas_call(functools.partial(panel_kernel, pieces, each, bool(final))...  8.85 us
    ppermute x8, starting transfers between devices, shifted(): lax.ppermute(value, axis, [(i, (i + 2 * shift) % count ^ flip) for i in r...  7.86 us
    pallas_call x1, Pallas kernels, mate_call(): pl.pallas_call(functools.partial(mate_kernel, count), out_shape=(shape_of...  6.7 us
    ppermute x8, starting transfers between devices, partner(): return lax.ppermute(value, axis, [(i, i ^ 1) for i in range(count)])  4.96 us
    unnamed x17, local copies, waits for them, and re-layouts  4.42 us
  transfers between devices with their start and end apart: 16, of which 7 were waited for; matrix products, arithmetic and copies ran while one was open for 0% of the time, Pallas kernels for 46%

profile of v1, /device:TPU:0, one launch (start us, length us, event | category | flops | bytes accessed | tf_op | source)
XLA Modules:
  0.0 85.6 jit_solution(12299776538797480446)
XLA Ops:
  1.3 0.7 copy-done.2
  2.7 3.8 %pack_feet.1 = (bf16[157,16,128]{2,1,0:T(8,128)(2,1)S(1)}, bf16[157,16,128]{2,1,0:T(8,128)(2,1)S(1)}) custom-call(s32[8,64]{1,0:T(8,128)S(1)} %bitcast.79, s32[2,1024]{1,0:T(2,128)S(1)} %copy-done.2, f32[1,1024]{1,0:T(1,128)S(1)} %bitcast.82, bf16[64,16,1024]{2,1,0:T(8,128)(2,1)} %feet_ref.3), custom_call_target="tpu_custom_call" | custom-call | flops 2700000000 | bytes 1000000 | tf_op jit(solution)/shard_map/pack_feet/pallas_call | solution.py:150
  7.1 2.6 %collective-permute-start.11 = (bf16[157,16,128]{2,1,0:T(8,128)(2,1)S(1)}, bf16[157,16,128]{2,1,0:T(8,128)(2,1)S(1)}, u32[]{:S(2)}, u32[]{:S(2)}) collective-permute-start(bf16[157,16,128]{2,1,0:T(8,128)(2,1)S(1)} %get-tuple-element.121.refs_0_), channel_id=1, source_target_pairs={{0,2},{1,3},{2,0},{3,1},{4,6},{5,7},{6,4},{7,5},{8,10},{9,11},{10,... | collective-permute-start | bytes 1929224 | tf_op jit(solution)/shard_map/ppermute | solution.py:631
  9.8 3.0 %pack_panel.1.refs_0_ = bf16[90,16,128]{2,1,0:T(8,128)(2,1)} custom-call(s32[8,64]{1,0:T(8,128)S(1)} %bitcast.80, s32[8,64]{1,0:T(8,128)S(1)} %bitcast.81, s32[128]{0:T(128)S(1)} %copy-done.7, s32[1]{0:T(128)} %bitcast.3.group_ref, bf16[64,16,1024]{2,1,0:T(8,128)(2,1)} %feet_ref.3), custom_call_target="tpu_custom_call" | custom-call | flops 1800000000 | bytes 1000000 | tf_op jit(solution)/shard_map/pack_panel/pallas_call | solution.py:199
  12.8 1.6 %collective-permute-start.7 = (bf16[90,16,128]{2,1,0:T(8,128)(2,1)}, bf16[90,16,128]{2,1,0:T(8,128)(2,1)}, u32[]{:S(2)}, u32[]{:S(2)}) collective-permute-start(bf16[90,16,128]{2,1,0:T(8,128)(2,1)} %pack_panel.1.refs_0_), channel_id=1, source_target_pairs={{0,8},{4,12},{8,16},{12,20},{16,24},{20,28},{24,0},{28,4},{1,9},{5... | collective-permute-start | bytes 1105928 | tf_op jit(solution)/shard_map/ppermute | solution.py:631
  15.4 10.5 %collective-permute-done.7.refs_2_ = bf16[90,16,128]{2,1,0:T(8,128)(2,1)} collective-permute-done((bf16[90,16,128]{2,1,0:T(8,128)(2,1)}, bf16[90,16,128]{2,1,0:T(8,128)(2,1)}, u32[]{:S(2)}, u32[]{:S(2)}) %collective-permute-start.7) | collective-permute-done | bytes 368672 | tf_op jit(solution)/shard_map/ppermute | solution.py:631
  25.9 1.5 %collective-permute-start.17 = (bf16[90,16,128]{2,1,0:T(8,128)(2,1)}, bf16[90,16,128]{2,1,0:T(8,128)(2,1)S(1)}, u32[]{:S(2)}, u32[]{:S(2)}) collective-permute-start(bf16[90,16,128]{2,1,0:T(8,128)(2,1)} %pack_panel.1.refs_0_), channel_id=1, source_target_pairs={{0,4},{4,0},{8,12},{12,8},{16,20},{20,16},{24,28},{28,24},{1,5},{5... | collective-permute-start | bytes 1105928 | tf_op jit(solution)/shard_map/ppermute | solution.py:627
  27.5 9.4 %own_product.1 = (f32[1024,1024]{1,0:T(8,128)S(1)}, bf16[1024,1024]{1,0:T(8,128)(2,1)S(1)}, bf16[1024,1024]{1,0:T(8,128)(2,1)S(1)}, f32[8,1024]{1,0:T(8,128)S(1)}) custom-call(bf16[157,16,128]{2,1,0:T(8,128)(2,1)S(1)} %get-tuple-element.121.refs_0_, bf16[157,16,128]{2,1,0:T(8,128)(2,1)S(1)} %get-tuple-element.122.refs_1_, ...), custom_call_target="tpu_custom_call" | custom-call | flops 8099999744 | bytes 1000000 | tf_op jit(solution)/shard_map/own_product/pallas_call | solution.py:339
  37.4 1.0 %collective-permute-done.12.refs_1_ = bf16[157,16,128]{2,1,0:T(8,128)(2,1)S(1)} collective-permute-done((bf16[157,16,128]{2,1,0:T(8,128)(2,1)S(1)}, bf16[157,16,128]{2,1,0:T(8,128)(2,1)S(1)}, u32[]{:S(2)}, u32[]{:S(2)}) %collective-permute-start.12) | collective-permute-done | bytes 643104 | tf_op jit(solution)/shard_map/ppermute | solution.py:631
  39.2 1.2 %collective-permute-start.9 = (bf16[90,16,128]{2,1,0:T(8,128)(2,1)S(1)}, bf16[90,16,128]{2,1,0:T(8,128)(2,1)S(1)}, u32[]{:S(2)}, u32[]{:S(2)}) collective-permute-start(bf16[90,16,128]{2,1,0:T(8,128)(2,1)S(1)} %collective-permute-done.8.refs_4_), channel_id=1, source_target_pairs={{0,8},{4,12},{8,16},{12,20},{16,24},{20,28},{24,0},{28,4},{1,9},{5... | collective-permute-start | bytes 1105928 | tf_op jit(solution)/shard_map/ppermute | solution.py:631
  40.3 6.7 %mate_product.1 = (f32[1024,1024]{1,0:T(8,128)S(1)}, bf16[2048,1024]{1,0:T(8,128)(2,1)S(1)}) custom-call(bf16[157,16,128]{2,1,0:T(8,128)(2,1)S(1)} %collective-permute-done.11.refs_0_, bf16[157,16,128]{2,1,0:T(8,128)(2,1)S(1)} %collective-permute-done.13.refs_1_.refs_2_, ...), custom_call_target="tpu_custom_call", output_to_operand_aliasing={{0}: (2, {})} | custom-call | flops 7200000000 | bytes 1000000 | tf_op jit(solution)/shard_map/mate_product/pallas_call | solution.py:393
  47.0 6.6 %first_rows.1 = (bf16[64,16,1024]{2,1,0:T(8,128)(2,1)S(1)}, s32[1]{0:T(128)}) custom-call(bf16[157,16,128]{2,1,0:T(8,128)(2,1)S(1)} %collective-permute-done.11.refs_0_, bf16[157,16,128]{2,1,0:T(8,128)(2,1)S(1)} %collective-permute-done.13.refs_1_.refs_2_, bf16[2048,1024]{1,0:T(8,128)(2,1)S(1)} %get-tuple-element.127.refs_2_.refs_4_, ...), custom_call_target="tpu_custom_call" | custom-call | flops 5400000000 | bytes 1000000 | tf_op jit(solution)/shard_map/first_rows/pallas_call | solution.py:487
  53.6 1.6 %collective-permute-start.19 = (bf16[90,16,128]{2,1,0:T(8,128)(2,1)S(1)}, bf16[90,16,128]{2,1,0:T(8,128)(2,1)S(1)}, u32[]{:S(2)}, u32[]{:S(2)}) collective-permute-start(bf16[90,16,128]{2,1,0:T(8,128)(2,1)S(1)} %collective-permute-done.8.refs_4_), channel_id=1, source_target_pairs={{0,4},{4,0},{8,12},{12,8},{16,20},{20,16},{24,28},{28,24},{1,5},{5... | collective-permute-start | bytes 1105928 | tf_op jit(solution)/shard_map/ppermute | solution.py:627
  55.7 8.6 %late_rows.1 = (bf16[64,16,1024]{2,1,0:T(8,128)(2,1)}, bf16[16,64,1024]{2,1,0:T(8,128)(2,1)S(1)}) custom-call(bf16[157,16,128]{2,1,0:T(8,128)(2,1)S(1)} %collective-permute-done.11.refs_0_, bf16[157,16,128]{2,1,0:T(8,128)(2,1)S(1)} %collective-permute-done.12.refs_1_, bf16[157,16,128]{2,1,0:T(8,128)(2,1)S(1)} %collective-permute-done.13.refs_1_.refs_2_, ...), custom_call_target="tpu_custom_call" | custom-call | flops 5400000000 | bytes 1000000 | tf_op jit(solution)/shard_map/late_rows/pallas_call | solution.py:487
  64.4 0.8 collective-permute-done.19.refs_5_
  65.1 5.1 %panel_first.1 = (f32[64,96]{1,0:T(8,128)S(1)}, s32[1]{0:T(128)}) custom-call(bf16[90,16,128]{2,1,0:T(8,128)(2,1)} %pack_panel.1.refs_0_, bf16[90,16,128]{2,1,0:T(8,128)(2,1)S(1)} %collective-permute-done.17.refs_1_, bf16[90,16,128]{2,1,0:T(8,128)(2,1)} %collective-permute-done.7.refs_2_, bf16[90,16,128]{2,1,0:T(8,128)(2,1)S(1)} %collective-permute-done.18.refs_3_, ...), custom_call_target="tpu_custom_call" | custom-call | flops 4499999744 | bytes 1000000 | tf_op jit(solution)/shard_map/panel_first/pallas_call | solution.py:608
  70.3 2.0 %collective-permute-done.10.refs_1_ = bf16[90,16,128]{2,1,0:T(8,128)(2,1)S(1)} collective-permute-done((bf16[90,16,128]{2,1,0:T(8,128)(2,1)S(1)}, bf16[90,16,128]{2,1,0:T(8,128)(2,1)S(1)}, u32[]{:S(2)}, u32[]{:S(2)}) %collective-permute-start.10) | collective-permute-done | bytes 368672 | tf_op jit(solution)/shard_map/ppermute | solution.py:627
  72.3 3.7 %panel_last.1 = f32[72,128]{1,0:T(8,128)S(1)} custom-call(bf16[90,16,128]{2,1,0:T(8,128)(2,1)S(1)} %collective-permute-done.9.refs_0_, bf16[90,16,128]{2,1,0:T(8,128)(2,1)S(1)} %collective-permute-done.10.refs_1_, s32[8]{0:T(128)S(1)} %fusion.22.refs_2_, bf16[16,64,1024]{2,1,0:T(8,128)(2,1)S(1)} %get-tuple-element.131.refs_6_.refs_3_, ...), custom_call_target="tpu_custom_call" | custom-call | flops 2700000000 | bytes 1000000 | tf_op jit(solution)/shard_map/panel_last/pallas_call | solution.py:608
  76.1 1.6 %collective-permute-start.21 = (f32[72,128]{1,0:T(8,128)S(1)}, f32[72,128]{1,0:T(8,128)S(1)}, u32[]{:S(2)}, u32[]{:S(2)}) collective-permute-start(f32[72,128]{1,0:T(8,128)S(1)} %panel_last.1), channel_id=1, source_target_pairs={{0,2},{1,3},{2,0},{3,1},{4,6},{5,7},{6,4},{7,5},{8,10},{9,11},{10,... | collective-permute-start | bytes 110600 | tf_op jit(solution)/shard_map/ppermute | solution.py:631
  78.1 2.1 %collective-permute-done.21 = f32[72,128]{1,0:T(8,128)S(1)} collective-permute-done((f32[72,128]{1,0:T(8,128)S(1)}, f32[72,128]{1,0:T(8,128)S(1)}, u32[]{:S(2)}, u32[]{:S(2)}) %collective-permute-start.21) | collective-permute-done | bytes 36896 | tf_op jit(solution)/shard_map/ppermute | solution.py:631
  80.1 1.0 %collective-permute-done.22 = f32[72,128]{1,0:T(8,128)S(1)} collective-permute-done((f32[72,128]{1,0:T(8,128)S(1)}, f32[72,128]{1,0:T(8,128)S(1)}, u32[]{:S(2)}, u32[]{:S(2)}) %collective-permute-start.22) | collective-permute-done | bytes 36896 | tf_op jit(solution)/shard_map/ppermute | solution.py:631
  81.7 0.7 slice_add_fusion
  82.5 0.7 copy.15
  84.1 1.5 %copy.17 = f32[64,128]{1,0:T(8,128)} copy(f32[64,128]{0,1:T(8,128)} %get-tuple-element.215) | data formatting | bytes 65536
  (40 shorter events, 6.1 us)
Async XLA Ops:
  0.6 0.7 copy-start
  1.3 0.7 copy-start.2
  2.0 0.7 copy-start.3
  2.7 7.1 %copy-start.1 = (s32[64,8]{0,1:T(8,128)S(1)}, s32[64,8]{0,1:T(8,128)}, u32[]{:S(2)}) copy-start(s32[64,8]{0,1:T(8,128)} %param.14) | copy-start | bytes 6148
  2.7 7.1 %copy-start.7 = (s32[128]{0:T(128)S(1)}, s32[128]{0:T(128)}, u32[]{:S(2)}) copy-start(s32[128]{0:T(128)} %index_ref.1) | copy-start | bytes 1540
  6.5 7.9 %copy-start.5 = (f32[16,16]{1,0:T(8,128)S(1)}, f32[16,16]{1,0:T(8,128)}, u32[]{:S(2)}) copy-start(f32[16,16]{1,0:T(8,128)} %time_ref.1) | copy-start | bytes 3076
  6.5 20.8 %collective-permute-start.15 = (bf16[157,16,128]{2,1,0:T(8,128)(2,1)S(1)}, bf16[157,16,128]{2,1,0:T(8,128)(2,1)S(1)}, u32[]{:S(2)}, u32[]{:S(2)}) collective-permute-start(bf16[157,16,128]{2,1,0:T(8,128)(2,1)S(1)} %get-tuple-element.121.refs_0_), channel_id=1, source_target_pairs={{0,1},{1,0},{2,3},{3,2},{4,5},{5,4},{6,7},{7,6},{8,9},{9,8},{10,11... | collective-permute-start | bytes 1929224 | tf_op jit(solution)/shard_map/ppermute | solution.py:627
  7.1 20.3 %collective-permute-start.11 = (bf16[157,16,128]{2,1,0:T(8,128)(2,1)S(1)}, bf16[157,16,128]{2,1,0:T(8,128)(2,1)S(1)}, u32[]{:S(2)}, u32[]{:S(2)}) collective-permute-start(bf16[157,16,128]{2,1,0:T(8,128)(2,1)S(1)} %get-tuple-element.121.refs_0_), channel_id=1, source_target_pairs={{0,2},{1,3},{2,0},{3,1},{4,6},{5,7},{6,4},{7,5},{8,10},{9,11},{10,... | collective-permute-start | bytes 1929224 | tf_op jit(solution)/shard_map/ppermute | solution.py:631
  9.6 17.8 %collective-permute-start.16 = (bf16[157,16,128]{2,1,0:T(8,128)(2,1)S(1)}, bf16[157,16,128]{2,1,0:T(8,128)(2,1)S(1)}, u32[]{:S(2)}, u32[]{:S(2)}) collective-permute-start(bf16[157,16,128]{2,1,0:T(8,128)(2,1)S(1)} %get-tuple-element.122.refs_1_), channel_id=1, source_target_pairs={{0,1},{1,0},{2,3},{3,2},{4,5},{5,4},{6,7},{7,6},{8,9},{9,8},{10,11... | collective-permute-start | bytes 1929224 | tf_op jit(solution)/shard_map/ppermute | solution.py:627
  12.8 13.1 %collective-permute-start.7 = (bf16[90,16,128]{2,1,0:T(8,128)(2,1)}, bf16[90,16,128]{2,1,0:T(8,128)(2,1)}, u32[]{:S(2)}, u32[]{:S(2)}) collective-permute-start(bf16[90,16,128]{2,1,0:T(8,128)(2,1)} %pack_panel.1.refs_0_), channel_id=1, source_target_pairs={{0,8},{4,12},{8,16},{12,20},{16,24},{20,28},{24,0},{28,4},{1,9},{5... | collective-permute-start | bytes 1105928 | tf_op jit(solution)/shard_map/ppermute | solution.py:631
  14.8 23.7 %collective-permute-start.12 = (bf16[157,16,128]{2,1,0:T(8,128)(2,1)S(1)}, bf16[157,16,128]{2,1,0:T(8,128)(2,1)S(1)}, u32[]{:S(2)}, u32[]{:S(2)}) collective-permute-start(bf16[157,16,128]{2,1,0:T(8,128)(2,1)S(1)} %get-tuple-element.122.refs_1_), channel_id=1, source_target_pairs={{0,2},{1,3},{2,0},{3,1},{4,6},{5,7},{6,4},{7,5},{8,10},{9,11},{10,... | collective-permute-start | bytes 1929224 | tf_op jit(solution)/shard_map/ppermute | solution.py:631
  25.9 38.5 %collective-permute-start.17 = (bf16[90,16,128]{2,1,0:T(8,128)(2,1)}, bf16[90,16,128]{2,1,0:T(8,128)(2,1)S(1)}, u32[]{:S(2)}, u32[]{:S(2)}) collective-permute-start(bf16[90,16,128]{2,1,0:T(8,128)(2,1)} %pack_panel.1.refs_0_), channel_id=1, source_target_pairs={{0,4},{4,0},{8,12},{12,8},{16,20},{20,16},{24,28},{28,24},{1,5},{5... | collective-permute-start | bytes 1105928 | tf_op jit(solution)/shard_map/ppermute | solution.py:627
  27.4 11.8 %collective-permute-start.8 = (bf16[90,16,128]{2,1,0:T(8,128)(2,1)}, bf16[90,16,128]{2,1,0:T(8,128)(2,1)S(1)}, u32[]{:S(2)}, u32[]{:S(2)}) collective-permute-start(bf16[90,16,128]{2,1,0:T(8,128)(2,1)} %collective-permute-done.7.refs_2_), channel_id=1, source_target_pairs={{0,8},{4,12},{8,16},{12,20},{16,24},{20,28},{24,0},{28,4},{1,9},{5... | collective-permute-start | bytes 1105928 | tf_op jit(solution)/shard_map/ppermute | solution.py:631
  27.4 12.9 %collective-permute-start.13 = (bf16[157,16,128]{2,1,0:T(8,128)(2,1)S(1)}, bf16[157,16,128]{2,1,0:T(8,128)(2,1)S(1)}, u32[]{:S(2)}, u32[]{:S(2)}) collective-permute-start(bf16[157,16,128]{2,1,0:T(8,128)(2,1)S(1)} %collective-permute-done.11.refs_0_), channel_id=1, source_target_pairs={{0,1},{1,0},{2,3},{3,2},{4,5},{5,4},{6,7},{7,6},{8,9},{9,8},{10,11... | collective-permute-start | bytes 1929224 | tf_op jit(solution)/shard_map/ppermute | solution.py:627
  36.9 27.5 %collective-permute-start.18 = (bf16[90,16,128]{2,1,0:T(8,128)(2,1)}, bf16[90,16,128]{2,1,0:T(8,128)(2,1)S(1)}, u32[]{:S(2)}, u32[]{:S(2)}) collective-permute-start(bf16[90,16,128]{2,1,0:T(8,128)(2,1)} %collective-permute-done.7.refs_2_), channel_id=1, source_target_pairs={{0,4},{4,0},{8,12},{12,8},{16,20},{20,16},{24,28},{28,24},{1,5},{5... | collective-permute-start | bytes 1105928 | tf_op jit(solution)/shard_map/ppermute | solution.py:627
  38.5 17.2 %collective-permute-start.14 = (bf16[157,16,128]{2,1,0:T(8,128)(2,1)S(1)}, bf16[157,16,128]{2,1,0:T(8,128)(2,1)S(1)}, u32[]{:S(2)}, u32[]{:S(2)}) collective-permute-start(bf16[157,16,128]{2,1,0:T(8,128)(2,1)S(1)} %collective-permute-done.12.refs_1_), channel_id=1, source_target_pairs={{0,1},{1,0},{2,3},{3,2},{4,5},{5,4},{6,7},{7,6},{8,9},{9,8},{10,11... | collective-permute-start | bytes 1929224 | tf_op jit(solution)/shard_map/ppermute | solution.py:627
  39.2 16.0 %collective-permute-start.9 = (bf16[90,16,128]{2,1,0:T(8,128)(2,1)S(1)}, bf16[90,16,128]{2,1,0:T(8,128)(2,1)S(1)}, u32[]{:S(2)}, u32[]{:S(2)}) collective-permute-start(bf16[90,16,128]{2,1,0:T(8,128)(2,1)S(1)} %collective-permute-done.8.refs_4_), channel_id=1, source_target_pairs={{0,8},{4,12},{8,16},{12,20},{16,24},{20,28},{24,0},{28,4},{1,9},{5... | collective-permute-start | bytes 1105928 | tf_op jit(solution)/shard_map/ppermute | solution.py:631
  53.6 11.5 %collective-permute-start.19 = (bf16[90,16,128]{2,1,0:T(8,128)(2,1)S(1)}, bf16[90,16,128]{2,1,0:T(8,128)(2,1)S(1)}, u32[]{:S(2)}, u32[]{:S(2)}) collective-permute-start(bf16[90,16,128]{2,1,0:T(8,128)(2,1)S(1)} %collective-permute-done.8.refs_4_), channel_id=1, source_target_pairs={{0,4},{4,0},{8,12},{12,8},{16,20},{20,16},{24,28},{28,24},{1,5},{5... | collective-permute-start | bytes 1105928 | tf_op jit(solution)/shard_map/ppermute | solution.py:627
  55.2 17.1 %collective-permute-start.10 = (bf16[90,16,128]{2,1,0:T(8,128)(2,1)S(1)}, bf16[90,16,128]{2,1,0:T(8,128)(2,1)S(1)}, u32[]{:S(2)}, u32[]{:S(2)}) collective-permute-start(bf16[90,16,128]{2,1,0:T(8,128)(2,1)S(1)} %collective-permute-done.9.refs_0_), channel_id=1, source_target_pairs={{0,4},{4,0},{8,12},{12,8},{16,20},{20,16},{24,28},{28,24},{1,5},{5... | collective-permute-start | bytes 1105928 | tf_op jit(solution)/shard_map/ppermute | solution.py:627
  72.3 11.5 %copy-start.6 = (f32[16,16]{1,0:T(8,128)S(1)}, f32[16,16]{1,0:T(8,128)}, u32[]{:S(2)}) copy-start(f32[16,16]{1,0:T(8,128)} %time_ref.1) | copy-start | bytes 3076
  76.0 2.0 %collective-permute-start.20 = (f32[72,128]{1,0:T(8,128)S(1)}, f32[72,128]{1,0:T(8,128)S(1)}, u32[]{:S(2)}, u32[]{:S(2)}) collective-permute-start(f32[72,128]{1,0:T(8,128)S(1)} %panel_last.1), channel_id=1, source_target_pairs={{0,1},{1,0},{2,3},{3,2},{4,5},{5,4},{6,7},{7,6},{8,9},{9,8},{10,11... | collective-permute-start | bytes 110600 | tf_op jit(solution)/shard_map/ppermute | solution.py:631
  76.1 4.0 %collective-permute-start.21 = (f32[72,128]{1,0:T(8,128)S(1)}, f32[72,128]{1,0:T(8,128)S(1)}, u32[]{:S(2)}, u32[]{:S(2)}) collective-permute-start(f32[72,128]{1,0:T(8,128)S(1)} %panel_last.1), channel_id=1, source_target_pairs={{0,2},{1,3},{2,0},{3,1},{4,6},{5,7},{6,4},{7,5},{8,10},{9,11},{10,... | collective-permute-start | bytes 110600 | tf_op jit(solution)/shard_map/ppermute | solution.py:631
  77.7 3.4 %collective-permute-start.22 = (f32[72,128]{1,0:T(8,128)S(1)}, f32[72,128]{1,0:T(8,128)S(1)}, u32[]{:S(2)}, u32[]{:S(2)}) collective-permute-start(f32[72,128]{1,0:T(8,128)S(1)} %panel_last.1), channel_id=1, source_target_pairs={{0,3},{1,2},{2,1},{3,0},{4,7},{5,6},{6,5},{7,4},{8,11},{9,10},{10,... | collective-permute-start | bytes 110600 | tf_op jit(solution)/shard_map/ppermute | solution.py:631

commit v2 on v1

--- a/solution.py
+++ b/solution.py
@@ -6,6 +6,7 @@
 from jax import lax
 from jax.experimental import pallas as pl
 from jax.experimental.pallas import tpu as pltpu
+from jax.experimental.layout import Layout, with_layout_constraint
 from jax.sharding import PartitionSpec as P
 
 
@@ -241,6 +242,12 @@
     copy.wait()
 
 
+def split(number, size):
+    if size & (size - 1):
+        return lax.div(number, size), lax.rem(number, size)
+    return lax.shift_right_logical(number, size.bit_length() - 1), lax.bitwise_and(number, size - 1)
+
+
 def expand(buf, bits, first, count, blocks, store, unrolled=False):
     lanes = buf.shape[2]
     batch = math.gcd(2, count)
@@ -248,8 +255,7 @@
     def some(i, _):
         tiles = []
         for j in range(batch):
-            base = (first + i * batch + j) * blocks
-            row, col = lax.div(base, lanes), lax.rem(base, lanes)
+            row, col = split(jnp.int32((first + i * batch + j) * blocks), lanes)
             tiles += [buf[bits[row, col + b]] for b in range(blocks)]
         for j in range(batch):
             for b in range(blocks):
@@ -296,69 +302,109 @@
         dst[aligned(dst_first + i * step, step), :] = (decay * (turned[at, 2:3] * s)).astype(BF16)
 
 
+def start_kernel(chunks, *refs):
+    msg = refs[:chunks]
+    dense, cov, info_ref, buf, bits_v, bits_s, turned, sem = refs[chunks:]
+    times, lanes = buf.shape[1:]
+    cells = cov.shape[1]
+    blocks = cells // lanes
+    rows = dense.shape[0] // times
+    copies = fetch(msg, buf, sem)
+    for copy in copies:
+        copy.wait()
+    read_info(buf, blocks, info_ref, turned)
+    read_head(buf, rows, blocks, bits_v)
+    copy = pltpu.make_async_copy(bits_v, bits_s, sem.at[chunks])
+    copy.start()
+    half = cells // 2
+    fine = math.gcd(4, rows // 2)
+
+    @pl.loop(0, fine)
+    def _(i):
+        fill_covariance(cov, i * (half // fine), i * (half // fine), half // fine, turned, info_ref)
+
+    copy.wait()
+
+    @pl.loop(0, fine)
+    def _(i):
+        first = half + i * (half // fine)
+        fill_covariance(cov, first, first, half // fine, turned, info_ref)
+        some = rows // fine
+        expand(buf, bits_s, i * some, some, blocks, into(dense, times, lanes, 0, i * some), unrolled=True)
+
+
+def start_call(own_msg, rows, cells):
+    times, lanes = own_msg[0].shape[1:]
+    slots = sum(chunk.shape[0] for chunk in own_msg)
+    chunks = len(own_msg)
+    return pl.pallas_call(
+        functools.partial(start_kernel, chunks),
+        out_shape=(
+            shape_of((rows * times, cells), BF16),
+            shape_of((cells, cells), BF16),
+            shape_of((INFO, cells), F32),
+        ),
+        in_specs=[ANY] * chunks,
+        out_specs=(VMEM,) * 3,
+        scratch_shapes=[
+            pltpu.VMEM((slots, times, lanes), BF16),
+            pltpu.VMEM((8, lanes), I32),
+            pltpu.SMEM((8, lanes), I32),
+            pltpu.VMEM((cells, INFO), F32),
+            pltpu.SemaphoreType.DMA((chunks + 1,)),
+        ],
+        compiler_params=params(12),
+        cost_estimate=cost(4),
+        name="own_start",
+    )(*own_msg)
+
+
 def own_kernel(chunks, *refs):
-    msgs = refs[:chunks], refs[chunks : 2 * chunks]
-    out_ref, mate_dense, next_ref, info_ref = refs[2 * chunks : 2 * chunks + 4]
-    bufs, bits_v, bits_s, dense, cov, turned, sem = refs[2 * chunks + 4 :]
-    times, lanes = bufs.shape[2:]
+    msg = refs[:chunks]
+    dense, cov, info_ref, out_ref, mate_dense, next_ref, buf, bits_v, bits_s, turned, sem = refs[chunks:]
+    times, lanes = buf.shape[1:]
     cells = cov.shape[1]
     blocks = cells // lanes
     rows = dense.shape[0] // times
     tall = min(256, rows * times)
     steps = rows * times // tall
     part = cells // steps
-    copies = [fetch(msg, bufs.at[k], sem.at[k]) for k, msg in enumerate(msgs)]
-    for k in range(2):
-        for copy in copies[k]:
-            copy.wait()
-        read_info(bufs.at[k], blocks, None if k else info_ref, turned.at[k])
-        read_head(bufs.at[k], rows, blocks, bits_v.at[k])
-    copy_in(bits_v, bits_s, sem.at[2, 0])
-    fine = math.gcd(8, rows // 2)
-    piece = cells // fine
-
-    @pl.loop(0, fine)
-    def _(i):
-        fill_covariance(cov, i * piece, i * piece, piece, turned.at[0], info_ref)
-        some = rows // fine
-        expand(bufs.at[0], bits_s.at[0], i * some, some, blocks, into(dense, times, lanes, 0, i * some), unrolled=True)
+    for copy in fetch(msg, buf, sem):
+        copy.wait()
+    read_info(buf, blocks, None, turned)
+    read_head(buf, rows, blocks, bits_v)
+    copy_in(bits_v, bits_s, sem.at[chunks])
 
     @pl.loop(0, steps)
     def _(u):
         here = aligned(u * tall, tall)
-        fill_covariance(next_ref, u * part, u * part, part, turned.at[1], info_ref)
+        fill_covariance(next_ref, u * part, u * part, part, turned, info_ref)
         out_ref[here, :] = jnp.dot(dense[here, :], cov[...], preferred_element_type=F32)
         some = rows // steps
-        expand(bufs.at[1], bits_s.at[1], u * some, some, blocks, into(mate_dense, times, lanes, 0, u * some), unrolled=True)
-
-
-def own_call(own_msg, mate_msg, rows, cells):
-    times, lanes = own_msg[0].shape[1:]
-    slots = sum(chunk.shape[0] for chunk in own_msg)
-    chunks = len(own_msg)
+        expand(buf, bits_s, u * some, some, blocks, into(mate_dense, times, lanes, 0, u * some), unrolled=True)
+
+
+def own_call(mate_msg, dense, cov, info):
+    times, lanes = mate_msg[0].shape[1:]
+    cells = cov.shape[1]
+    slots = sum(chunk.shape[0] for chunk in mate_msg)
+    chunks = len(mate_msg)
     return pl.pallas_call(
         functools.partial(own_kernel, chunks),
-        out_shape=(
-            shape_of((rows * times, cells), F32),
-            shape_of((rows * times, cells), BF16),
-            shape_of((cells, cells), BF16),
-            shape_of((INFO, cells), F32),
-        ),
-        in_specs=[ANY] * (2 * chunks),
-        out_specs=(VMEM,) * 4,
+        out_shape=(shape_of(dense.shape, F32), shape_of(dense.shape, BF16), shape_of((cells, cells), BF16)),
+        in_specs=[ANY] * chunks + [VMEM] * 3,
+        out_specs=(VMEM,) * 3,
         scratch_shapes=[
-            pltpu.VMEM((2, slots, times, lanes), BF16),
-            pltpu.VMEM((2, 8, lanes), I32),
-            pltpu.SMEM((2, 8, lanes), I32),
-            pltpu.VMEM((rows * times, cells), BF16),
-            pltpu.VMEM((cells, cells), BF16),
-            pltpu.VMEM((2, cells, INFO), F32),
-            pltpu.SemaphoreType.DMA((3, chunks)),
+            pltpu.VMEM((slots, times, lanes), BF16),
+            pltpu.VMEM((8, lanes), I32),
+            pltpu.SMEM((8, lanes), I32),
+            pltpu.VMEM((cells, INFO), F32),
+            pltpu.SemaphoreType.DMA((chunks + 1,)),
         ],
         compiler_params=params(16),
-        cost_estimate=cost(9),
+        cost_estimate=cost(6),
         name="own_product",
-    )(*own_msg, *mate_msg)
+    )(*mate_msg, dense, cov, info)
 
 
 def mate_kernel(count, *refs):
@@ -426,11 +472,12 @@
         start_ref, done_ref, out_ref, turned_ref = refs[3:7]
     else:
         out_ref, next_ref = refs[3:5]
-    bufs, bits_v, bits_s, dense, sem = refs[-5:]
+    bufs, bits_v, bits_s, dense_a, dense_b, sem = refs[-6:]
     times, lanes = bufs.shape[2:]
     cells = near_ref.shape[1]
     blocks = cells // lanes
     rows = out_ref.shape[0]
+    few = count // 2
     deep = -(-rows * blocks // lanes)
     copies = [fetch(msgs[k], bufs.at[k], sem.at[k]) for k in range(count)]
     for k in range(count):
@@ -440,11 +487,17 @@
     copy = pltpu.make_async_copy(bits_v, bits_s, sem.at[count, 0])
     copy.start()
 
+    def place(u, begin, end, dense):
+        for k in range(begin, end):
+            store = into(dense, times, lanes, (k - begin) * cells)
+            expand(bufs.at[k], bits_s.at[k], u * unit, unit, blocks, store, unrolled=count <= 4)
+
     def step(u, _):
-        for k in range(count):
-            expand(bufs.at[k], bits_s.at[k], u * unit, unit, blocks, into(dense, times, lanes, k * cells))
         here = aligned(u * unit * times, unit * times)
-        value = near_ref[here, :] + jnp.dot(dense[...], cov_ref[...], preferred_element_type=F32)
+        place(u, few, count, dense_b)
+        value = near_ref[here, :] + jnp.dot(dense_a[...], cov_ref[: few * cells, :], preferred_element_type=F32)
+        place(jnp.minimum(u + 1, rows // unit - 1), 0, few, dense_a)
+        value = value + jnp.dot(dense_b[...], cov_ref[few * cells :, :], preferred_element_type=F32)
         mixed = mixed_unit(mix_ref, value)
         at = aligned(u * unit, unit)
         out_ref[at] = mixed.reshape(unit, times, cells)
@@ -463,6 +516,7 @@
         first = start_ref[0]
         lax.fori_loop(0, first, carry_over, 0)
         copy.wait()
+        place(jnp.minimum(first, rows // unit - 1), 0, few, dense_a)
         lax.fori_loop(first, rows // unit, step, 0)
     else:
         copy.wait()
@@ -474,6 +528,7 @@
                 whole = whole * (bits_s[k, deep, (u + 1) * unit - 1] <= limit).astype(I32)
             ready = ready + whole
         next_ref[0] = ready
+        place(jnp.int32(0), 0, few, dense_a)
         lax.fori_loop(0, ready, step, 0)
 
 
@@ -493,7 +548,8 @@
             pltpu.VMEM((count, slots, times, lanes), BF16),
             pltpu.VMEM((count, 8, lanes), I32),
             pltpu.SMEM((count, 8, lanes), I32),
-            pltpu.VMEM((unit * times, count * cells), BF16),
+            pltpu.VMEM((unit * times, count // 2 * cells), BF16),
+            pltpu.VMEM((unit * times, (count - count // 2) * cells), BF16),
             pltpu.SemaphoreType.DMA((count + 1, chunks)),
         ],
         compiler_params=params(16),
@@ -538,7 +594,7 @@
     msgs = refs[:pieces]
     refs = refs[pieces:]
     if final:
-        sources_ref, turned, before_ref, over_ref, out_ref = refs[:5]
+        group_ref, turned, before_ref, over_ref, out_ref = refs[:5]
     else:
         turned, out_ref, over_ref = refs[:3]
     bufs, bits_v, bits_s, panel, sem = refs[-5:]
@@ -579,9 +635,13 @@
     value = jnp.concatenate([before_ref[...], total], axis=1)
     size = value.shape[1]
     row = lax.broadcasted_iota(I32, (size, size), 0)
+    half = size // each // 2
+    hi, lo = split(group_ref[0], 2)
     target = row
     for k in range(size // each):
-        target = jnp.where(row // each == k, sources_ref[k] * each + row % each, target)
+        back = hi - k // 2
+        source = jnp.where(back < 0, back + half, back) * 2 + lax.bitwise_xor(lo, k % 2)
+        target = jnp.where((row >= k * each) & (row < (k + 1) * each), row + (source - k) * each, target)
     select = (lax.broadcasted_iota(I32, (size, size), 1) == target).astype(F32).astype(BF16)
     total = jnp.zeros(value.shape, F32)
     for _ in range(3):
@@ -598,8 +658,8 @@
     pieces = len(msgs)
     width = pieces * each
     if final:
-        sources, before, over = final
-        operands, in_specs = (sources, turned, before, over), [SMEM, VMEM, VMEM, SMEM]
+        group, before, over = final
+        operands, in_specs = (group[None], turned, before, over), [SMEM, VMEM, VMEM, SMEM]
         out_shape = shape_of((rows + 8, before.shape[1] + width), F32)
         out_specs = VMEM
     else:
@@ -631,6 +691,10 @@
     return lax.ppermute(value, axis, [(i, ((i + 2 * shift) % count) ^ flip) for i in range(count)])
 
 
+def row_major(value):
+    return with_layout_constraint(value, Layout(tuple(range(value.ndim))))
+
+
 def add_cells(part, cells):
     total = part
     for shift in range(cells // 2):
@@ -686,8 +750,6 @@
     slots = slot_count(obs_rows * blocks, 1 + blocks)
     chunks = (slots - slots // 2, slots // 2)
     mask = block_mask.T
-    order = jnp.arange(observers, dtype=I32)
-    sources = (group // 2 - order // 2) % half * 2 + (group % 2 ^ (order % 2))
 
     room = slots - 2 - blocks - 1
     own_panel = pack_panel(mask, panel_index, group, footprint, each, slot_count(each * blocks, 1), room)
@@ -705,34 +767,36 @@
     for shift in range(1, cells // 2):
         far_msgs.append([partner(c, "cell", cells) for c in far_msgs[shift - 1]])
 
-    near, mate_dense, mate_cov, info = own_call(own_msg, mate_msg, obs_rows, cell_local)
+    dense, own_cov, info = start_call(own_msg, obs_rows, cell_local)
+    near, mate_dense, mate_cov = own_call(mate_msg, dense, own_cov, info)
     near, far_cov = mate_call([msg[0] for msg in far_msgs], near, mate_dense, mate_cov, info)
     mix = mixing(time_cov, unit)
     first_cov, start = some_rows([msg[:1] for msg in far_msgs], far_cov, near, mix, obs_rows, unit, slots)
     cov_product, turned = some_rows(far_msgs, far_cov, near, mix, obs_rows, unit, slots, (start, first_cov))
     cut = len(messages) * 3 // 4
     before, over = panel_part(messages[:cut], turned, each)
-    part = panel_part(messages[cut:], turned, each, (sources, before, over))
-
-    def innovation_of(total):
+    part = panel_part(messages[cut:], turned, each, (group, before, over))
+
+    def innovation_of(total, group):
         positions = jnp.arange(obs_rows, dtype=I32)
         on_diagonal = ((group * obs_rows + positions)[:, None] == panel_index[None, :]).astype(F32)
         return total + error_var[:, None] * on_diagonal
 
+    part, late_group, late_mask = lax.optimization_barrier((part, group, mask))
     total = add_cells(part, cells)
 
     def again(carry):
         wanted = carry[0]
-        mask, cell_info, place, from_group = (
-            jnp.where(wanted, value, 0) for value in (block_mask, info, group, sources)
-        )
+        kept, cell_info, place = (jnp.where(wanted, value, 0) for value in (late_mask, info, late_group))
+        order = jnp.arange(observers, dtype=I32)
+        from_group = (place // 2 - order // 2) % half * 2 + (place % 2 ^ (order % 2))
         mine = lax.dynamic_slice_in_dim(panel_index, place * each, each) - place * obs_rows
         cov_product, total = dense_way(
-            cells, observers, footprint, mask, cell_info, time_cov, mine, from_group
+            cells, observers, footprint, kept.T, cell_info, time_cov, mine, from_group
         )
-        return jnp.bool_(False), cov_product, innovation_of(total)
-
-    carry = (total[obs_rows, 0] > 0, cov_product, innovation_of(total[:obs_rows]))
+        return jnp.bool_(False), cov_product, row_major(innovation_of(total, place))
+
+    carry = (total[obs_rows, 0] > 0, cov_product, row_major(innovation_of(total[:obs_rows], late_group)))
     return lax.while_loop(lambda carry: carry[0], again, carry)[1:]
 
 

time: 86.1 us -> 86.6 us (level)
  waiting for transfers between devices: 18.1 us -> 21.9 us
  Pallas kernels: 47.2 us -> 44.5 us
  local copies, waits for them, and re-layouts: 5 us -> 2.65 us
  starting transfers between devices: 12.8 us -> 14 us
    pallas_call x0 -> x1, Pallas kernels: none -> 4.59 us  [start_call(): pl.pallas_call(functools.partial(start_kernel, chunks), out_shape=(shape_...]
    pallas_call x1, Pallas kernels: 9.39 us -> 5.52 us  [own_call(): pl.pallas_call(functools.partial(own_kernel, chunks), out_shape=(shape_of...]
    ppermute x8, waiting for transfers between devices: 15.3 us -> 18.6 us  [shifted(): lax.ppermute(value, axis, [(i, (i + 2 * shift) % count ^ flip) for i in r...]
    unnamed x17 -> x14, local copies, waits for them, and re-layouts: 4.42 us -> 2.08 us
    pallas_call x2, Pallas kernels: 15.2 us -> 12.9 us  [some_rows(): pl.pallas_call(functools.partial(rows_kernel, count, chunks, unit, late),...]
  transfers between devices with their start and end apart: 16 -> 16, of which waited for: 7 -> 6; matrix products, arithmetic and copies ran while one was open for 0% -> 0% of each run, Pallas kernels for 46% -> 43%
where the time goes in v2:
time: 86.6 us; the launch traced here: 86.1 us
  Pallas kernels  44.5 us (51%)
  waiting for transfers between devices  21.9 us (25%)
  starting transfers between devices  14 us (16%)
  local copies, waits for them, and re-layouts  2.65 us (3%)
  between operations  1.53 us (2%)
  other arithmetic  1.37 us (2%)
    ppermute x8, waiting for transfers between devices, shifted(): lax.ppermute(value, axis, [(i, (i + 2 * shift) % count ^ flip) for i in r...  18.6 us
    pallas_call x2, Pallas kernels, some_rows(): pl.pallas_call(functools.partial(rows_kernel, count, chunks, unit, late),...  12.9 us
    ppermute x8, starting transfers between devices, shifted(): lax.ppermute(value, axis, [(i, (i + 2 * shift) % count ^ flip) for i in r...  8.69 us
    pallas_call x2, Pallas kernels, panel_part(): pl.pallas_call(functools.partial(panel_kernel, pieces, each, bool(final))...  8.07 us
    pallas_call x1, Pallas kernels, mate_call(): pl.pallas_call(functools.partial(mate_kernel, count), out_shape=(shape_of...  6.7 us
    pallas_call x1, Pallas kernels, own_call(): pl.pallas_call(functools.partial(own_kernel, chunks), out_shape=(shape_of...  5.52 us
    ppermute x8, starting transfers between devices, partner(): return lax.ppermute(value, axis, [(i, i ^ 1) for i in range(count)])  5.29 us
    pallas_call x1, Pallas kernels, start_call(): pl.pallas_call(functools.partial(start_kernel, chunks), out_shape=(shape_...  4.59 us
  transfers between devices with their start and end apart: 16, of which 6 were waited for; matrix products, arithmetic and copies ran while one was open for 0% of the time, Pallas kernels for 43%

profile of v2, /device:TPU:0, one launch (start us, length us, event | category | flops | bytes accessed | tf_op | source)
XLA Modules:
  0.0 86.1 jit_solution(678375256476154033)
XLA Ops:
  1.3 0.7 copy-done.2
  2.0 0.7 copy-done.3
  2.7 4.2 %pack_feet.1 = (bf16[157,16,128]{2,1,0:T(8,128)(2,1)}, bf16[157,16,128]{2,1,0:T(8,128)(2,1)S(1)}) custom-call(s32[8,64]{1,0:T(8,128)S(1)} %bitcast.74, s32[2,1024]{1,0:T(2,128)S(1)} %copy-done.2, f32[1,1024]{1,0:T(1,128)S(1)} %bitcast.78, bf16[64,16,1024]{2,1,0:T(8,128)(2,1)} %feet_ref.3), custom_call_target="tpu_custom_call" | custom-call | flops 2700000000 | bytes 1000000 | tf_op jit(solution)/shard_map/pack_feet/pallas_call | solution.py:151
  6.9 3.0 %collective-permute-start.11 = (bf16[157,16,128]{2,1,0:T(8,128)(2,1)}, bf16[157,16,128]{2,1,0:T(8,128)(2,1)S(1)}, u32[]{:S(2)}, u32[]{:S(2)}) collective-permute-start(bf16[157,16,128]{2,1,0:T(8,128)(2,1)} %get-tuple-element.121.refs_0_), channel_id=1, source_target_pairs={{0,2},{1,3},{2,0},{3,1},{4,6},{5,7},{6,4},{7,5},{8,10},{9,11},{10,... | collective-permute-start | bytes 1929224 | tf_op jit(solution)/shard_map/ppermute | solution.py:691
  10.5 2.2 %pack_panel.1.refs_0_ = bf16[90,16,128]{2,1,0:T(8,128)(2,1)S(1)} custom-call(s32[8,64]{1,0:T(8,128)S(1)} %bitcast.75, s32[8,64]{1,0:T(8,128)S(1)} %bitcast.76, s32[128]{0:T(128)S(1)} %copy-done.7, s32[1]{0:T(128)} %bitcast.12.group_ref.refs_2_, bf16[64,16,1024]{2,1,0:T(8,128)(2,1)} %feet_ref.3), custom_call_target="tpu_custom_call" | custom-call | flops 1800000000 | bytes 1000000 | tf_op jit(solution)/shard_map/pack_panel/pallas_call | solution.py:200
  12.8 2.1 %collective-permute-start.7 = (bf16[90,16,128]{2,1,0:T(8,128)(2,1)S(1)}, bf16[90,16,128]{2,1,0:T(8,128)(2,1)S(1)}, u32[]{:S(2)}, u32[]{:S(2)}) collective-permute-start(bf16[90,16,128]{2,1,0:T(8,128)(2,1)S(1)} %pack_panel.1.refs_0_), channel_id=1, source_target_pairs={{0,8},{4,12},{8,16},{12,20},{16,24},{20,28},{24,0},{28,4},{1,9},{5... | collective-permute-start | bytes 1105928 | tf_op jit(solution)/shard_map/ppermute | solution.py:691
  14.9 10.6 %collective-permute-done.11.refs_0_ = bf16[157,16,128]{2,1,0:T(8,128)(2,1)S(1)} collective-permute-done((bf16[157,16,128]{2,1,0:T(8,128)(2,1)}, bf16[157,16,128]{2,1,0:T(8,128)(2,1)S(1)}, u32[]{:S(2)}, u32[]{:S(2)}) %collective-permute-start.11) | collective-permute-done | bytes 643104 | tf_op jit(solution)/shard_map/ppermute | solution.py:691
  25.5 4.6 %own_start.1 = (bf16[1024,1024]{1,0:T(8,128)(2,1)S(1)}, bf16[1024,1024]{1,0:T(8,128)(2,1)S(1)}, f32[8,1024]{1,0:T(8,128)S(1)}) custom-call(bf16[157,16,128]{2,1,0:T(8,128)(2,1)} %get-tuple-element.121.refs_0_, bf16[157,16,128]{2,1,0:T(8,128)(2,1)S(1)} %get-tuple-element.122.refs_1_), custom_call_target="tpu_custom_call" | custom-call | flops 3600000000 | bytes 1000000 | tf_op jit(solution)/shard_map/own_start/pallas_call | solution.py:340
  30.4 2.1 %collective-permute-start.17 = (bf16[90,16,128]{2,1,0:T(8,128)(2,1)S(1)}, bf16[90,16,128]{2,1,0:T(8,128)(2,1)S(1)}, u32[]{:S(2)}, u32[]{:S(2)}) collective-permute-start(bf16[90,16,128]{2,1,0:T(8,128)(2,1)S(1)} %pack_panel.1.refs_0_), channel_id=1, source_target_pairs={{0,4},{4,0},{8,12},{12,8},{16,20},{20,16},{24,28},{28,24},{1,5},{5... | collective-permute-start | bytes 1105928 | tf_op jit(solution)/shard_map/ppermute | solution.py:687
  32.5 1.6 %collective-permute-start.8 = (bf16[90,16,128]{2,1,0:T(8,128)(2,1)S(1)}, bf16[90,16,128]{2,1,0:T(8,128)(2,1)S(1)}, u32[]{:S(2)}, u32[]{:S(2)}) collective-permute-start(bf16[90,16,128]{2,1,0:T(8,128)(2,1)S(1)} %collective-permute-done.7.refs_2_), channel_id=1, source_target_pairs={{0,8},{4,12},{8,16},{12,20},{16,24},{20,28},{24,0},{28,4},{1,9},{5... | collective-permute-start | bytes 1105928 | tf_op jit(solution)/shard_map/ppermute | solution.py:691
  34.1 5.5 %own_product.1 = (f32[1024,1024]{1,0:T(8,128)S(1)}, bf16[1024,1024]{1,0:T(8,128)(2,1)S(1)}, bf16[1024,1024]{1,0:T(8,128)(2,1)S(1)}) custom-call(bf16[157,16,128]{2,1,0:T(8,128)(2,1)S(1)} %collective-permute-done.15.refs_0_, bf16[157,16,128]{2,1,0:T(8,128)(2,1)S(1)} %collective-permute-done.16.refs_1_, bf16[1024,1024]{1,0:T(8,128)(2,1)S(1)} %get-tuple-element.123.refs_2_, ...), custom_call_target="tpu_custom_call" | custom-call | flops 5400000000 | bytes 1000000 | tf_op jit(solution)/shard_map/own_product/pallas_call | solution.py:392
  40.2 4.9 %collective-permute-done.8.refs_4_ = bf16[90,16,128]{2,1,0:T(8,128)(2,1)S(1)} collective-permute-done((bf16[90,16,128]{2,1,0:T(8,128)(2,1)S(1)}, bf16[90,16,128]{2,1,0:T(8,128)(2,1)S(1)}, u32[]{:S(2)}, u32[]{:S(2)}) %collective-permute-start.8) | collective-permute-done | bytes 368672 | tf_op jit(solution)/shard_map/ppermute | solution.py:691
  45.1 6.7 %mate_product.1 = (f32[1024,1024]{1,0:T(8,128)S(1)}, bf16[2048,1024]{1,0:T(8,128)(2,1)S(1)}) custom-call(bf16[157,16,128]{2,1,0:T(8,128)(2,1)S(1)} %collective-permute-done.11.refs_0_, bf16[157,16,128]{2,1,0:T(8,128)(2,1)S(1)} %collective-permute-done.13.refs_1_.refs_2_, ...), custom_call_target="tpu_custom_call", output_to_operand_aliasing={{0}: (2, {})} | custom-call | flops 7200000000 | bytes 1000000 | tf_op jit(solution)/shard_map/mate_product/pallas_call | solution.py:439
  51.8 5.4 %first_rows.1 = (bf16[64,16,1024]{2,1,0:T(8,128)(2,1)S(1)}, s32[1]{0:T(128)}) custom-call(bf16[157,16,128]{2,1,0:T(8,128)(2,1)S(1)} %collective-permute-done.11.refs_0_, bf16[157,16,128]{2,1,0:T(8,128)(2,1)S(1)} %collective-permute-done.13.refs_1_.refs_2_, bf16[2048,1024]{1,0:T(8,128)(2,1)S(1)} %get-tuple-element.129.refs_2_.refs_4_, ...), custom_call_target="tpu_custom_call" | custom-call | flops 5400000000 | bytes 1000000 | tf_op jit(solution)/shard_map/first_rows/pallas_call | solution.py:542
  57.7 1.6 %collective-permute-start.10 = (bf16[90,16,128]{2,1,0:T(8,128)(2,1)S(1)}, bf16[90,16,128]{2,1,0:T(8,128)(2,1)S(1)}, u32[]{:S(2)}, u32[]{:S(2)}) collective-permute-start(bf16[90,16,128]{2,1,0:T(8,128)(2,1)S(1)} %collective-permute-done.9.refs_0_), channel_id=1, source_target_pairs={{0,4},{4,0},{8,12},{12,8},{16,20},{20,16},{24,28},{28,24},{1,5},{5... | collective-permute-start | bytes 1105928 | tf_op jit(solution)/shard_map/ppermute | solution.py:687
  59.3 7.5 %late_rows.1 = (bf16[64,16,1024]{2,1,0:T(8,128)(2,1)}, bf16[16,64,1024]{2,1,0:T(8,128)(2,1)S(1)}) custom-call(bf16[157,16,128]{2,1,0:T(8,128)(2,1)S(1)} %collective-permute-done.11.refs_0_, bf16[157,16,128]{2,1,0:T(8,128)(2,1)S(1)} %collective-permute-done.12.refs_1_, bf16[157,16,128]{2,1,0:T(8,128)(2,1)S(1)} %collective-permute-done.13.refs_1_.refs_2_, ...), custom_call_target="tpu_custom_call" | custom-call | flops 5400000000 | bytes 1000000 | tf_op jit(solution)/shard_map/late_rows/pallas_call | solution.py:542
  66.9 1.9 %collective-permute-done.19.refs_5_ = bf16[90,16,128]{2,1,0:T(8,128)(2,1)S(1)} collective-permute-done((bf16[90,16,128]{2,1,0:T(8,128)(2,1)S(1)}, bf16[90,16,128]{2,1,0:T(8,128)(2,1)S(1)}, u32[]{:S(2)}, u32[]{:S(2)}) %collective-permute-start.19) | collective-permute-done | bytes 368672 | tf_op jit(solution)/shard_map/ppermute | solution.py:687
  68.7 4.9 %panel_first.1 = (f32[64,96]{1,0:T(8,128)S(1)}, s32[1]{0:T(128)}) custom-call(bf16[90,16,128]{2,1,0:T(8,128)(2,1)S(1)} %pack_panel.1.refs_0_, bf16[90,16,128]{2,1,0:T(8,128)(2,1)S(1)} %collective-permute-done.17.refs_1_, bf16[90,16,128]{2,1,0:T(8,128)(2,1)S(1)} %collective-permute-done.7.refs_2_, bf16[90,16,128]{2,1,0:T(8,128)(2,1)S(1)} %collective-permute-done.18.refs_3_, ...), custom_call_target="tpu_custom_call" | custom-call | flops 4499999744 | bytes 1000000 | tf_op jit(solution)/shard_map/panel_first/pallas_call | solution.py:668
  73.6 1.4 %collective-permute-done.10.refs_1_ = bf16[90,16,128]{2,1,0:T(8,128)(2,1)S(1)} collective-permute-done((bf16[90,16,128]{2,1,0:T(8,128)(2,1)S(1)}, bf16[90,16,128]{2,1,0:T(8,128)(2,1)S(1)}, u32[]{:S(2)}, u32[]{:S(2)}) %collective-permute-start.10) | collective-permute-done | bytes 368672 | tf_op jit(solution)/shard_map/ppermute | solution.py:687
  75.0 3.2 %panel_last.1 = f32[72,128]{1,0:T(8,128)S(1)} custom-call(bf16[90,16,128]{2,1,0:T(8,128)(2,1)S(1)} %collective-permute-done.9.refs_0_, bf16[90,16,128]{2,1,0:T(8,128)(2,1)S(1)} %collective-permute-done.10.refs_1_, s32[1]{0:T(128)} %bitcast.12.group_ref.refs_2_, bf16[16,64,1024]{2,1,0:T(8,128)(2,1)S(1)} %get-tuple-element.133.refs_6_.refs_3_, ...), custom_call_target="tpu_custom_call" | custom-call | flops 2700000000 | bytes 1000000 | tf_op jit(solution)/shard_map/panel_last/pallas_call | solution.py:668
  78.3 1.6 %collective-permute-start.21 = (f32[72,128]{1,0:T(8,128)S(1)}, f32[72,128]{1,0:T(8,128)S(1)}, u32[]{:S(2)}, u32[]{:S(2)}) collective-permute-start(f32[72,128]{1,0:T(8,128)S(1)} %panel_last.1), channel_id=1, source_target_pairs={{0,2},{1,3},{2,0},{3,1},{4,6},{5,7},{6,4},{7,5},{8,10},{9,11},{10,... | collective-permute-start | bytes 110600 | tf_op jit(solution)/shard_map/ppermute | solution.py:691
  80.2 2.1 %collective-permute-done.21 = f32[72,128]{1,0:T(8,128)S(1)} collective-permute-done((f32[72,128]{1,0:T(8,128)S(1)}, f32[72,128]{1,0:T(8,128)S(1)}, u32[]{:S(2)}, u32[]{:S(2)}) %collective-permute-start.21) | collective-permute-done | bytes 36896 | tf_op jit(solution)/shard_map/ppermute | solution.py:691
  82.3 1.0 %collective-permute-done.22 = f32[72,128]{1,0:T(8,128)S(1)} collective-permute-done((f32[72,128]{1,0:T(8,128)S(1)}, f32[72,128]{1,0:T(8,128)S(1)}, u32[]{:S(2)}, u32[]{:S(2)}) %collective-permute-start.22) | collective-permute-done | bytes 36896 | tf_op jit(solution)/shard_map/ppermute | solution.py:691
  83.8 1.4 %slice_add_fusion = f32[64,128]{1,0:T(8,128)} fusion(f32[72,128]{1,0:T(8,128)S(1)} %add_add_fusion, f32[64]{0:T(128)} %param.18, s32[128]{0:T(128)S(1)} %copy-done.7, s32[64]{0:T(128)S(1)} %iota_add_fusion.1), kind=kLoop, calls=%fused_computation.46 | loop fusion | flops 24576 | bytes 66560 | tf_op jit(solution)/shard_map/add | solution.py:783
  (38 shorter events, 3.9 us)
Async XLA Ops:
  0.6 0.7 copy-start
  1.3 0.7 copy-start.2
  2.0 0.7 copy-start.3
  2.7 7.8 %copy-start.1 = (s32[64,8]{0,1:T(8,128)S(1)}, s32[64,8]{0,1:T(8,128)}, u32[]{:S(2)}) copy-start(s32[64,8]{0,1:T(8,128)} %param.14) | copy-start | bytes 6148
  2.7 7.8 %copy-start.7 = (s32[128]{0:T(128)S(1)}, s32[128]{0:T(128)}, u32[]{:S(2)}) copy-start(s32[128]{0:T(128)} %index_ref.1) | copy-start | bytes 1540
  6.9 18.6 %collective-permute-start.11 = (bf16[157,16,128]{2,1,0:T(8,128)(2,1)}, bf16[157,16,128]{2,1,0:T(8,128)(2,1)S(1)}, u32[]{:S(2)}, u32[]{:S(2)}) collective-permute-start(bf16[157,16,128]{2,1,0:T(8,128)(2,1)} %get-tuple-element.121.refs_0_), channel_id=1, source_target_pairs={{0,2},{1,3},{2,0},{3,1},{4,6},{5,7},{6,4},{7,5},{8,10},{9,11},{10,... | collective-permute-start | bytes 1929224 | tf_op jit(solution)/shard_map/ppermute | solution.py:691
  9.9 22.6 %collective-permute-start.15 = (bf16[157,16,128]{2,1,0:T(8,128)(2,1)}, bf16[157,16,128]{2,1,0:T(8,128)(2,1)S(1)}, u32[]{:S(2)}, u32[]{:S(2)}) collective-permute-start(bf16[157,16,128]{2,1,0:T(8,128)(2,1)} %get-tuple-element.121.refs_0_), channel_id=1, source_target_pairs={{0,1},{1,0},{2,3},{3,2},{4,5},{5,4},{6,7},{7,6},{8,9},{9,8},{10,11... | collective-permute-start | bytes 1929224 | tf_op jit(solution)/shard_map/ppermute | solution.py:687
  9.9 24.2 %collective-permute-start.16 = (bf16[157,16,128]{2,1,0:T(8,128)(2,1)S(1)}, bf16[157,16,128]{2,1,0:T(8,128)(2,1)S(1)}, u32[]{:S(2)}, u32[]{:S(2)}) collective-permute-start(bf16[157,16,128]{2,1,0:T(8,128)(2,1)S(1)} %get-tuple-element.122.refs_1_), channel_id=1, source_target_pairs={{0,1},{1,0},{2,3},{3,2},{4,5},{5,4},{6,7},{7,6},{8,9},{9,8},{10,11... | collective-permute-start | bytes 1929224 | tf_op jit(solution)/shard_map/ppermute | solution.py:687
  10.5 29.8 %collective-permute-start.12 = (bf16[157,16,128]{2,1,0:T(8,128)(2,1)S(1)}, bf16[157,16,128]{2,1,0:T(8,128)(2,1)S(1)}, u32[]{:S(2)}, u32[]{:S(2)}) collective-permute-start(bf16[157,16,128]{2,1,0:T(8,128)(2,1)S(1)} %get-tuple-element.122.refs_1_), channel_id=1, source_target_pairs={{0,2},{1,3},{2,0},{3,1},{4,6},{5,7},{6,4},{7,5},{8,10},{9,11},{10,... | collective-permute-start | bytes 1929224 | tf_op jit(solution)/shard_map/ppermute | solution.py:691
  12.8 17.3 %copy-start.5 = (f32[16,16]{1,0:T(8,128)S(1)}, f32[16,16]{1,0:T(8,128)}, u32[]{:S(2)}) copy-start(f32[16,16]{1,0:T(8,128)} %time_ref.1) | copy-start | bytes 3076
  12.8 17.6 %collective-permute-start.7 = (bf16[90,16,128]{2,1,0:T(8,128)(2,1)S(1)}, bf16[90,16,128]{2,1,0:T(8,128)(2,1)S(1)}, u32[]{:S(2)}, u32[]{:S(2)}) collective-permute-start(bf16[90,16,128]{2,1,0:T(8,128)(2,1)S(1)} %pack_panel.1.refs_0_), channel_id=1, source_target_pairs={{0,8},{4,12},{8,16},{12,20},{16,24},{20,28},{24,0},{28,4},{1,9},{5... | collective-permute-start | bytes 1105928 | tf_op jit(solution)/shard_map/ppermute | solution.py:691
  25.5 19.6 %collective-permute-start.13 = (bf16[157,16,128]{2,1,0:T(8,128)(2,1)S(1)}, bf16[157,16,128]{2,1,0:T(8,128)(2,1)S(1)}, u32[]{:S(2)}, u32[]{:S(2)}) collective-permute-start(bf16[157,16,128]{2,1,0:T(8,128)(2,1)S(1)} %collective-permute-done.11.refs_0_), channel_id=1, source_target_pairs={{0,1},{1,0},{2,3},{3,2},{4,5},{5,4},{6,7},{7,6},{8,9},{9,8},{10,11... | collective-permute-start | bytes 1929224 | tf_op jit(solution)/shard_map/ppermute | solution.py:687
  30.4 36.4 %collective-permute-start.17 = (bf16[90,16,128]{2,1,0:T(8,128)(2,1)S(1)}, bf16[90,16,128]{2,1,0:T(8,128)(2,1)S(1)}, u32[]{:S(2)}, u32[]{:S(2)}) collective-permute-start(bf16[90,16,128]{2,1,0:T(8,128)(2,1)S(1)} %pack_panel.1.refs_0_), channel_id=1, source_target_pairs={{0,4},{4,0},{8,12},{12,8},{16,20},{20,16},{24,28},{28,24},{1,5},{5... | collective-permute-start | bytes 1105928 | tf_op jit(solution)/shard_map/ppermute | solution.py:687
  32.5 12.6 %collective-permute-start.8 = (bf16[90,16,128]{2,1,0:T(8,128)(2,1)S(1)}, bf16[90,16,128]{2,1,0:T(8,128)(2,1)S(1)}, u32[]{:S(2)}, u32[]{:S(2)}) collective-permute-start(bf16[90,16,128]{2,1,0:T(8,128)(2,1)S(1)} %collective-permute-done.7.refs_2_), channel_id=1, source_target_pairs={{0,8},{4,12},{8,16},{12,20},{16,24},{20,28},{24,0},{28,4},{1,9},{5... | collective-permute-start | bytes 1105928 | tf_op jit(solution)/shard_map/ppermute | solution.py:691
  39.6 27.2 %collective-permute-start.18 = (bf16[90,16,128]{2,1,0:T(8,128)(2,1)S(1)}, bf16[90,16,128]{2,1,0:T(8,128)(2,1)S(1)}, u32[]{:S(2)}, u32[]{:S(2)}) collective-permute-start(bf16[90,16,128]{2,1,0:T(8,128)(2,1)S(1)} %collective-permute-done.7.refs_2_), channel_id=1, source_target_pairs={{0,4},{4,0},{8,12},{12,8},{16,20},{20,16},{24,28},{28,24},{1,5},{5... | collective-permute-start | bytes 1105928 | tf_op jit(solution)/shard_map/ppermute | solution.py:687
  40.2 19.1 %collective-permute-start.14 = (bf16[157,16,128]{2,1,0:T(8,128)(2,1)S(1)}, bf16[157,16,128]{2,1,0:T(8,128)(2,1)S(1)}, u32[]{:S(2)}, u32[]{:S(2)}) collective-permute-start(bf16[157,16,128]{2,1,0:T(8,128)(2,1)S(1)} %collective-permute-done.12.refs_1_), channel_id=1, source_target_pairs={{0,1},{1,0},{2,3},{3,2},{4,5},{5,4},{6,7},{7,6},{8,9},{9,8},{10,11... | collective-permute-start | bytes 1929224 | tf_op jit(solution)/shard_map/ppermute | solution.py:687
  45.1 12.6 %collective-permute-start.9 = (bf16[90,16,128]{2,1,0:T(8,128)(2,1)S(1)}, bf16[90,16,128]{2,1,0:T(8,128)(2,1)S(1)}, u32[]{:S(2)}, u32[]{:S(2)}) collective-permute-start(bf16[90,16,128]{2,1,0:T(8,128)(2,1)S(1)} %collective-permute-done.8.refs_4_), channel_id=1, source_target_pairs={{0,8},{4,12},{8,16},{12,20},{16,24},{20,28},{24,0},{28,4},{1,9},{5... | collective-permute-start | bytes 1105928 | tf_op jit(solution)/shard_map/ppermute | solution.py:691
  57.2 11.5 %collective-permute-start.19 = (bf16[90,16,128]{2,1,0:T(8,128)(2,1)S(1)}, bf16[90,16,128]{2,1,0:T(8,128)(2,1)S(1)}, u32[]{:S(2)}, u32[]{:S(2)}) collective-permute-start(bf16[90,16,128]{2,1,0:T(8,128)(2,1)S(1)} %collective-permute-done.8.refs_4_), channel_id=1, source_target_pairs={{0,4},{4,0},{8,12},{12,8},{16,20},{20,16},{24,28},{28,24},{1,5},{5... | collective-permute-start | bytes 1105928 | tf_op jit(solution)/shard_map/ppermute | solution.py:687
  57.7 17.3 %collective-permute-start.10 = (bf16[90,16,128]{2,1,0:T(8,128)(2,1)S(1)}, bf16[90,16,128]{2,1,0:T(8,128)(2,1)S(1)}, u32[]{:S(2)}, u32[]{:S(2)}) collective-permute-start(bf16[90,16,128]{2,1,0:T(8,128)(2,1)S(1)} %collective-permute-done.9.refs_0_), channel_id=1, source_target_pairs={{0,4},{4,0},{8,12},{12,8},{16,20},{20,16},{24,28},{28,24},{1,5},{5... | collective-permute-start | bytes 1105928 | tf_op jit(solution)/shard_map/ppermute | solution.py:687
  75.0 10.7 %copy-start.6 = (f32[16,16]{1,0:T(8,128)S(1)}, f32[16,16]{1,0:T(8,128)}, u32[]{:S(2)}) copy-start(f32[16,16]{1,0:T(8,128)} %time_ref.1) | copy-start | bytes 3076
  78.2 2.0 %collective-permute-start.20 = (f32[72,128]{1,0:T(8,128)S(1)}, f32[72,128]{1,0:T(8,128)S(1)}, u32[]{:S(2)}, u32[]{:S(2)}) collective-permute-start(f32[72,128]{1,0:T(8,128)S(1)} %panel_last.1), channel_id=1, source_target_pairs={{0,1},{1,0},{2,3},{3,2},{4,5},{5,4},{6,7},{7,6},{8,9},{9,8},{10,11... | collective-permute-start | bytes 110600 | tf_op jit(solution)/shard_map/ppermute | solution.py:691
  78.3 4.0 %collective-permute-start.21 = (f32[72,128]{1,0:T(8,128)S(1)}, f32[72,128]{1,0:T(8,128)S(1)}, u32[]{:S(2)}, u32[]{:S(2)}) collective-permute-start(f32[72,128]{1,0:T(8,128)S(1)} %panel_last.1), channel_id=1, source_target_pairs={{0,2},{1,3},{2,0},{3,1},{4,6},{5,7},{6,4},{7,5},{8,10},{9,11},{10,... | collective-permute-start | bytes 110600 | tf_op jit(solution)/shard_map/ppermute | solution.py:691
  79.9 3.4 %collective-permute-start.22 = (f32[72,128]{1,0:T(8,128)S(1)}, f32[72,128]{1,0:T(8,128)S(1)}, u32[]{:S(2)}, u32[]{:S(2)}) collective-permute-start(f32[72,128]{1,0:T(8,128)S(1)} %panel_last.1), channel_id=1, source_target_pairs={{0,3},{1,2},{2,1},{3,0},{4,7},{5,6},{6,5},{7,4},{8,11},{9,10},{10,... | collective-permute-start | bytes 110600 | tf_op jit(solution)/shard_map/ppermute | solution.py:691

commit v3 on v2

--- a/solution.py
+++ b/solution.py
@@ -42,6 +42,12 @@
 def slot_count(tiles, extra):
     room = tiles / 2 + 4.1 * math.sqrt(tiles / 4)
     return extra + min(tiles + 1, 2 * math.ceil(room / 2) + 1)
+
+
+def chunk_sizes(slots, tiles, extra):
+    most = min(slots - 2, extra + math.ceil(tiles * 3 / 8 + 3.4 * math.sqrt(tiles * 3 / 16)))
+    least = min(extra + tiles // 10, most - 1)
+    return least, most - least, slots - most
 
 
 def pack_rows(mask_at, feet_at, begin, end, blocks, buf, carry):
@@ -230,9 +236,9 @@
     head = buf[0].astype(F32)
     scale = float(1 << SHIFT)
     bits_v[0:deep, :] = jnp.minimum(head[0:deep] * scale + head[deep : 2 * deep], slots - 1.0).astype(I32)
-    bits_v[deep : deep + 1, :] = (head[2 * deep : 2 * deep + 1] * scale + head[2 * deep + 1 : 2 * deep + 2]).astype(I32)
+    bits_v[5:6, :] = (head[2 * deep : 2 * deep + 1] * scale + head[2 * deep + 1 : 2 * deep + 2]).astype(I32)
     if flagged:
-        bits_v[deep + 1 : deep + 2, :] = head[2 * deep + 2 : 2 * deep + 3].astype(I32)
+        bits_v[6:7, :] = head[2 * deep + 2 : 2 * deep + 3].astype(I32)
     buf[0] = jnp.zeros(buf.shape[1:], buf.dtype)
 
 
@@ -464,98 +470,169 @@
     return jnp.swapaxes(value.reshape(rows, times, value.shape[1]), 0, 1)
 
 
-def rows_kernel(count, chunks, unit, late, *refs):
+def unit_step(u, count, unit, bufs, bits_s, dense_a, dense_b, near_ref, cov_ref, mix_ref, rows):
+    times, _ = bufs.shape[2:]
+    cells = near_ref.shape[1]
+    few = count // 2
+    here = aligned(u * unit * times, unit * times)
+    place(u, few, count, unit, bufs, bits_s, dense_b, cells)
+    value = near_ref[here, :] + jnp.dot(dense_a[...], cov_ref[: few * cells, :], preferred_element_type=F32)
+    place(jnp.minimum(u + 1, rows // unit - 1), 0, few, unit, bufs, bits_s, dense_a, cells)
+    value = value + jnp.dot(dense_b[...], cov_ref[few * cells :, :], preferred_element_type=F32)
+    return mixed_unit(mix_ref, value)
+
+
+def place(u, begin, end, unit, bufs, bits_s, dense, cells):
+    times, lanes = bufs.shape[2:]
+    for k in range(begin, end):
+        store = into(dense, times, lanes, (k - begin) * cells)
+        expand(bufs.at[k], bits_s.at[k], u * unit, unit, cells // lanes, store, unrolled=bufs.shape[0] <= 4)
+
+
+def first_kernel(count, chunks, unit, *refs):
     msgs = [refs[k * chunks : (k + 1) * chunks] for k in range(count)]
-    refs = refs[count * chunks :]
-    cov_ref, near_ref, mix_ref = refs[:3]
-    if late:
-        start_ref, done_ref, out_ref, turned_ref = refs[3:7]
-    else:
-        out_ref, next_ref = refs[3:5]
-    bufs, bits_v, bits_s, dense_a, dense_b, sem = refs[-6:]
+    cov_ref, near_ref, mix_ref, out_ref, next_ref, bufs, bits_v, bits_s, dense_a, dense_b, sem = refs[count * chunks :]
     times, lanes = bufs.shape[2:]
     cells = near_ref.shape[1]
     blocks = cells // lanes
     rows = out_ref.shape[0]
-    few = count // 2
-    deep = -(-rows * blocks // lanes)
+    limit = sum(chunk.shape[0] for chunk in msgs[0])
     copies = [fetch(msgs[k], bufs.at[k], sem.at[k]) for k in range(count)]
     for k in range(count):
         for copy in copies[k]:
             copy.wait()
         read_head(bufs.at[k], rows, blocks, bits_v.at[k])
-    copy = pltpu.make_async_copy(bits_v, bits_s, sem.at[count, 0])
-    copy.start()
-
-    def place(u, begin, end, dense):
-        for k in range(begin, end):
-            store = into(dense, times, lanes, (k - begin) * cells)
-            expand(bufs.at[k], bits_s.at[k], u * unit, unit, blocks, store, unrolled=count <= 4)
+    copy_in(bits_v, bits_s, sem.at[count, 0])
+    ready = jnp.int32(0)
+    for u in range(rows // unit):
+        whole = jnp.int32(1)
+        for k in range(count):
+            whole = whole * (bits_s[k, 5, (u + 1) * unit - 1] <= limit).astype(I32)
+        ready = ready + whole
+    next_ref[0] = ready
+    place(jnp.int32(0), 0, count // 2, unit, bufs, bits_s, dense_a, cells)
 
     def step(u, _):
-        here = aligned(u * unit * times, unit * times)
-        place(u, few, count, dense_b)
-        value = near_ref[here, :] + jnp.dot(dense_a[...], cov_ref[: few * cells, :], preferred_element_type=F32)
-        place(jnp.minimum(u + 1, rows // unit - 1), 0, few, dense_a)
-        value = value + jnp.dot(dense_b[...], cov_ref[few * cells :, :], preferred_element_type=F32)
-        mixed = mixed_unit(mix_ref, value)
-        at = aligned(u * unit, unit)
-        out_ref[at] = mixed.reshape(unit, times, cells)
-        if late:
-            turned_ref[:, at, :] = turn(mixed, unit, times)
+        mixed = unit_step(u, count, unit, bufs, bits_s, dense_a, dense_b, near_ref, cov_ref, mix_ref, rows)
+        out_ref[aligned(u * unit, unit)] = mixed.reshape(unit, times, cells)
         return 0
 
-    def carry_over(u, _):
-        at = aligned(u * unit, unit)
-        value = done_ref[at]
-        out_ref[at] = value
-        turned_ref[:, at, :] = turn(value.reshape(unit * times, cells), unit, times)
-        return 0
-
-    if late:
-        first = start_ref[0]
-        lax.fori_loop(0, first, carry_over, 0)
-        copy.wait()
-        place(jnp.minimum(first, rows // unit - 1), 0, few, dense_a)
-        lax.fori_loop(first, rows // unit, step, 0)
-    else:
-        copy.wait()
-        limit = sum(chunk.shape[0] for chunk in msgs[0])
-        ready = jnp.int32(0)
-        for u in range(rows // unit):
-            whole = jnp.int32(1)
-            for k in range(count):
-                whole = whole * (bits_s[k, deep, (u + 1) * unit - 1] <= limit).astype(I32)
-            ready = ready + whole
-        next_ref[0] = ready
-        place(jnp.int32(0), 0, few, dense_a)
-        lax.fori_loop(0, ready, step, 0)
-
-
-def some_rows(msgs, cov, near, mix, rows, unit, slots, carried=None):
+    lax.fori_loop(0, ready, step, 0)
+
+
+def rows_scratch(count, chunks, slots, times, lanes, unit, cells, more):
+    return [
+        pltpu.VMEM((count, slots, times, lanes), BF16),
+        pltpu.VMEM((count + more, 8, lanes), I32),
+        pltpu.SMEM((count + more, 8, lanes), I32),
+        pltpu.VMEM((unit * times, count // 2 * cells), BF16),
+        pltpu.VMEM((unit * times, (count - count // 2) * cells), BF16),
+        pltpu.SemaphoreType.DMA((count + 1, chunks)),
+    ]
+
+
+def first_rows(msgs, cov, near, mix, rows, unit, slots):
     times, lanes = msgs[0][0].shape[1:]
     cells = near.shape[1]
     count, chunks = len(msgs), len(msgs[0])
-    late = carried is not None
     flat = [chunk for msg in msgs for chunk in msg]
-    out = shape_of((rows, times, cells), BF16)
     return pl.pallas_call(
-        functools.partial(rows_kernel, count, chunks, unit, late),
-        out_shape=(out, shape_of((times, rows, cells), BF16) if late else shape_of((1,), I32)),
-        in_specs=[ANY] * len(flat) + [VMEM] * 3 + ([SMEM, VMEM] if late else []),
-        out_specs=(VMEM, VMEM if late else SMEM),
-        scratch_shapes=[
-            pltpu.VMEM((count, slots, times, lanes), BF16),
-            pltpu.VMEM((count, 8, lanes), I32),
-            pltpu.SMEM((count, 8, lanes), I32),
-            pltpu.VMEM((unit * times, count // 2 * cells), BF16),
-            pltpu.VMEM((unit * times, (count - count // 2) * cells), BF16),
-            pltpu.SemaphoreType.DMA((count + 1, chunks)),
+        functools.partial(first_kernel, count, chunks, unit),
+        out_shape=(shape_of((rows, times, cells), BF16), shape_of((1,), I32)),
+        in_specs=[ANY] * len(flat) + [VMEM] * 3,
+        out_specs=(VMEM, SMEM),
+        scratch_shapes=rows_scratch(count, chunks, slots, times, lanes, unit, cells, 0),
+        compiler_params=params(16),
+        cost_estimate=cost(7),
+        name="first_rows",
+    )(*flat, cov, near, mix)
+
+
+def late_kernel(count, chunks, unit, pieces, each, *refs):
+    msgs = [refs[k * chunks : (k + 1) * chunks] for k in range(count)]
+    panel_msgs = refs[count * chunks : count * chunks + pieces]
+    refs = refs[count * chunks + pieces :]
+    cov_ref, near_ref, mix_ref, start_ref, done_ref, out_ref, turned_ref, part_ref, over_ref = refs[:9]
+    bufs, bits_v, bits_s, dense_a, dense_b, sem, panel_bufs, stage, panel, panel_sem, out_sem = refs[9:]
+    times, lanes = bufs.shape[2:]
+    cells = near_ref.shape[1]
+    blocks = cells // lanes
+    rows = stage.shape[0]
+    copies = [fetch(msgs[k], bufs.at[k], sem.at[k]) for k in range(count)]
+    panel_copies = [pltpu.make_async_copy(msg, panel_bufs.at[k], panel_sem.at[k]) for k, msg in enumerate(panel_msgs)]
+    for copy in panel_copies:
+        copy.start()
+    for k in range(count):
+        for copy in copies[k]:
+            copy.wait()
+        read_head(bufs.at[k], rows, blocks, bits_v.at[k])
+    for k, copy in enumerate(panel_copies):
+        copy.wait()
+        read_head(panel_bufs.at[k], each, blocks, bits_v.at[count + k], flagged=True)
+    bits_copy = pltpu.make_async_copy(bits_v, bits_s, sem.at[count, 0])
+    bits_copy.start()
+    first = start_ref[0]
+
+    def outgoing(u, src):
+        at = aligned(u * unit, unit)
+        return pltpu.make_async_copy(src.at[at], out_ref.at[at], out_sem.at[u])
+
+    def carry_over(u, _):
+        outgoing(u, done_ref).start()
+        at = aligned(u * unit, unit)
+        turned_ref[:, at, :] = turn(done_ref[at].reshape(unit * times, cells), unit, times)
+        return 0
+
+    lax.fori_loop(0, first, carry_over, 0)
+    bits_copy.wait()
+    place(jnp.minimum(first, rows // unit - 1), 0, count // 2, unit, bufs, bits_s, dense_a, cells)
+
+    def step(u, _):
+        mixed = unit_step(u, count, unit, bufs, bits_s, dense_a, dense_b, near_ref, cov_ref, mix_ref, rows)
+        at = aligned(u * unit, unit)
+        stage[at] = mixed.reshape(unit, times, cells)
+        outgoing(u, stage).start()
+        turned_ref[:, at, :] = turn(mixed, unit, times)
+        return 0
+
+    lax.fori_loop(first, rows // unit, step, 0)
+    over_ref[0] = panel_over(panel_bufs, bits_s, count, pieces, each)
+    part_ref[...] = panel_products(panel_bufs, bits_s, count, pieces, each, turned_ref, panel)
+
+    def settle(u, _):
+        outgoing(u, stage).wait()
+        return 0
+
+    lax.fori_loop(0, rows // unit, settle, 0)
+
+
+def late_rows(msgs, panel_msgs, each, cov, near, mix, start, done, unit, slots):
+    times, lanes = msgs[0][0].shape[1:]
+    rows, _, cells = done.shape
+    count, chunks, pieces = len(msgs), len(msgs[0]), len(panel_msgs)
+    flat = [chunk for msg in msgs for chunk in msg] + list(panel_msgs)
+    return pl.pallas_call(
+        functools.partial(late_kernel, count, chunks, unit, pieces, each),
+        out_shape=(
+            shape_of(done.shape, BF16),
+            shape_of((times, rows, cells), BF16),
+            shape_of((rows, pieces * each), F32),
+            shape_of((1,), I32),
+        ),
+        in_specs=[ANY] * len(flat) + [VMEM] * 3 + [SMEM, VMEM],
+        out_specs=(HBM, VMEM, VMEM, SMEM),
+        scratch_shapes=rows_scratch(count, chunks, slots, times, lanes, unit, cells, pieces)
+        + [
+            pltpu.VMEM((pieces, panel_msgs[0].shape[0], times, lanes), BF16),
+            pltpu.VMEM((rows, times, cells), BF16),
+            pltpu.VMEM((times, pieces * each, cells), BF16),
+            pltpu.SemaphoreType.DMA((pieces,)),
+            pltpu.SemaphoreType.DMA((rows // unit,)),
         ],
-        compiler_params=params(16),
-        cost_estimate=cost(6),
-        name="late_rows" if late else "first_rows",
-    )(*flat, cov, near, mix, *(carried or ()))
+        compiler_params=params(20),
+        cost_estimate=cost(9),
+        name="late_rows",
+    )(*flat, cov, near, mix, start, done)
 
 
 def mix_kernel(unit, time_ref, out_ref):
@@ -590,28 +667,18 @@
     )(time_cov)
 
 
-def panel_kernel(pieces, each, final, *refs):
-    msgs = refs[:pieces]
-    refs = refs[pieces:]
-    if final:
-        group_ref, turned, before_ref, over_ref, out_ref = refs[:5]
-    else:
-        turned, out_ref, over_ref = refs[:3]
-    bufs, bits_v, bits_s, panel, sem = refs[-5:]
-    slots, times, lanes = bufs.shape[1:]
-    rows, cells = turned.shape[1:]
-    blocks = cells // lanes
-    deep = -(-each * blocks // lanes)
-    copies = [pltpu.make_async_copy(msg, bufs.at[k], sem.at[k]) for k, msg in enumerate(msgs)]
-    for copy in copies:
-        copy.start()
-    for k, copy in enumerate(copies):
-        copy.wait()
-        read_head(bufs.at[k], each, blocks, bits_v.at[k], flagged=True)
-    copy_in(bits_v, bits_s, sem.at[pieces])
-    over = over_ref[0] if final else jnp.int32(0)
+def panel_over(bufs, bits_s, base, pieces, each):
+    slots, _, _ = bufs.shape[1:]
+    over = jnp.int32(0)
     for k in range(pieces):
-        over = over + (bits_s[k, deep, each - 1] > slots - 1).astype(I32) + bits_s[k, deep + 1, 0]
+        ends = bits_s.shape[1] - 3
+        over = over + (bits_s[base + k, ends, each - 1] > slots - 1).astype(I32) + bits_s[base + k, ends + 1, 0]
+    return over
+
+
+def panel_products(bufs, bits_s, base, pieces, each, turned, panel):
+    times, lanes = bufs.shape[2:]
+    blocks = panel.shape[2] // lanes
     group = max(1, 16 // each)
 
     @pl.loop(0, pieces // group)
@@ -620,7 +687,7 @@
             tiles = []
             for i in range(group * each):
                 k, place = g * group + i // each, i % each * blocks + b
-                tiles.append(bufs[k, bits_s[k, place // lanes, place % lanes]])
+                tiles.append(bufs[k, bits_s[base + k, place // lanes, place % lanes]])
             value = turn(jnp.concatenate(tiles, axis=0), group * each, times)
             panel[:, aligned(g * group * each, group * each), b * lanes : (b + 1) * lanes] = value
 
@@ -628,12 +695,23 @@
     for t in range(times):
         value = lax.dot_general(turned[t], panel[t], (((1,), (1,)), ((), ())), preferred_element_type=F32)
         total = value if total is None else total + value
-    if not final:
-        out_ref[...] = total
-        over_ref[0] = over
-        return
-    value = jnp.concatenate([before_ref[...], total], axis=1)
-    size = value.shape[1]
+    return total
+
+
+def last_kernel(pieces, each, *refs):
+    msgs = refs[:pieces]
+    group_ref, turned, before_ref, over_ref, out_ref, bufs, bits_v, bits_s, panel, sem = refs[pieces:]
+    _, lanes = bufs.shape[2:]
+    rows, cells = turned.shape[1:]
+    copies = [pltpu.make_async_copy(msg, bufs.at[k], sem.at[k]) for k, msg in enumerate(msgs)]
+    for copy in copies:
+        copy.start()
+    for k, copy in enumerate(copies):
+        copy.wait()
+        read_head(bufs.at[k], each, cells // lanes, bits_v.at[k], flagged=True)
+    bits_copy = pltpu.make_async_copy(bits_v, bits_s, sem.at[pieces])
+    bits_copy.start()
+    size = out_ref.shape[1]
     row = lax.broadcasted_iota(I32, (size, size), 0)
     half = size // each // 2
     hi, lo = split(group_ref[0], 2)
@@ -643,6 +721,10 @@
         source = jnp.where(back < 0, back + half, back) * 2 + lax.bitwise_xor(lo, k % 2)
         target = jnp.where((row >= k * each) & (row < (k + 1) * each), row + (source - k) * each, target)
     select = (lax.broadcasted_iota(I32, (size, size), 1) == target).astype(F32).astype(BF16)
+    bits_copy.wait()
+    over = over_ref[0] + panel_over(bufs, bits_s, 0, pieces, each)
+    total = panel_products(bufs, bits_s, 0, pieces, each, turned, panel)
+    value = jnp.concatenate([before_ref[...], total], axis=1)
     total = jnp.zeros(value.shape, F32)
     for _ in range(3):
         high = value.astype(BF16)
@@ -652,35 +734,26 @@
     out_ref[rows:, :] = jnp.broadcast_to(over, (8, size)).astype(F32)
 
 
-def panel_part(msgs, turned, each, final=None):
+def panel_last(msgs, turned, each, group, before, over):
     slots, times, lanes = msgs[0].shape
     rows, cells = turned.shape[1:]
     pieces = len(msgs)
-    width = pieces * each
-    if final:
-        group, before, over = final
-        operands, in_specs = (group[None], turned, before, over), [SMEM, VMEM, VMEM, SMEM]
-        out_shape = shape_of((rows + 8, before.shape[1] + width), F32)
-        out_specs = VMEM
-    else:
-        operands, in_specs = (turned,), [VMEM]
-        out_shape, out_specs = (shape_of((rows, width), F32), shape_of((1,), I32)), (VMEM, SMEM)
     return pl.pallas_call(
-        functools.partial(panel_kernel, pieces, each, bool(final)),
-        out_shape=out_shape,
-        in_specs=[ANY] * pieces + in_specs,
-        out_specs=out_specs,
+        functools.partial(last_kernel, pieces, each),
+        out_shape=shape_of((rows + 8, before.shape[1] + pieces * each), F32),
+        in_specs=[ANY] * pieces + [SMEM, VMEM, VMEM, SMEM],
+        out_specs=VMEM,
         scratch_shapes=[
             pltpu.VMEM((pieces, slots, times, lanes), BF16),
             pltpu.VMEM((pieces, 8, lanes), I32),
             pltpu.SMEM((pieces, 8, lanes), I32),
-            pltpu.VMEM((times, width, cells), BF16),
+            pltpu.VMEM((times, pieces * each, cells), BF16),
             pltpu.SemaphoreType.DMA((pieces + 1,)),
         ],
         compiler_params=params(14),
-        cost_estimate=cost(3 if final else 5),
-        name="panel_last" if final else "panel_first",
-    )(*msgs, *operands)
+        cost_estimate=cost(3),
+        name="panel_last",
+    )(*msgs, group[None], turned, before, over)
 
 
 def partner(value, axis, count):
@@ -748,7 +821,7 @@
     half = observers // 2
     unit = math.gcd(16, obs_rows)
     slots = slot_count(obs_rows * blocks, 1 + blocks)
-    chunks = (slots - slots // 2, slots // 2)
+    chunks = chunk_sizes(slots, obs_rows * blocks, 1 + blocks)
     mask = block_mask.T
 
     room = slots - 2 - blocks - 1
@@ -771,11 +844,12 @@
     near, mate_dense, mate_cov = own_call(mate_msg, dense, own_cov, info)
     near, far_cov = mate_call([msg[0] for msg in far_msgs], near, mate_dense, mate_cov, info)
     mix = mixing(time_cov, unit)
-    first_cov, start = some_rows([msg[:1] for msg in far_msgs], far_cov, near, mix, obs_rows, unit, slots)
-    cov_product, turned = some_rows(far_msgs, far_cov, near, mix, obs_rows, unit, slots, (start, first_cov))
+    first_cov, start = first_rows([msg[:-1] for msg in far_msgs], far_cov, near, mix, obs_rows, unit, slots)
     cut = len(messages) * 3 // 4
-    before, over = panel_part(messages[:cut], turned, each)
-    part = panel_part(messages[cut:], turned, each, (group, before, over))
+    cov_product, turned, before, over = late_rows(
+        far_msgs, messages[:cut], each, far_cov, near, mix, start, first_cov, unit, slots
+    )
+    part = panel_last(messages[cut:], turned, each, group, before, over)
 
     def innovation_of(total, group):
         positions = jnp.arange(obs_rows, dtype=I32)

time: 86.6 us -> 90.9 us (1.050)
  local copies, waits for them, and re-layouts: 2.65 us -> 5.34 us
  starting transfers between devices: 14 us -> 15.5 us
    unnamed x14 -> x22, local copies, waits for them, and re-layouts: 2.08 us -> 4.74 us
    ppermute x8 -> x9, waiting for transfers between devices: 18.6 us -> 20.5 us  [shifted(): lax.ppermute(value, axis, [(i, (i + 2 * shift) % count ^ flip) for i in r...]
    ppermute x8 -> x10, waiting for transfers between devices: 3.27 us -> 1.93 us  [partner(): return lax.ppermute(value, axis, [(i, i ^ 1) for i in range(count)])]
    ppermute x8 -> x9, starting transfers between devices: 8.69 us -> 9.95 us  [shifted(): lax.ppermute(value, axis, [(i, (i + 2 * shift) % count ^ flip) for i in r...]
    ppermute x8 -> x10, starting transfers between devices: 5.29 us -> 5.55 us  [partner(): return lax.ppermute(value, axis, [(i, i ^ 1) for i in range(count)])]
    pallas_call x4 -> x3, Pallas kernels: 21 us -> 21.2 us  [the longest x1 10.2 us: late_rows(): pl.pallas_call(functools.partial(late_kernel, count, chunks, unit, pieces...]
  transfers between devices with their start and end apart: 16 -> 19, of which waited for: 6 -> 7; matrix products, arithmetic and copies ran while one was open for 0% -> 0% of each run, Pallas kernels for 43% -> 41%
where the time goes in v3:
time: 90.9 us; the launch traced here: 90.6 us
  Pallas kernels  44.8 us (49%)
  waiting for transfers between devices  22.4 us (25%)
  starting transfers between devices  15.5 us (17%)
  local copies, waits for them, and re-layouts  5.34 us (6%)
  between operations  1.55 us (2%)
    ppermute x9, waiting for transfers between devices, shifted(): lax.ppermute(value, axis, [(i, (i + 2 * shift) % count ^ flip) for i in r...  20.5 us
    pallas_call x1, Pallas kernels, late_rows(): pl.pallas_call(functools.partial(late_kernel, count, chunks, unit, pieces...  10.2 us
    ppermute x9, starting transfers between devices, shifted(): lax.ppermute(value, axis, [(i, (i + 2 * shift) % count ^ flip) for i in r...  9.95 us
    pallas_call x1, Pallas kernels, first_rows(): pl.pallas_call(functools.partial(first_kernel, count, chunks, unit), out_...  7.89 us
    pallas_call x1, Pallas kernels, mate_call(): pl.pallas_call(functools.partial(mate_kernel, count), out_shape=(shape_of...  6.7 us
    pallas_call x1, Pallas kernels, own_call(): pl.pallas_call(functools.partial(own_kernel, chunks), out_shape=(shape_of...  5.83 us
    ppermute x10, starting transfers between devices, partner(): return lax.ppermute(value, axis, [(i, i ^ 1) for i in range(count)])  5.55 us
    unnamed x22, local copies, waits for them, and re-layouts  4.74 us
  transfers between devices with their start and end apart: 19, of which 7 were waited for; matrix products, arithmetic and copies ran while one was open for 0% of the time, Pallas kernels for 41%

profile of v3, /device:TPU:0, one launch (start us, length us, event | category | flops | bytes accessed | tf_op | source)
XLA Modules:
  0.0 90.6 jit_solution(17447163949930197957)
XLA Ops:
  2.7 4.2 %pack_feet.1 = (bf16[60,16,128]{2,1,0:T(8,128)(2,1)S(1)}, bf16[175,16,128]{2,1,0:T(8,128)(2,1)S(1)}, bf16[79,16,128]{2,1,0:T(8,128)(2,1)S(1)}) custom-call(s32[8,64]{1,0:T(8,128)S(1)} %bitcast.74, s32[2,1024]{1,0:T(2,128)S(1)} %copy-done.2, f32[1,1024]{1,0:T(1,128)S(1)} %bitcast.78, bf16[64,16,1024]{2,1,0:T(8,128)(2,1)} %feet_ref.3), custom_call_target="tpu_custom_call" | custom-call | flops 2700000000 | bytes 1000000 | tf_op jit(solution)/shard_map/pack_feet/pallas_call | solution.py:157
  6.9 3.0 %collective-permute-start.12 = (bf16[175,16,128]{2,1,0:T(8,128)(2,1)S(1)}, bf16[175,16,128]{2,1,0:T(8,128)(2,1)S(1)}, u32[]{:S(2)}, u32[]{:S(2)}) collective-permute-start(bf16[175,16,128]{2,1,0:T(8,128)(2,1)S(1)} %get-tuple-element.123.refs_1_), channel_id=1, source_target_pairs={{0,2},{1,3},{2,0},{3,1},{4,6},{5,7},{6,4},{7,5},{8,10},{9,11},{10,... | collective-permute-start | bytes 2150408 | tf_op jit(solution)/shard_map/ppermute | solution.py:764
  10.5 4.2 %own_start.1 = (bf16[1024,1024]{1,0:T(8,128)(2,1)S(1)}, bf16[1024,1024]{1,0:T(8,128)(2,1)S(1)}, f32[8,1024]{1,0:T(8,128)S(1)}) custom-call(bf16[60,16,128]{2,1,0:T(8,128)(2,1)S(1)} %get-tuple-element.122.refs_0_, bf16[175,16,128]{2,1,0:T(8,128)(2,1)S(1)} %get-tuple-element.123.refs_1_, bf16[79,16,128]{2,1,0:T(8,128)(2,1)S(1)} %get-tuple-element.124.refs_2_), custom_call_target="tpu_custom_call" | custom-call | flops 3600000000 | bytes 1000000 | tf_op jit(solution)/shard_map/own_start/pallas_call | solution.py:346
  14.7 1.3 %copy-done.4 = bf16[1024,1024]{1,0:T(8,128)(2,1)} copy-done((bf16[1024,1024]{1,0:T(8,128)(2,1)}, bf16[1024,1024]{1,0:T(8,128)(2,1)S(1)}, u32[]{:S(2)}) %copy-start.4) | copy-done | bytes 2097176
  16.0 1.3 %copy-done.6 = bf16[1024,1024]{1,0:T(8,128)(2,1)} copy-done((bf16[1024,1024]{1,0:T(8,128)(2,1)}, bf16[1024,1024]{1,0:T(8,128)(2,1)S(1)}, u32[]{:S(2)}) %copy-start.6) | copy-done | bytes 2097176
  17.8 2.4 %pack_panel.1.refs_6_ = bf16[90,16,128]{2,1,0:T(8,128)(2,1)S(1)} custom-call(s32[8,64]{1,0:T(8,128)S(1)} %bitcast.75, s32[8,64]{1,0:T(8,128)S(1)} %bitcast.76, s32[128]{0:T(128)S(1)} %copy-done.10, s32[1]{0:T(128)} %bitcast.12.group_ref.refs_2_, bf16[64,16,1024]{2,1,0:T(8,128)(2,1)} %feet_ref.3), custom_call_target="tpu_custom_call" | custom-call | flops 1800000000 | bytes 1000000 | tf_op jit(solution)/shard_map/pack_panel/pallas_call | solution.py:206
  20.3 1.8 %collective-permute-start.13 = (bf16[79,16,128]{2,1,0:T(8,128)(2,1)S(1)}, bf16[79,16,128]{2,1,0:T(8,128)(2,1)S(1)}, u32[]{:S(2)}, u32[]{:S(2)}) collective-permute-start(bf16[79,16,128]{2,1,0:T(8,128)(2,1)S(1)} %get-tuple-element.124.refs_2_), channel_id=1, source_target_pairs={{0,2},{1,3},{2,0},{3,1},{4,6},{5,7},{6,4},{7,5},{8,10},{9,11},{10,... | collective-permute-start | bytes 970760 | tf_op jit(solution)/shard_map/ppermute | solution.py:764
  22.1 10.0 %collective-permute-done.11.refs_0_ = bf16[60,16,128]{2,1,0:T(8,128)(2,1)S(1)} collective-permute-done((bf16[60,16,128]{2,1,0:T(8,128)(2,1)S(1)}, bf16[60,16,128]{2,1,0:T(8,128)(2,1)S(1)}, u32[]{:S(2)}, u32[]{:S(2)}) %collective-permute-start.11) | collective-permute-done | bytes 245792 | tf_op jit(solution)/shard_map/ppermute | solution.py:764
  32.1 2.1 %collective-permute-start.7 = (bf16[90,16,128]{2,1,0:T(8,128)(2,1)S(1)}, bf16[90,16,128]{2,1,0:T(8,128)(2,1)S(1)}, u32[]{:S(2)}, u32[]{:S(2)}) collective-permute-start(bf16[90,16,128]{2,1,0:T(8,128)(2,1)S(1)} %pack_panel.1.refs_6_), channel_id=1, source_target_pairs={{0,8},{4,12},{8,16},{12,20},{16,24},{20,28},{24,0},{28,4},{1,9},{5... | collective-permute-start | bytes 1105928 | tf_op jit(solution)/shard_map/ppermute | solution.py:764
  34.7 5.8 %own_product.1 = (f32[1024,1024]{1,0:T(8,128)S(1)}, bf16[1024,1024]{1,0:T(8,128)(2,1)S(1)}, bf16[1024,1024]{1,0:T(8,128)(2,1)S(1)}) custom-call(bf16[60,16,128]{2,1,0:T(8,128)(2,1)S(1)} %collective-permute-done.20.refs_0_, bf16[175,16,128]{2,1,0:T(8,128)(2,1)S(1)} %collective-permute-done.21.refs_1_, ...), custom_call_target="tpu_custom_call" | custom-call | flops 5400000000 | bytes 1000000 | tf_op jit(solution)/shard_map/own_product/pallas_call | solution.py:398
  40.6 1.6 %collective-permute-start.17 = (bf16[90,16,128]{2,1,0:T(8,128)(2,1)S(1)}, bf16[90,16,128]{2,1,0:T(8,128)(2,1)S(1)}, u32[]{:S(2)}, u32[]{:S(2)}) collective-permute-start(bf16[90,16,128]{2,1,0:T(8,128)(2,1)S(1)} %pack_panel.1.refs_6_), channel_id=1, source_target_pairs={{0,4},{4,0},{8,12},{12,8},{16,20},{20,16},{24,28},{28,24},{1,5},{5... | collective-permute-start | bytes 1105928 | tf_op jit(solution)/shard_map/ppermute | solution.py:760
  42.8 1.0 %collective-permute-start.8 = (bf16[90,16,128]{2,1,0:T(8,128)(2,1)S(1)}, bf16[90,16,128]{2,1,0:T(8,128)(2,1)S(1)}, u32[]{:S(2)}, u32[]{:S(2)}) collective-permute-start(bf16[90,16,128]{2,1,0:T(8,128)(2,1)S(1)} %collective-permute-done.7.refs_8_), channel_id=1, source_target_pairs={{0,8},{4,12},{8,16},{12,20},{16,24},{20,28},{24,0},{28,4},{1,9},{5... | collective-permute-start | bytes 1105928 | tf_op jit(solution)/shard_map/ppermute | solution.py:764
  43.8 6.7 %mate_product.1 = (f32[1024,1024]{1,0:T(8,128)S(1)}, bf16[2048,1024]{1,0:T(8,128)(2,1)S(1)}) custom-call(bf16[60,16,128]{2,1,0:T(8,128)(2,1)S(1)} %collective-permute-done.11.refs_0_, bf16[60,16,128]{2,1,0:T(8,128)(2,1)S(1)} %collective-permute-done.14.refs_1_.refs_2_.refs_3_, ...), custom_call_target="tpu_custom_call", output_to_operand_aliasing={{0}: (2, {})} | custom-call | flops 7200000000 | bytes 1000000 | tf_op jit(solution)/shard_map/mate_product/pallas_call | solution.py:445
  51.2 3.8 %collective-permute-done.8.refs_10_ = bf16[90,16,128]{2,1,0:T(8,128)(2,1)S(1)} collective-permute-done((bf16[90,16,128]{2,1,0:T(8,128)(2,1)S(1)}, bf16[90,16,128]{2,1,0:T(8,128)(2,1)S(1)}, u32[]{:S(2)}, u32[]{:S(2)}) %collective-permute-start.8) | collective-permute-done | bytes 368672 | tf_op jit(solution)/shard_map/ppermute | solution.py:764
  55.5 7.9 %first_rows.1 = (bf16[64,16,1024]{2,1,0:T(8,128)(2,1)S(1)}, s32[1]{0:T(128)}) custom-call(bf16[60,16,128]{2,1,0:T(8,128)(2,1)S(1)} %collective-permute-done.11.refs_0_, bf16[175,16,128]{2,1,0:T(8,128)(2,1)S(1)} %collective-permute-done.12.refs_1_, bf16[60,16,128]{2,1,0:T(8,128)(2,1)S(1)} %collective-permute-done.14.refs_1_.refs_2_.refs_3_, ...), custom_call_target="tpu_custom_call" | custom-call | flops 6300000256 | bytes 1000000 | tf_op jit(solution)/shard_map/first_rows/pallas_call | solution.py:539
  63.4 2.9 %collective-permute-done.9.refs_0_ = bf16[90,16,128]{2,1,0:T(8,128)(2,1)S(1)} collective-permute-done((bf16[90,16,128]{2,1,0:T(8,128)(2,1)S(1)}, bf16[90,16,128]{2,1,0:T(8,128)(2,1)S(1)}, u32[]{:S(2)}, u32[]{:S(2)}) %collective-permute-start.9) | collective-permute-done | bytes 368672 | tf_op jit(solution)/shard_map/ppermute | solution.py:764
  66.3 1.7 %collective-permute-start.10 = (bf16[90,16,128]{2,1,0:T(8,128)(2,1)S(1)}, bf16[90,16,128]{2,1,0:T(8,128)(2,1)S(1)}, u32[]{:S(2)}, u32[]{:S(2)}) collective-permute-start(bf16[90,16,128]{2,1,0:T(8,128)(2,1)S(1)} %collective-permute-done.9.refs_0_), channel_id=1, source_target_pairs={{0,4},{4,0},{8,12},{12,8},{16,20},{20,16},{24,28},{28,24},{1,5},{5... | collective-permute-start | bytes 1105928 | tf_op jit(solution)/shard_map/ppermute | solution.py:760
  68.0 1.9 %collective-permute-done.19.refs_11_ = bf16[90,16,128]{2,1,0:T(8,128)(2,1)S(1)} collective-permute-done((bf16[90,16,128]{2,1,0:T(8,128)(2,1)S(1)}, bf16[90,16,128]{2,1,0:T(8,128)(2,1)S(1)}, u32[]{:S(2)}, u32[]{:S(2)}) %collective-permute-start.19) | collective-permute-done | bytes 368672 | tf_op jit(solution)/shard_map/ppermute | solution.py:760
  70.0 10.2 %late_rows.1 = (bf16[64,16,1024]{2,1,0:T(8,128)(2,1)}, bf16[16,64,1024]{2,1,0:T(8,128)(2,1)S(1)}, f32[64,96]{1,0:T(8,128)S(1)}, s32[1]{0:T(128)}) custom-call(bf16[60,16,128]{2,1,0:T(8,128)(2,1)S(1)} %collective-permute-done.11.refs_0_, bf16[175,16,128]{2,1,0:T(8,128)(2,1)S(1)} %collective-permute-done.12.refs_1_, ...), custom_call_target="tpu_custom_call" | custom-call | flops 8099999744 | bytes 1000000 | tf_op jit(solution)/shard_map/late_rows/pallas_call | solution.py:614
  80.2 3.1 %panel_last.1 = f32[72,128]{1,0:T(8,128)S(1)} custom-call(bf16[90,16,128]{2,1,0:T(8,128)(2,1)S(1)} %collective-permute-done.9.refs_0_, bf16[90,16,128]{2,1,0:T(8,128)(2,1)S(1)} %collective-permute-done.10.refs_1_, s32[1]{0:T(128)} %bitcast.12.group_ref.refs_2_, bf16[16,64,1024]{2,1,0:T(8,128)(2,1)S(1)} %get-tuple-element.135.refs_3_, ...), custom_call_target="tpu_custom_call" | custom-call | flops 2700000000 | bytes 1000000 | tf_op jit(solution)/shard_map/panel_last/pallas_call | solution.py:741
  83.4 1.6 %collective-permute-start.24 = (f32[72,128]{1,0:T(8,128)S(1)}, f32[72,128]{1,0:T(8,128)S(1)}, u32[]{:S(2)}, u32[]{:S(2)}) collective-permute-start(f32[72,128]{1,0:T(8,128)S(1)} %panel_last.1), channel_id=1, source_target_pairs={{0,2},{1,3},{2,0},{3,1},{4,6},{5,7},{6,4},{7,5},{8,10},{9,11},{10,... | collective-permute-start | bytes 110600 | tf_op jit(solution)/shard_map/ppermute | solution.py:764
  85.3 2.1 %collective-permute-done.24 = f32[72,128]{1,0:T(8,128)S(1)} collective-permute-done((f32[72,128]{1,0:T(8,128)S(1)}, f32[72,128]{1,0:T(8,128)S(1)}, u32[]{:S(2)}, u32[]{:S(2)}) %collective-permute-start.24) | collective-permute-done | bytes 36896 | tf_op jit(solution)/shard_map/ppermute | solution.py:764
  87.4 1.0 %collective-permute-done.25 = f32[72,128]{1,0:T(8,128)S(1)} collective-permute-done((f32[72,128]{1,0:T(8,128)S(1)}, f32[72,128]{1,0:T(8,128)S(1)}, u32[]{:S(2)}, u32[]{:S(2)}) %collective-permute-start.25) | collective-permute-done | bytes 36896 | tf_op jit(solution)/shard_map/ppermute | solution.py:764
  88.9 0.7 slice_add_fusion
  (51 shorter events, 6.6 us)
Async XLA Ops:
  6.9 27.3 %collective-permute-start.12 = (bf16[175,16,128]{2,1,0:T(8,128)(2,1)S(1)}, bf16[175,16,128]{2,1,0:T(8,128)(2,1)S(1)}, u32[]{:S(2)}, u32[]{:S(2)}) collective-permute-start(bf16[175,16,128]{2,1,0:T(8,128)(2,1)S(1)} %get-tuple-element.123.refs_1_), channel_id=1, source_target_pairs={{0,2},{1,3},{2,0},{3,1},{4,6},{5,7},{6,4},{7,5},{8,10},{9,11},{10,... | collective-permute-start | bytes 2150408 | tf_op jit(solution)/shard_map/ppermute | solution.py:764
  9.9 24.8 %collective-permute-start.21 = (bf16[175,16,128]{2,1,0:T(8,128)(2,1)S(1)}, bf16[175,16,128]{2,1,0:T(8,128)(2,1)S(1)}, u32[]{:S(2)}, u32[]{:S(2)}) collective-permute-start(bf16[175,16,128]{2,1,0:T(8,128)(2,1)S(1)} %get-tuple-element.123.refs_1_), channel_id=1, source_target_pairs={{0,1},{1,0},{2,3},{3,2},{4,5},{5,4},{6,7},{7,6},{8,9},{9,8},{10,11... | collective-permute-start | bytes 2150408 | tf_op jit(solution)/shard_map/ppermute | solution.py:760
  9.9 24.3 %collective-permute-start.22 = (bf16[79,16,128]{2,1,0:T(8,128)(2,1)S(1)}, bf16[79,16,128]{2,1,0:T(8,128)(2,1)S(1)}, u32[]{:S(2)}, u32[]{:S(2)}) collective-permute-start(bf16[79,16,128]{2,1,0:T(8,128)(2,1)S(1)} %get-tuple-element.124.refs_2_), channel_id=1, source_target_pairs={{0,1},{1,0},{2,3},{3,2},{4,5},{5,4},{6,7},{7,6},{8,9},{9,8},{10,11... | collective-permute-start | bytes 970760 | tf_op jit(solution)/shard_map/ppermute | solution.py:760
  10.5 7.4 %copy-start.1 = (s32[64,8]{0,1:T(8,128)S(1)}, s32[64,8]{0,1:T(8,128)}, u32[]{:S(2)}) copy-start(s32[64,8]{0,1:T(8,128)} %param.14) | copy-start | bytes 6148
  10.5 7.4 %copy-start.10 = (s32[128]{0:T(128)S(1)}, s32[128]{0:T(128)}, u32[]{:S(2)}) copy-start(s32[128]{0:T(128)} %index_ref.1) | copy-start | bytes 1540
  10.5 9.8 %collective-permute-start.20 = (bf16[60,16,128]{2,1,0:T(8,128)(2,1)S(1)}, bf16[60,16,128]{2,1,0:T(8,128)(2,1)S(1)}, u32[]{:S(2)}, u32[]{:S(2)}) collective-permute-start(bf16[60,16,128]{2,1,0:T(8,128)(2,1)S(1)} %get-tuple-element.122.refs_0_), channel_id=1, source_target_pairs={{0,1},{1,0},{2,3},{3,2},{4,5},{5,4},{6,7},{7,6},{8,9},{9,8},{10,11... | collective-permute-start | bytes 737288 | tf_op jit(solution)/shard_map/ppermute | solution.py:760
  17.4 17.4 %copy-start.5 = (bf16[1024,1024]{1,0:T(8,128)(2,1)S(1)}, bf16[1024,1024]{1,0:T(8,128)(2,1)}, u32[]{:S(2)}) copy-start(bf16[1024,1024]{1,0:T(8,128)(2,1)} %copy-done.4) | copy-start | bytes 6291460
  17.4 17.4 %copy-start.7 = (bf16[1024,1024]{1,0:T(8,128)(2,1)S(1)}, bf16[1024,1024]{1,0:T(8,128)(2,1)}, u32[]{:S(2)}) copy-start(bf16[1024,1024]{1,0:T(8,128)(2,1)} %copy-done.6) | copy-start | bytes 6291460
  17.4 14.7 %collective-permute-start.11 = (bf16[60,16,128]{2,1,0:T(8,128)(2,1)S(1)}, bf16[60,16,128]{2,1,0:T(8,128)(2,1)S(1)}, u32[]{:S(2)}, u32[]{:S(2)}) collective-permute-start(bf16[60,16,128]{2,1,0:T(8,128)(2,1)S(1)} %get-tuple-element.122.refs_0_), channel_id=1, source_target_pairs={{0,2},{1,3},{2,0},{3,1},{4,6},{5,7},{6,4},{7,5},{8,10},{9,11},{10,... | collective-permute-start | bytes 737288 | tf_op jit(solution)/shard_map/ppermute | solution.py:764
  20.3 21.9 %collective-permute-start.13 = (bf16[79,16,128]{2,1,0:T(8,128)(2,1)S(1)}, bf16[79,16,128]{2,1,0:T(8,128)(2,1)S(1)}, u32[]{:S(2)}, u32[]{:S(2)}) collective-permute-start(bf16[79,16,128]{2,1,0:T(8,128)(2,1)S(1)} %get-tuple-element.124.refs_2_), channel_id=1, source_target_pairs={{0,2},{1,3},{2,0},{3,1},{4,6},{5,7},{6,4},{7,5},{8,10},{9,11},{10,... | collective-permute-start | bytes 970760 | tf_op jit(solution)/shard_map/ppermute | solution.py:764
  32.1 10.7 %collective-permute-start.7 = (bf16[90,16,128]{2,1,0:T(8,128)(2,1)S(1)}, bf16[90,16,128]{2,1,0:T(8,128)(2,1)S(1)}, u32[]{:S(2)}, u32[]{:S(2)}) collective-permute-start(bf16[90,16,128]{2,1,0:T(8,128)(2,1)S(1)} %pack_panel.1.refs_6_), channel_id=1, source_target_pairs={{0,8},{4,12},{8,16},{12,20},{16,24},{20,28},{24,0},{28,4},{1,9},{5... | collective-permute-start | bytes 1105928 | tf_op jit(solution)/shard_map/ppermute | solution.py:764
  34.2 9.6 %collective-permute-start.14 = (bf16[60,16,128]{2,1,0:T(8,128)(2,1)S(1)}, bf16[60,16,128]{2,1,0:T(8,128)(2,1)S(1)}, u32[]{:S(2)}, u32[]{:S(2)}) collective-permute-start(bf16[60,16,128]{2,1,0:T(8,128)(2,1)S(1)} %collective-permute-done.11.refs_0_), channel_id=1, source_target_pairs={{0,1},{1,0},{2,3},{3,2},{4,5},{5,4},{6,7},{7,6},{8,9},{9,8},{10,11... | collective-permute-start | bytes 737288 | tf_op jit(solution)/shard_map/ppermute | solution.py:760
  34.2 21.3 %collective-permute-start.15 = (bf16[175,16,128]{2,1,0:T(8,128)(2,1)S(1)}, bf16[175,16,128]{2,1,0:T(8,128)(2,1)S(1)}, u32[]{:S(2)}, u32[]{:S(2)}) collective-permute-start(bf16[175,16,128]{2,1,0:T(8,128)(2,1)S(1)} %collective-permute-done.12.refs_1_), channel_id=1, source_target_pairs={{0,1},{1,0},{2,3},{3,2},{4,5},{5,4},{6,7},{7,6},{8,9},{9,8},{10,11... | collective-permute-start | bytes 2150408 | tf_op jit(solution)/shard_map/ppermute | solution.py:760
  40.6 27.5 %collective-permute-start.17 = (bf16[90,16,128]{2,1,0:T(8,128)(2,1)S(1)}, bf16[90,16,128]{2,1,0:T(8,128)(2,1)S(1)}, u32[]{:S(2)}, u32[]{:S(2)}) collective-permute-start(bf16[90,16,128]{2,1,0:T(8,128)(2,1)S(1)} %pack_panel.1.refs_6_), channel_id=1, source_target_pairs={{0,4},{4,0},{8,12},{12,8},{16,20},{20,16},{24,28},{28,24},{1,5},{5... | collective-permute-start | bytes 1105928 | tf_op jit(solution)/shard_map/ppermute | solution.py:760
  42.2 25.9 %collective-permute-start.16 = (bf16[79,16,128]{2,1,0:T(8,128)(2,1)S(1)}, bf16[79,16,128]{2,1,0:T(8,128)(2,1)S(1)}, u32[]{:S(2)}, u32[]{:S(2)}) collective-permute-start(bf16[79,16,128]{2,1,0:T(8,128)(2,1)S(1)} %collective-permute-done.13.refs_2_), channel_id=1, source_target_pairs={{0,1},{1,0},{2,3},{3,2},{4,5},{5,4},{6,7},{7,6},{8,9},{9,8},{10,11... | collective-permute-start | bytes 970760 | tf_op jit(solution)/shard_map/ppermute | solution.py:760
  42.8 12.2 %collective-permute-start.8 = (bf16[90,16,128]{2,1,0:T(8,128)(2,1)S(1)}, bf16[90,16,128]{2,1,0:T(8,128)(2,1)S(1)}, u32[]{:S(2)}, u32[]{:S(2)}) collective-permute-start(bf16[90,16,128]{2,1,0:T(8,128)(2,1)S(1)} %collective-permute-done.7.refs_8_), channel_id=1, source_target_pairs={{0,8},{4,12},{8,16},{12,20},{16,24},{20,28},{24,0},{28,4},{1,9},{5... | collective-permute-start | bytes 1105928 | tf_op jit(solution)/shard_map/ppermute | solution.py:764
  50.5 17.5 %collective-permute-start.18 = (bf16[90,16,128]{2,1,0:T(8,128)(2,1)S(1)}, bf16[90,16,128]{2,1,0:T(8,128)(2,1)S(1)}, u32[]{:S(2)}, u32[]{:S(2)}) collective-permute-start(bf16[90,16,128]{2,1,0:T(8,128)(2,1)S(1)} %collective-permute-done.7.refs_8_), channel_id=1, source_target_pairs={{0,4},{4,0},{8,12},{12,8},{16,20},{20,16},{24,28},{28,24},{1,5},{5... | collective-permute-start | bytes 1105928 | tf_op jit(solution)/shard_map/ppermute | solution.py:760
  55.0 15.0 %collective-permute-start.19 = (bf16[90,16,128]{2,1,0:T(8,128)(2,1)S(1)}, bf16[90,16,128]{2,1,0:T(8,128)(2,1)S(1)}, u32[]{:S(2)}, u32[]{:S(2)}) collective-permute-start(bf16[90,16,128]{2,1,0:T(8,128)(2,1)S(1)} %collective-permute-done.8.refs_10_), channel_id=1, source_target_pairs={{0,4},{4,0},{8,12},{12,8},{16,20},{20,16},{24,28},{28,24},{1,5},{5... | collective-permute-start | bytes 1105928 | tf_op jit(solution)/shard_map/ppermute | solution.py:760
  55.5 10.8 %collective-permute-start.9 = (bf16[90,16,128]{2,1,0:T(8,128)(2,1)S(1)}, bf16[90,16,128]{2,1,0:T(8,128)(2,1)S(1)}, u32[]{:S(2)}, u32[]{:S(2)}) collective-permute-start(bf16[90,16,128]{2,1,0:T(8,128)(2,1)S(1)} %collective-permute-done.8.refs_10_), channel_id=1, source_target_pairs={{0,8},{4,12},{8,16},{12,20},{16,24},{20,28},{24,0},{28,4},{1,9},{5... | collective-permute-start | bytes 1105928 | tf_op jit(solution)/shard_map/ppermute | solution.py:764
  66.3 13.8 %collective-permute-start.10 = (bf16[90,16,128]{2,1,0:T(8,128)(2,1)S(1)}, bf16[90,16,128]{2,1,0:T(8,128)(2,1)S(1)}, u32[]{:S(2)}, u32[]{:S(2)}) collective-permute-start(bf16[90,16,128]{2,1,0:T(8,128)(2,1)S(1)} %collective-permute-done.9.refs_0_), channel_id=1, source_target_pairs={{0,4},{4,0},{8,12},{12,8},{16,20},{20,16},{24,28},{28,24},{1,5},{5... | collective-permute-start | bytes 1105928 | tf_op jit(solution)/shard_map/ppermute | solution.py:760
  80.2 8.8 %copy-start.11 = (f32[64]{0:T(128)S(1)}, f32[64]{0:T(128)}, u32[]{:S(2)}) copy-start(f32[64]{0:T(128)} %param.18) | copy-start | bytes 772
  83.3 2.0 %collective-permute-start.23 = (f32[72,128]{1,0:T(8,128)S(1)}, f32[72,128]{1,0:T(8,128)S(1)}, u32[]{:S(2)}, u32[]{:S(2)}) collective-permute-start(f32[72,128]{1,0:T(8,128)S(1)} %panel_last.1), channel_id=1, source_target_pairs={{0,1},{1,0},{2,3},{3,2},{4,5},{5,4},{6,7},{7,6},{8,9},{9,8},{10,11... | collective-permute-start | bytes 110600 | tf_op jit(solution)/shard_map/ppermute | solution.py:764
  83.4 4.0 %collective-permute-start.24 = (f32[72,128]{1,0:T(8,128)S(1)}, f32[72,128]{1,0:T(8,128)S(1)}, u32[]{:S(2)}, u32[]{:S(2)}) collective-permute-start(f32[72,128]{1,0:T(8,128)S(1)} %panel_last.1), channel_id=1, source_target_pairs={{0,2},{1,3},{2,0},{3,1},{4,6},{5,7},{6,4},{7,5},{8,10},{9,11},{10,... | collective-permute-start | bytes 110600 | tf_op jit(solution)/shard_map/ppermute | solution.py:764
  85.0 3.4 %collective-permute-start.25 = (f32[72,128]{1,0:T(8,128)S(1)}, f32[72,128]{1,0:T(8,128)S(1)}, u32[]{:S(2)}, u32[]{:S(2)}) collective-permute-start(f32[72,128]{1,0:T(8,128)S(1)} %panel_last.1), channel_id=1, source_target_pairs={{0,3},{1,2},{2,1},{3,0},{4,7},{5,6},{6,5},{7,4},{8,11},{9,10},{10,... | collective-permute-start | bytes 110600 | tf_op jit(solution)/shard_map/ppermute | solution.py:764
  (6 other events, 11.8 us)

commit v4 on v3

--- a/solution.py
+++ b/solution.py
@@ -45,9 +45,8 @@
 
 
 def chunk_sizes(slots, tiles, extra):
-    most = min(slots - 2, extra + math.ceil(tiles * 3 / 8 + 3.4 * math.sqrt(tiles * 3 / 16)))
-    least = min(extra + tiles // 10, most - 1)
-    return least, most - least, slots - most
+    most = min(slots - 2, extra + math.ceil(tiles / 4 + 3 * math.sqrt(tiles / 8)))
+    return most, slots - most
 
 
 def pack_rows(mask_at, feet_at, begin, end, blocks, buf, carry):
@@ -175,7 +174,7 @@
     )(mask, coords, sigma, feet)
 
 
-def pack_panel_kernel(room, mask_ref, mask_hbm, index_ref, group_ref, feet_ref, out_ref, mask_v, rows_buf, head_v, small_sem, sem):
+def pack_panel_kernel(room, mask_ref, mask_hbm, index_ref, group_ref, member_ref, feet_ref, out_ref, mask_v, rows_buf, head_v, small_sem, sem):
     count = rows_buf.shape[0]
     blocks, obs = mask_ref.shape
     lanes = out_ref.shape[2]
@@ -200,13 +199,13 @@
     write_head(carry, count, blocks, out_ref, head_v, flag)
 
 
-def pack_panel(mask, panel_index, group, feet, count, slots, room):
+def pack_panel(mask, panel_index, group, member, feet, count, slots, room):
     _, times, cells = feet.shape
     lanes = cells // mask.shape[0]
     return pl.pallas_call(
         functools.partial(pack_panel_kernel, room),
         out_shape=shape_of((slots, times, lanes), BF16),
-        in_specs=[SMEM, HBM, SMEM, SMEM, HBM],
+        in_specs=[SMEM, HBM, SMEM, SMEM, SMEM, HBM],
         out_specs=VMEM,
         scratch_shapes=[
             pltpu.VMEM(mask.shape, I32),
@@ -218,7 +217,7 @@
         compiler_params=params(8),
         cost_estimate=cost(2),
         name="pack_panel",
-    )(mask, mask, panel_index, group[None], feet)
+    )(mask, mask, panel_index, group[None], member[None], feet)
 
 
 def fetch(chunks, buf, sem):
@@ -700,7 +699,7 @@
 
 def last_kernel(pieces, each, *refs):
     msgs = refs[:pieces]
-    group_ref, turned, before_ref, over_ref, out_ref, bufs, bits_v, bits_s, panel, sem = refs[pieces:]
+    group_ref, member_ref, index_ref, var_ref, turned, before_ref, over_ref, out_ref, bufs, bits_v, bits_s, panel, sem = refs[pieces:]
     _, lanes = bufs.shape[2:]
     rows, cells = turned.shape[1:]
     copies = [pltpu.make_async_copy(msg, bufs.at[k], sem.at[k]) for k, msg in enumerate(msgs)]
@@ -721,11 +720,14 @@
         source = jnp.where(back < 0, back + half, back) * 2 + lax.bitwise_xor(lo, k % 2)
         target = jnp.where((row >= k * each) & (row < (k + 1) * each), row + (source - k) * each, target)
     select = (lax.broadcasted_iota(I32, (size, size), 1) == target).astype(F32).astype(BF16)
+    spot = lax.broadcasted_iota(I32, (rows, size), 0) + group_ref[0] * rows
+    variance = jnp.broadcast_to(var_ref[...], (8, rows)).T[:, 0:1]
+    diagonal = jnp.where((spot == index_ref[...]) & (member_ref[0] == 0), variance, 0.0)
     bits_copy.wait()
     over = over_ref[0] + panel_over(bufs, bits_s, 0, pieces, each)
     total = panel_products(bufs, bits_s, 0, pieces, each, turned, panel)
     value = jnp.concatenate([before_ref[...], total], axis=1)
-    total = jnp.zeros(value.shape, F32)
+    total = diagonal
     for _ in range(3):
         high = value.astype(BF16)
         total = total + jnp.dot(high, select, preferred_element_type=F32)
@@ -734,14 +736,14 @@
     out_ref[rows:, :] = jnp.broadcast_to(over, (8, size)).astype(F32)
 
 
-def panel_last(msgs, turned, each, group, before, over):
+def panel_last(msgs, turned, each, group, member, panel_index, error_var, before, over):
     slots, times, lanes = msgs[0].shape
     rows, cells = turned.shape[1:]
     pieces = len(msgs)
     return pl.pallas_call(
         functools.partial(last_kernel, pieces, each),
         out_shape=shape_of((rows + 8, before.shape[1] + pieces * each), F32),
-        in_specs=[ANY] * pieces + [SMEM, VMEM, VMEM, SMEM],
+        in_specs=[ANY] * pieces + [SMEM, SMEM, VMEM, VMEM, VMEM, VMEM, SMEM],
         out_specs=VMEM,
         scratch_shapes=[
             pltpu.VMEM((pieces, slots, times, lanes), BF16),
@@ -753,7 +755,7 @@
         compiler_params=params(14),
         cost_estimate=cost(3),
         name="panel_last",
-    )(*msgs, group[None], turned, before, over)
+    )(*msgs, group[None], member[None], panel_index[None, :], error_var[None, :], turned, before, over)
 
 
 def partner(value, axis, count):
@@ -819,13 +821,14 @@
     group = lax.axis_index("obs")
     each = panel_index.shape[0] // observers
     half = observers // 2
+    member = lax.axis_index("cell")
     unit = math.gcd(16, obs_rows)
     slots = slot_count(obs_rows * blocks, 1 + blocks)
     chunks = chunk_sizes(slots, obs_rows * blocks, 1 + blocks)
     mask = block_mask.T
 
     room = slots - 2 - blocks - 1
-    own_panel = pack_panel(mask, panel_index, group, footprint, each, slot_count(each * blocks, 1), room)
+    own_panel = pack_panel(mask, panel_index, group, member, footprint, each, slot_count(each * blocks, 1), room)
     ring = [own_panel]
     for _ in range(1, half):
         ring.append(shifted(ring[-1], "obs", observers, 1))
@@ -849,12 +852,7 @@
     cov_product, turned, before, over = late_rows(
         far_msgs, messages[:cut], each, far_cov, near, mix, start, first_cov, unit, slots
     )
-    part = panel_last(messages[cut:], turned, each, group, before, over)
-
-    def innovation_of(total, group):
-        positions = jnp.arange(obs_rows, dtype=I32)
-        on_diagonal = ((group * obs_rows + positions)[:, None] == panel_index[None, :]).astype(F32)
-        return total + error_var[:, None] * on_diagonal
+    part = panel_last(messages[cut:], turned, each, group, member, panel_index, error_var, before, over)
 
     part, late_group, late_mask = lax.optimization_barrier((part, group, mask))
     total = add_cells(part, cells)
@@ -868,9 +866,11 @@
         cov_product, total = dense_way(
             cells, observers, footprint, kept.T, cell_info, time_cov, mine, from_group
         )
-        return jnp.bool_(False), cov_product, row_major(innovation_of(total, place))
-
-    carry = (total[obs_rows, 0] > 0, cov_product, row_major(innovation_of(total[:obs_rows], late_group)))
+        positions = jnp.arange(obs_rows, dtype=I32) + place * obs_rows
+        on_diagonal = (positions[:, None] == panel_index[None, :]).astype(F32)
+        return jnp.bool_(False), cov_product, row_major(total + error_var[:, None] * on_diagonal)
+
+    carry = (total[obs_rows, 0] > 0, cov_product, row_major(total[:obs_rows]))
     return lax.while_loop(lambda carry: carry[0], again, carry)[1:]
 
 

time: 90.9 us -> 87.2 us (0.959)
  local copies, waits for them, and re-layouts: 5.34 us -> 3.36 us
  waiting for transfers between devices: 22.4 us -> 24.1 us
  starting transfers between devices: 15.5 us -> 13.8 us
  Pallas kernels: 44.8 us -> 43.6 us
    ppermute x9 -> x8, waiting for transfers between devices: 20.5 us -> 24.1 us  [shifted(): lax.ppermute(value, axis, [(i, (i + 2 * shift) % count ^ flip) for i in r...]
    unnamed x22 -> x14, local copies, waits for them, and re-layouts: 4.74 us -> 2.08 us
    pallas_call x1, Pallas kernels: 7.89 us -> 5.39 us  [first_rows(): pl.pallas_call(functools.partial(first_kernel, count, chunks, unit), out_...]
    ppermute x10 -> x8, waiting for transfers between devices: 1.93 us -> 0.02 us  [partner(): return lax.ppermute(value, axis, [(i, i ^ 1) for i in range(count)])]
    ppermute x9 -> x8, starting transfers between devices: 9.95 us -> 8.75 us  [shifted(): lax.ppermute(value, axis, [(i, (i + 2 * shift) % count ^ flip) for i in r...]
    pallas_call x1, Pallas kernels: 10.2 us -> 11.1 us  [late_rows(): pl.pallas_call(functools.partial(late_kernel, count, chunks, unit, pieces...]
    ppermute x10 -> x8, starting transfers between devices: 5.55 us -> 5.01 us  [partner(): return lax.ppermute(value, axis, [(i, i ^ 1) for i in range(count)])]
  transfers between devices with their start and end apart: 19 -> 16, of which waited for: 7 -> 5; matrix products, arithmetic and copies ran while one was open for 0% -> 0% of each run, Pallas kernels for 41% -> 42%
where the time goes in v4:
time: 87.2 us; the launch traced here: 86.7 us
  Pallas kernels  43.6 us (50%)
  waiting for transfers between devices  24.1 us (28%)
  starting transfers between devices  13.8 us (16%)
  local copies, waits for them, and re-layouts  3.36 us (4%)
  between operations  1.66 us (2%)
    ppermute x8, waiting for transfers between devices, shifted(): lax.ppermute(value, axis, [(i, (i + 2 * shift) % count ^ flip) for i in r...  24.1 us
    pallas_call x1, Pallas kernels, late_rows(): pl.pallas_call(functools.partial(late_kernel, count, chunks, unit, pieces...  11.1 us
    ppermute x8, starting transfers between devices, shifted(): lax.ppermute(value, axis, [(i, (i + 2 * shift) % count ^ flip) for i in r...  8.75 us
    pallas_call x1, Pallas kernels, mate_call(): pl.pallas_call(functools.partial(mate_kernel, count), out_shape=(shape_of...  6.68 us
    pallas_call x1, Pallas kernels, own_call(): pl.pallas_call(functools.partial(own_kernel, chunks), out_shape=(shape_of...  6.4 us
    pallas_call x1, Pallas kernels, first_rows(): pl.pallas_call(functools.partial(first_kernel, count, chunks, unit), out_...  5.39 us
    ppermute x8, starting transfers between devices, partner(): return lax.ppermute(value, axis, [(i, i ^ 1) for i in range(count)])  5.01 us
    pallas_call x1, Pallas kernels, start_call(): pl.pallas_call(functools.partial(start_kernel, chunks), out_shape=(shape_...  3.88 us
  transfers between devices with their start and end apart: 16, of which 5 were waited for; matrix products, arithmetic and copies ran while one was open for 0% of the time, Pallas kernels for 42%

profile of v4, /device:TPU:0, one launch (start us, length us, event | category | flops | bytes accessed | tf_op | source)
XLA Modules:
  0.0 86.7 jit_solution(17684397326890439538)
XLA Ops:
  0.6 0.7 copy-done
  1.3 0.7 copy-done.2
  2.0 0.7 copy-done.3
  2.7 3.8 %pack_feet.1 = (bf16[161,16,128]{2,1,0:T(8,128)(2,1)S(1)}, bf16[153,16,128]{2,1,0:T(8,128)(2,1)S(1)}) custom-call(s32[8,64]{1,0:T(8,128)S(1)} %bitcast.77, s32[2,1024]{1,0:T(2,128)S(1)} %copy-done.2, f32[1,1024]{1,0:T(1,128)S(1)} %bitcast.81, bf16[64,16,1024]{2,1,0:T(8,128)(2,1)} %feet_ref.3), custom_call_target="tpu_custom_call" | custom-call | flops 2700000000 | bytes 1000000 | tf_op jit(solution)/shard_map/pack_feet/pallas_call | solution.py:156
  6.5 3.0 %collective-permute-start.11 = (bf16[161,16,128]{2,1,0:T(8,128)(2,1)S(1)}, bf16[161,16,128]{2,1,0:T(8,128)(2,1)S(1)}, u32[]{:S(2)}, u32[]{:S(2)}) collective-permute-start(bf16[161,16,128]{2,1,0:T(8,128)(2,1)S(1)} %get-tuple-element.121.refs_0_), channel_id=1, source_target_pairs={{0,2},{1,3},{2,0},{3,1},{4,6},{5,7},{6,4},{7,5},{8,10},{9,11},{10,... | collective-permute-start | bytes 1978376 | tf_op jit(solution)/shard_map/ppermute | solution.py:766
  10.2 2.2 %pack_panel.1.refs_4_ = bf16[90,16,128]{2,1,0:T(8,128)(2,1)S(1)} custom-call(s32[8,64]{1,0:T(8,128)S(1)} %bitcast.78, s32[8,64]{1,0:T(8,128)S(1)} %bitcast.79, s32[128]{0:T(128)S(1)} %copy-done.7, s32[1]{0:T(128)} %bitcast.12.group_ref.refs_2_, s32[1]{0:T(128)} %bitcast.13.member_ref.refs_3_, bf16[64,16,1024]{2,1,0:T(8,128)(2,1)} %feet_ref.3), custom_call_target="tpu_custom_call" | custom-call | flops 1800000000 | bytes 1000000 | tf_op jit(solution)/shard_map/pack_panel/pallas_call | solution.py:205
  12.4 2.1 %collective-permute-start.7 = (bf16[90,16,128]{2,1,0:T(8,128)(2,1)S(1)}, bf16[90,16,128]{2,1,0:T(8,128)(2,1)S(1)}, u32[]{:S(2)}, u32[]{:S(2)}) collective-permute-start(bf16[90,16,128]{2,1,0:T(8,128)(2,1)S(1)} %pack_panel.1.refs_4_), channel_id=1, source_target_pairs={{0,8},{4,12},{8,16},{12,20},{16,24},{20,28},{24,0},{28,4},{1,9},{5... | collective-permute-start | bytes 1105928 | tf_op jit(solution)/shard_map/ppermute | solution.py:766
  14.5 10.8 %collective-permute-done.11.refs_0_ = bf16[161,16,128]{2,1,0:T(8,128)(2,1)S(1)} collective-permute-done((bf16[161,16,128]{2,1,0:T(8,128)(2,1)S(1)}, bf16[161,16,128]{2,1,0:T(8,128)(2,1)S(1)}, u32[]{:S(2)}, u32[]{:S(2)}) %collective-permute-start.11) | collective-permute-done | bytes 659488 | tf_op jit(solution)/shard_map/ppermute | solution.py:766
  25.2 3.9 %own_start.1 = (bf16[1024,1024]{1,0:T(8,128)(2,1)S(1)}, bf16[1024,1024]{1,0:T(8,128)(2,1)S(1)}, f32[8,1024]{1,0:T(8,128)S(1)}) custom-call(bf16[161,16,128]{2,1,0:T(8,128)(2,1)S(1)} %get-tuple-element.121.refs_0_, bf16[153,16,128]{2,1,0:T(8,128)(2,1)S(1)} %get-tuple-element.122.refs_1_), custom_call_target="tpu_custom_call" | custom-call | flops 3600000000 | bytes 1000000 | tf_op jit(solution)/shard_map/own_start/pallas_call | solution.py:345
  29.5 2.1 %collective-permute-start.15 = (bf16[90,16,128]{2,1,0:T(8,128)(2,1)S(1)}, bf16[90,16,128]{2,1,0:T(8,128)(2,1)S(1)}, u32[]{:S(2)}, u32[]{:S(2)}) collective-permute-start(bf16[90,16,128]{2,1,0:T(8,128)(2,1)S(1)} %pack_panel.1.refs_4_), channel_id=1, source_target_pairs={{0,4},{4,0},{8,12},{12,8},{16,20},{20,16},{24,28},{28,24},{1,5},{5... | collective-permute-start | bytes 1105928 | tf_op jit(solution)/shard_map/ppermute | solution.py:762
  31.6 1.6 %collective-permute-start.8 = (bf16[90,16,128]{2,1,0:T(8,128)(2,1)S(1)}, bf16[90,16,128]{2,1,0:T(8,128)(2,1)S(1)}, u32[]{:S(2)}, u32[]{:S(2)}) collective-permute-start(bf16[90,16,128]{2,1,0:T(8,128)(2,1)S(1)} %collective-permute-done.7.refs_6_), channel_id=1, source_target_pairs={{0,8},{4,12},{8,16},{12,20},{16,24},{20,28},{24,0},{28,4},{1,9},{5... | collective-permute-start | bytes 1105928 | tf_op jit(solution)/shard_map/ppermute | solution.py:766
  33.2 6.4 %own_product.1 = (f32[1024,1024]{1,0:T(8,128)S(1)}, bf16[1024,1024]{1,0:T(8,128)(2,1)S(1)}, bf16[1024,1024]{1,0:T(8,128)(2,1)S(1)}) custom-call(bf16[161,16,128]{2,1,0:T(8,128)(2,1)S(1)} %collective-permute-done.18.refs_0_, bf16[153,16,128]{2,1,0:T(8,128)(2,1)} %collective-permute-done.19.refs_1_, bf16[1024,1024]{1,0:T(8,128)(2,1)S(1)} %get-tuple-element.123.refs_2_, ...), custom_call_target="tpu_custom_call" | custom-call | flops 5400000000 | bytes 1000000 | tf_op jit(solution)/shard_map/own_product/pallas_call | solution.py:397
  40.2 4.0 %collective-permute-done.8.refs_8_ = bf16[90,16,128]{2,1,0:T(8,128)(2,1)S(1)} collective-permute-done((bf16[90,16,128]{2,1,0:T(8,128)(2,1)S(1)}, bf16[90,16,128]{2,1,0:T(8,128)(2,1)S(1)}, u32[]{:S(2)}, u32[]{:S(2)}) %collective-permute-start.8) | collective-permute-done | bytes 368672 | tf_op jit(solution)/shard_map/ppermute | solution.py:766
  44.7 6.7 %mate_product.1 = (f32[1024,1024]{1,0:T(8,128)S(1)}, bf16[2048,1024]{1,0:T(8,128)(2,1)S(1)}) custom-call(bf16[161,16,128]{2,1,0:T(8,128)(2,1)S(1)} %collective-permute-done.11.refs_0_, bf16[161,16,128]{2,1,0:T(8,128)(2,1)S(1)} %collective-permute-done.13.refs_1_.refs_2_, ...), custom_call_target="tpu_custom_call", output_to_operand_aliasing={{0}: (2, {})} | custom-call | flops 7200000000 | bytes 1000000 | tf_op jit(solution)/shard_map/mate_product/pallas_call | solution.py:444
  51.4 5.4 %first_rows.1 = (bf16[64,16,1024]{2,1,0:T(8,128)(2,1)S(1)}, s32[1]{0:T(128)}) custom-call(bf16[161,16,128]{2,1,0:T(8,128)(2,1)S(1)} %collective-permute-done.11.refs_0_, bf16[161,16,128]{2,1,0:T(8,128)(2,1)S(1)} %collective-permute-done.13.refs_1_.refs_2_, bf16[2048,1024]{1,0:T(8,128)(2,1)S(1)} %get-tuple-element.129.refs_2_.refs_10_, ...), custom_call_target="tpu_custom_call" | custom-call | flops 6300000256 | bytes 1000000 | tf_op jit(solution)/shard_map/first_rows/pallas_call | solution.py:538
  56.8 6.3 %collective-permute-done.9.refs_0_ = bf16[90,16,128]{2,1,0:T(8,128)(2,1)S(1)} collective-permute-done((bf16[90,16,128]{2,1,0:T(8,128)(2,1)S(1)}, bf16[90,16,128]{2,1,0:T(8,128)(2,1)S(1)}, u32[]{:S(2)}, u32[]{:S(2)}) %collective-permute-start.9) | collective-permute-done | bytes 368672 | tf_op jit(solution)/shard_map/ppermute | solution.py:766
  63.1 1.3 %collective-permute-start.10 = (bf16[90,16,128]{2,1,0:T(8,128)(2,1)S(1)}, bf16[90,16,128]{2,1,0:T(8,128)(2,1)S(1)}, u32[]{:S(2)}, u32[]{:S(2)}) collective-permute-start(bf16[90,16,128]{2,1,0:T(8,128)(2,1)S(1)} %collective-permute-done.9.refs_0_), channel_id=1, source_target_pairs={{0,4},{4,0},{8,12},{12,8},{16,20},{20,16},{24,28},{28,24},{1,5},{5... | collective-permute-start | bytes 1105928 | tf_op jit(solution)/shard_map/ppermute | solution.py:762
  64.4 11.1 %late_rows.1 = (bf16[64,16,1024]{2,1,0:T(8,128)(2,1)}, bf16[16,64,1024]{2,1,0:T(8,128)(2,1)S(1)}, f32[64,96]{1,0:T(8,128)S(1)}, s32[1]{0:T(128)}) custom-call(bf16[161,16,128]{2,1,0:T(8,128)(2,1)S(1)} %collective-permute-done.11.refs_0_, bf16[153,16,128]{2,1,0:T(8,128)(2,1)S(1)} %collective-permute-done.12.refs_1_, ...), custom_call_target="tpu_custom_call" | custom-call | flops 8099999744 | bytes 1000000 | tf_op jit(solution)/shard_map/late_rows/pallas_call | solution.py:613
  75.6 3.8 %panel_last.1 = f32[72,128]{1,0:T(8,128)S(1)} custom-call(bf16[90,16,128]{2,1,0:T(8,128)(2,1)S(1)} %collective-permute-done.9.refs_0_, bf16[90,16,128]{2,1,0:T(8,128)(2,1)S(1)} %collective-permute-done.10.refs_1_, s32[1]{0:T(128)} %bitcast.12.group_ref.refs_2_, s32[1]{0:T(128)} %bitcast.13.member_ref.refs_3_, s32[1,128]{1,0:T(1,128)S(1)} %bitcast.98, ...), custom_call_target="tpu_custom_call" | custom-call | flops 2700000000 | bytes 1000000 | tf_op jit(solution)/shard_map/panel_last/pallas_call | solution.py:743
  79.5 1.5 %collective-permute-start.21 = (f32[72,128]{1,0:T(8,128)S(1)}, f32[72,128]{1,0:T(8,128)S(1)}, u32[]{:S(2)}, u32[]{:S(2)}) collective-permute-start(f32[72,128]{1,0:T(8,128)S(1)} %panel_last.1), channel_id=1, source_target_pairs={{0,2},{1,3},{2,0},{3,1},{4,6},{5,7},{6,4},{7,5},{8,10},{9,11},{10,... | collective-permute-start | bytes 110600 | tf_op jit(solution)/shard_map/ppermute | solution.py:766
  81.4 2.1 %collective-permute-done.21 = f32[72,128]{1,0:T(8,128)S(1)} collective-permute-done((f32[72,128]{1,0:T(8,128)S(1)}, f32[72,128]{1,0:T(8,128)S(1)}, u32[]{:S(2)}, u32[]{:S(2)}) %collective-permute-start.21) | collective-permute-done | bytes 36896 | tf_op jit(solution)/shard_map/ppermute | solution.py:766
  83.5 0.9 %collective-permute-done.22 = f32[72,128]{1,0:T(8,128)S(1)} collective-permute-done((f32[72,128]{1,0:T(8,128)S(1)}, f32[72,128]{1,0:T(8,128)S(1)}, u32[]{:S(2)}, u32[]{:S(2)}) %collective-permute-start.22) | collective-permute-done | bytes 36896 | tf_op jit(solution)/shard_map/ppermute | solution.py:766
  84.5 0.6 slice.35
  85.1 0.6 slice.34
  (36 shorter events, 2.8 us)
Async XLA Ops:
  0.6 0.7 copy-start
  1.3 0.7 copy-start.2
  2.0 0.7 copy-start.3
  2.7 7.4 %copy-start.1 = (s32[64,8]{0,1:T(8,128)S(1)}, s32[64,8]{0,1:T(8,128)}, u32[]{:S(2)}) copy-start(s32[64,8]{0,1:T(8,128)} %param.14) | copy-start | bytes 6148
  2.7 7.4 %copy-start.7 = (s32[128]{0:T(128)S(1)}, s32[128]{0:T(128)}, u32[]{:S(2)}) copy-start(s32[128]{0:T(128)} %index_ref.1) | copy-start | bytes 1540
  6.5 18.7 %collective-permute-start.11 = (bf16[161,16,128]{2,1,0:T(8,128)(2,1)S(1)}, bf16[161,16,128]{2,1,0:T(8,128)(2,1)S(1)}, u32[]{:S(2)}, u32[]{:S(2)}) collective-permute-start(bf16[161,16,128]{2,1,0:T(8,128)(2,1)S(1)} %get-tuple-element.121.refs_0_), channel_id=1, source_target_pairs={{0,2},{1,3},{2,0},{3,1},{4,6},{5,7},{6,4},{7,5},{8,10},{9,11},{10,... | collective-permute-start | bytes 1978376 | tf_op jit(solution)/shard_map/ppermute | solution.py:766
  9.6 23.6 %collective-permute-start.18 = (bf16[161,16,128]{2,1,0:T(8,128)(2,1)S(1)}, bf16[161,16,128]{2,1,0:T(8,128)(2,1)S(1)}, u32[]{:S(2)}, u32[]{:S(2)}) collective-permute-start(bf16[161,16,128]{2,1,0:T(8,128)(2,1)S(1)} %get-tuple-element.121.refs_0_), channel_id=1, source_target_pairs={{0,1},{1,0},{2,3},{3,2},{4,5},{5,4},{6,7},{7,6},{8,9},{9,8},{10,11... | collective-permute-start | bytes 1978376 | tf_op jit(solution)/shard_map/ppermute | solution.py:762
  9.6 22.0 %collective-permute-start.19 = (bf16[153,16,128]{2,1,0:T(8,128)(2,1)S(1)}, bf16[153,16,128]{2,1,0:T(8,128)(2,1)}, u32[]{:S(2)}, u32[]{:S(2)}) collective-permute-start(bf16[153,16,128]{2,1,0:T(8,128)(2,1)S(1)} %get-tuple-element.122.refs_1_), channel_id=1, source_target_pairs={{0,1},{1,0},{2,3},{3,2},{4,5},{5,4},{6,7},{7,6},{8,9},{9,8},{10,11... | collective-permute-start | bytes 1880072 | tf_op jit(solution)/shard_map/ppermute | solution.py:762
  10.1 30.1 %collective-permute-start.12 = (bf16[153,16,128]{2,1,0:T(8,128)(2,1)S(1)}, bf16[153,16,128]{2,1,0:T(8,128)(2,1)S(1)}, u32[]{:S(2)}, u32[]{:S(2)}) collective-permute-start(bf16[153,16,128]{2,1,0:T(8,128)(2,1)S(1)} %get-tuple-element.122.refs_1_), channel_id=1, source_target_pairs={{0,2},{1,3},{2,0},{3,1},{4,6},{5,7},{6,4},{7,5},{8,10},{9,11},{10,... | collective-permute-start | bytes 1880072 | tf_op jit(solution)/shard_map/ppermute | solution.py:766
  12.4 16.8 %copy-start.5 = (f32[16,16]{1,0:T(8,128)S(1)}, f32[16,16]{1,0:T(8,128)}, u32[]{:S(2)}) copy-start(f32[16,16]{1,0:T(8,128)} %time_ref.1) | copy-start | bytes 3076
  12.4 17.1 %collective-permute-start.7 = (bf16[90,16,128]{2,1,0:T(8,128)(2,1)S(1)}, bf16[90,16,128]{2,1,0:T(8,128)(2,1)S(1)}, u32[]{:S(2)}, u32[]{:S(2)}) collective-permute-start(bf16[90,16,128]{2,1,0:T(8,128)(2,1)S(1)} %pack_panel.1.refs_4_), channel_id=1, source_target_pairs={{0,8},{4,12},{8,16},{12,20},{16,24},{20,28},{24,0},{28,4},{1,9},{5... | collective-permute-start | bytes 1105928 | tf_op jit(solution)/shard_map/ppermute | solution.py:766
  25.2 19.4 %collective-permute-start.13 = (bf16[161,16,128]{2,1,0:T(8,128)(2,1)S(1)}, bf16[161,16,128]{2,1,0:T(8,128)(2,1)S(1)}, u32[]{:S(2)}, u32[]{:S(2)}) collective-permute-start(bf16[161,16,128]{2,1,0:T(8,128)(2,1)S(1)} %collective-permute-done.11.refs_0_), channel_id=1, source_target_pairs={{0,1},{1,0},{2,3},{3,2},{4,5},{5,4},{6,7},{7,6},{8,9},{9,8},{10,11... | collective-permute-start | bytes 1978376 | tf_op jit(solution)/shard_map/ppermute | solution.py:762
  29.5 34.9 %collective-permute-start.15 = (bf16[90,16,128]{2,1,0:T(8,128)(2,1)S(1)}, bf16[90,16,128]{2,1,0:T(8,128)(2,1)S(1)}, u32[]{:S(2)}, u32[]{:S(2)}) collective-permute-start(bf16[90,16,128]{2,1,0:T(8,128)(2,1)S(1)} %pack_panel.1.refs_4_), channel_id=1, source_target_pairs={{0,4},{4,0},{8,12},{12,8},{16,20},{20,16},{24,28},{28,24},{1,5},{5... | collective-permute-start | bytes 1105928 | tf_op jit(solution)/shard_map/ppermute | solution.py:762
  31.6 12.6 %collective-permute-start.8 = (bf16[90,16,128]{2,1,0:T(8,128)(2,1)S(1)}, bf16[90,16,128]{2,1,0:T(8,128)(2,1)S(1)}, u32[]{:S(2)}, u32[]{:S(2)}) collective-permute-start(bf16[90,16,128]{2,1,0:T(8,128)(2,1)S(1)} %collective-permute-done.7.refs_6_), channel_id=1, source_target_pairs={{0,8},{4,12},{8,16},{12,20},{16,24},{20,28},{24,0},{28,4},{1,9},{5... | collective-permute-start | bytes 1105928 | tf_op jit(solution)/shard_map/ppermute | solution.py:766
  39.6 24.8 %collective-permute-start.16 = (bf16[90,16,128]{2,1,0:T(8,128)(2,1)S(1)}, bf16[90,16,128]{2,1,0:T(8,128)(2,1)S(1)}, u32[]{:S(2)}, u32[]{:S(2)}) collective-permute-start(bf16[90,16,128]{2,1,0:T(8,128)(2,1)S(1)} %collective-permute-done.7.refs_6_), channel_id=1, source_target_pairs={{0,4},{4,0},{8,12},{12,8},{16,20},{20,16},{24,28},{28,24},{1,5},{5... | collective-permute-start | bytes 1105928 | tf_op jit(solution)/shard_map/ppermute | solution.py:762
  40.2 24.2 %collective-permute-start.14 = (bf16[153,16,128]{2,1,0:T(8,128)(2,1)S(1)}, bf16[153,16,128]{2,1,0:T(8,128)(2,1)S(1)}, u32[]{:S(2)}, u32[]{:S(2)}) collective-permute-start(bf16[153,16,128]{2,1,0:T(8,128)(2,1)S(1)} %collective-permute-done.12.refs_1_), channel_id=1, source_target_pairs={{0,1},{1,0},{2,3},{3,2},{4,5},{5,4},{6,7},{7,6},{8,9},{9,8},{10,11... | collective-permute-start | bytes 1880072 | tf_op jit(solution)/shard_map/ppermute | solution.py:762
  44.2 20.2 %collective-permute-start.17 = (bf16[90,16,128]{2,1,0:T(8,128)(2,1)S(1)}, bf16[90,16,128]{2,1,0:T(8,128)(2,1)S(1)}, u32[]{:S(2)}, u32[]{:S(2)}) collective-permute-start(bf16[90,16,128]{2,1,0:T(8,128)(2,1)S(1)} %collective-permute-done.8.refs_8_), channel_id=1, source_target_pairs={{0,4},{4,0},{8,12},{12,8},{16,20},{20,16},{24,28},{28,24},{1,5},{5... | collective-permute-start | bytes 1105928 | tf_op jit(solution)/shard_map/ppermute | solution.py:762
  51.4 11.7 %collective-permute-start.9 = (bf16[90,16,128]{2,1,0:T(8,128)(2,1)S(1)}, bf16[90,16,128]{2,1,0:T(8,128)(2,1)S(1)}, u32[]{:S(2)}, u32[]{:S(2)}) collective-permute-start(bf16[90,16,128]{2,1,0:T(8,128)(2,1)S(1)} %collective-permute-done.8.refs_8_), channel_id=1, source_target_pairs={{0,8},{4,12},{8,16},{12,20},{16,24},{20,28},{24,0},{28,4},{1,9},{5... | collective-permute-start | bytes 1105928 | tf_op jit(solution)/shard_map/ppermute | solution.py:766
  63.1 12.5 %collective-permute-start.10 = (bf16[90,16,128]{2,1,0:T(8,128)(2,1)S(1)}, bf16[90,16,128]{2,1,0:T(8,128)(2,1)S(1)}, u32[]{:S(2)}, u32[]{:S(2)}) collective-permute-start(bf16[90,16,128]{2,1,0:T(8,128)(2,1)S(1)} %collective-permute-done.9.refs_0_), channel_id=1, source_target_pairs={{0,4},{4,0},{8,12},{12,8},{16,20},{20,16},{24,28},{28,24},{1,5},{5... | collective-permute-start | bytes 1105928 | tf_op jit(solution)/shard_map/ppermute | solution.py:762
  75.5 10.8 %copy-start.6 = (f32[16,16]{1,0:T(8,128)S(1)}, f32[16,16]{1,0:T(8,128)}, u32[]{:S(2)}) copy-start(f32[16,16]{1,0:T(8,128)} %time_ref.1) | copy-start | bytes 3076
  79.4 2.0 %collective-permute-start.20 = (f32[72,128]{1,0:T(8,128)S(1)}, f32[72,128]{1,0:T(8,128)S(1)}, u32[]{:S(2)}, u32[]{:S(2)}) collective-permute-start(f32[72,128]{1,0:T(8,128)S(1)} %panel_last.1), channel_id=1, source_target_pairs={{0,1},{1,0},{2,3},{3,2},{4,5},{5,4},{6,7},{7,6},{8,9},{9,8},{10,11... | collective-permute-start | bytes 110600 | tf_op jit(solution)/shard_map/ppermute | solution.py:766
  79.5 4.0 %collective-permute-start.21 = (f32[72,128]{1,0:T(8,128)S(1)}, f32[72,128]{1,0:T(8,128)S(1)}, u32[]{:S(2)}, u32[]{:S(2)}) collective-permute-start(f32[72,128]{1,0:T(8,128)S(1)} %panel_last.1), channel_id=1, source_target_pairs={{0,2},{1,3},{2,0},{3,1},{4,6},{5,7},{6,4},{7,5},{8,10},{9,11},{10,... | collective-permute-start | bytes 110600 | tf_op jit(solution)/shard_map/ppermute | solution.py:766
  81.0 3.4 %collective-permute-start.22 = (f32[72,128]{1,0:T(8,128)S(1)}, f32[72,128]{1,0:T(8,128)S(1)}, u32[]{:S(2)}, u32[]{:S(2)}) collective-permute-start(f32[72,128]{1,0:T(8,128)S(1)} %panel_last.1), channel_id=1, source_target_pairs={{0,3},{1,2},{2,1},{3,0},{4,7},{5,6},{6,5},{7,4},{8,11},{9,10},{10,... | collective-permute-start | bytes 110600 | tf_op jit(solution)/shard_map/ppermute | solution.py:766

commit v5 on v4

--- a/solution.py
+++ b/solution.py
@@ -40,13 +40,13 @@
 
 
 def slot_count(tiles, extra):
-    room = tiles / 2 + 4.1 * math.sqrt(tiles / 4)
+    room = tiles / 2 + 4.0 * math.sqrt(tiles / 4)
     return extra + min(tiles + 1, 2 * math.ceil(room / 2) + 1)
 
 
 def chunk_sizes(slots, tiles, extra):
     most = min(slots - 2, extra + math.ceil(tiles / 4 + 3 * math.sqrt(tiles / 8)))
-    return most, slots - most
+    return extra, most - extra, slots - most
 
 
 def pack_rows(mask_at, feet_at, begin, end, blocks, buf, carry):
@@ -303,7 +303,7 @@
         dx = turned[at, 0:1] - x
         dy = turned[at, 1:2] - y
         square = dx * dx + dy * dy + 1.0
-        decay = jnp.exp(square * lax.rsqrt(square) * (-1.0 / LENGTH))
+        decay = jnp.exp2(square * lax.rsqrt(square) * (-math.log2(math.e) / LENGTH))
         dst[aligned(dst_first + i * step, step), :] = (decay * (turned[at, 2:3] * s)).astype(BF16)
 
 
@@ -412,22 +412,62 @@
     )(*mate_msg, dense, cov, info)
 
 
+def far_info(firsts, info_buf, turned, sem):
+    blocks = info_buf.shape[1] - 1
+    cells = turned.shape[0] // len(firsts)
+    copies = []
+    for k, first in enumerate(firsts):
+        copies.append(pltpu.make_async_copy(first.at[pl.ds(0, 1 + blocks)], info_buf.at[k], sem.at[k]))
+        copies[-1].start()
+    for k, copy in enumerate(copies):
+        copy.wait()
+        read_info(info_buf.at[k], blocks, None, turned.at[pl.ds(k * cells, cells)])
+
+
+def far_start_kernel(count, *refs):
+    firsts = refs[:count]
+    info_ref, far_ref, info_buf, turned, sem = refs[count:]
+    far_info(firsts, info_buf, turned, sem)
+    cells = info_ref.shape[1]
+    piece = min(128, cells)
+
+    @pl.loop(0, count * cells // piece)
+    def _(i):
+        fill_covariance(far_ref, i * piece, i * piece, piece, turned, info_ref)
+
+
+def far_scratch(firsts, cells):
+    times, lanes = firsts[0].shape[1:]
+    return [
+        pltpu.VMEM((len(firsts), 1 + cells // lanes, times, lanes), BF16),
+        pltpu.VMEM((len(firsts) * cells, INFO), F32),
+        pltpu.SemaphoreType.DMA((len(firsts),)),
+    ]
+
+
+def far_start(firsts, info):
+    cells = info.shape[1]
+    count = len(firsts)
+    return pl.pallas_call(
+        functools.partial(far_start_kernel, count),
+        out_shape=shape_of((count * cells, cells), BF16),
+        in_specs=[ANY] * count + [VMEM],
+        out_specs=VMEM,
+        scratch_shapes=far_scratch(firsts, cells),
+        compiler_params=params(10),
+        cost_estimate=cost(4),
+        name="far_start",
+    )(*firsts, info)
+
+
 def mate_kernel(count, *refs):
     firsts = refs[:count]
     near_ref, dense, cov_ref, info_ref, out_ref, far_ref, info_buf, turned, sem = refs[count:]
-    _, lanes = info_buf.shape[2:]
     cells = cov_ref.shape[1]
-    blocks = cells // lanes
     tall = min(256, dense.shape[0])
     steps = dense.shape[0] // tall
     part = count * cells // steps
-    copies = []
-    for k in range(count):
-        copies.append(pltpu.make_async_copy(firsts[k].at[pl.ds(0, 1 + blocks)], info_buf.at[k], sem.at[k]))
-        copies[-1].start()
-    for k in range(count):
-        copies[k].wait()
-        read_info(info_buf.at[k], blocks, None, turned.at[pl.ds(k * cells, cells)])
+    far_info(firsts, info_buf, turned, sem)
 
     @pl.loop(0, steps)
     def _(u):
@@ -437,23 +477,17 @@
 
 
 def mate_call(firsts, near, mate_dense, cov, info):
-    times, lanes = firsts[0].shape[1:]
     cells = cov.shape[1]
-    blocks = cells // lanes
     count = len(firsts)
     return pl.pallas_call(
         functools.partial(mate_kernel, count),
         out_shape=(shape_of(near.shape, F32), shape_of((count * cells, cells), BF16)),
         in_specs=[ANY] * count + [VMEM] * 4,
         out_specs=(VMEM, VMEM),
-        scratch_shapes=[
-            pltpu.VMEM((count, 1 + blocks, times, lanes), BF16),
-            pltpu.VMEM((count * cells, INFO), F32),
-            pltpu.SemaphoreType.DMA((count,)),
-        ],
+        scratch_shapes=far_scratch(firsts, cells),
         input_output_aliases={count: 0},
         compiler_params=params(16),
-        cost_estimate=cost(8),
+        cost_estimate=cost(5),
         name="mate_product",
     )(*firsts, near, mate_dense, cov, info)
 
@@ -469,15 +503,15 @@
     return jnp.swapaxes(value.reshape(rows, times, value.shape[1]), 0, 1)
 
 
-def unit_step(u, count, unit, bufs, bits_s, dense_a, dense_b, near_ref, cov_ref, mix_ref, rows):
+def unit_step(u, count, unit, bufs, bits_s, dense_a, dense_b, near_ref, cov_refs, mix_ref, rows):
     times, _ = bufs.shape[2:]
     cells = near_ref.shape[1]
     few = count // 2
     here = aligned(u * unit * times, unit * times)
     place(u, few, count, unit, bufs, bits_s, dense_b, cells)
-    value = near_ref[here, :] + jnp.dot(dense_a[...], cov_ref[: few * cells, :], preferred_element_type=F32)
+    value = near_ref[here, :] + jnp.dot(dense_a[...], cov_refs[0][...], preferred_element_type=F32)
     place(jnp.minimum(u + 1, rows // unit - 1), 0, few, unit, bufs, bits_s, dense_a, cells)
-    value = value + jnp.dot(dense_b[...], cov_ref[few * cells :, :], preferred_element_type=F32)
+    value = value + jnp.dot(dense_b[...], cov_refs[1][...], preferred_element_type=F32)
     return mixed_unit(mix_ref, value)
 
 
@@ -490,7 +524,7 @@
 
 def first_kernel(count, chunks, unit, *refs):
     msgs = [refs[k * chunks : (k + 1) * chunks] for k in range(count)]
-    cov_ref, near_ref, mix_ref, out_ref, next_ref, bufs, bits_v, bits_s, dense_a, dense_b, sem = refs[count * chunks :]
+    *cov_refs, near_ref, mix_ref, out_ref, next_ref, bufs, bits_v, bits_s, dense_a, dense_b, sem = refs[count * chunks :]
     times, lanes = bufs.shape[2:]
     cells = near_ref.shape[1]
     blocks = cells // lanes
@@ -512,7 +546,7 @@
     place(jnp.int32(0), 0, count // 2, unit, bufs, bits_s, dense_a, cells)
 
     def step(u, _):
-        mixed = unit_step(u, count, unit, bufs, bits_s, dense_a, dense_b, near_ref, cov_ref, mix_ref, rows)
+        mixed = unit_step(u, count, unit, bufs, bits_s, dense_a, dense_b, near_ref, cov_refs, mix_ref, rows)
         out_ref[aligned(u * unit, unit)] = mixed.reshape(unit, times, cells)
         return 0
 
@@ -530,7 +564,7 @@
     ]
 
 
-def first_rows(msgs, cov, near, mix, rows, unit, slots):
+def first_rows(msgs, covs, near, mix, rows, unit, slots):
     times, lanes = msgs[0][0].shape[1:]
     cells = near.shape[1]
     count, chunks = len(msgs), len(msgs[0])
@@ -538,21 +572,21 @@
     return pl.pallas_call(
         functools.partial(first_kernel, count, chunks, unit),
         out_shape=(shape_of((rows, times, cells), BF16), shape_of((1,), I32)),
-        in_specs=[ANY] * len(flat) + [VMEM] * 3,
+        in_specs=[ANY] * len(flat) + [VMEM] * 4,
         out_specs=(VMEM, SMEM),
         scratch_shapes=rows_scratch(count, chunks, slots, times, lanes, unit, cells, 0),
         compiler_params=params(16),
         cost_estimate=cost(7),
         name="first_rows",
-    )(*flat, cov, near, mix)
+    )(*flat, *covs, near, mix)
 
 
 def late_kernel(count, chunks, unit, pieces, each, *refs):
     msgs = [refs[k * chunks : (k + 1) * chunks] for k in range(count)]
     panel_msgs = refs[count * chunks : count * chunks + pieces]
     refs = refs[count * chunks + pieces :]
-    cov_ref, near_ref, mix_ref, start_ref, done_ref, out_ref, turned_ref, part_ref, over_ref = refs[:9]
-    bufs, bits_v, bits_s, dense_a, dense_b, sem, panel_bufs, stage, panel, panel_sem, out_sem = refs[9:]
+    *cov_refs, near_ref, mix_ref, start_ref, done_ref, out_ref, turned_ref, part_ref, over_ref = refs[:10]
+    bufs, bits_v, bits_s, dense_a, dense_b, sem, panel_bufs, stage, panel, panel_sem, out_sem = refs[10:]
     times, lanes = bufs.shape[2:]
     cells = near_ref.shape[1]
     blocks = cells // lanes
@@ -587,7 +621,7 @@
     place(jnp.minimum(first, rows // unit - 1), 0, count // 2, unit, bufs, bits_s, dense_a, cells)
 
     def step(u, _):
-        mixed = unit_step(u, count, unit, bufs, bits_s, dense_a, dense_b, near_ref, cov_ref, mix_ref, rows)
+        mixed = unit_step(u, count, unit, bufs, bits_s, dense_a, dense_b, near_ref, cov_refs, mix_ref, rows)
         at = aligned(u * unit, unit)
         stage[at] = mixed.reshape(unit, times, cells)
         outgoing(u, stage).start()
@@ -605,7 +639,7 @@
     lax.fori_loop(0, rows // unit, settle, 0)
 
 
-def late_rows(msgs, panel_msgs, each, cov, near, mix, start, done, unit, slots):
+def late_rows(msgs, panel_msgs, each, covs, near, mix, start, done, unit, slots):
     times, lanes = msgs[0][0].shape[1:]
     rows, _, cells = done.shape
     count, chunks, pieces = len(msgs), len(msgs[0]), len(panel_msgs)
@@ -618,7 +652,7 @@
             shape_of((rows, pieces * each), F32),
             shape_of((1,), I32),
         ),
-        in_specs=[ANY] * len(flat) + [VMEM] * 3 + [SMEM, VMEM],
+        in_specs=[ANY] * len(flat) + [VMEM] * 4 + [SMEM, VMEM],
         out_specs=(HBM, VMEM, VMEM, SMEM),
         scratch_shapes=rows_scratch(count, chunks, slots, times, lanes, unit, cells, pieces)
         + [
@@ -631,7 +665,7 @@
         compiler_params=params(20),
         cost_estimate=cost(9),
         name="late_rows",
-    )(*flat, cov, near, mix, start, done)
+    )(*flat, *covs, near, mix, start, done)
 
 
 def mix_kernel(unit, time_ref, out_ref):
@@ -845,7 +879,11 @@
 
     dense, own_cov, info = start_call(own_msg, obs_rows, cell_local)
     near, mate_dense, mate_cov = own_call(mate_msg, dense, own_cov, info)
-    near, far_cov = mate_call([msg[0] for msg in far_msgs], near, mate_dense, mate_cov, info)
+    firsts = [msg[0] for msg in far_msgs]
+    few = len(firsts) // 2
+    some_cov = far_start(firsts[:few], info)
+    near, more_cov = mate_call(firsts[few:], near, mate_dense, mate_cov, info)
+    far_cov = (some_cov, more_cov)
     mix = mixing(time_cov, unit)
     first_cov, start = first_rows([msg[:-1] for msg in far_msgs], far_cov, near, mix, obs_rows, unit, slots)
     cut = len(messages) * 3 // 4

time: 87.2 us -> 87.5 us (level)
  waiting for transfers between devices: 24.1 us -> 20.7 us
  local copies, waits for them, and re-layouts: 3.36 us -> 5.96 us
  starting transfers between devices: 13.8 us -> 14.7 us
    ppermute x8 -> x9, waiting for transfers between devices: 24.1 us -> 19 us  [shifted(): lax.ppermute(value, axis, [(i, (i + 2 * shift) % count ^ flip) for i in r...]
    pallas_call x0 -> x1, Pallas kernels: none -> 2.67 us  [far_start(): pl.pallas_call(functools.partial(far_start_kernel, count), out_shape=shap...]
    unnamed x14 -> x18, local copies, waits for them, and re-layouts: 2.08 us -> 4.74 us
    pallas_call x1, Pallas kernels: 6.68 us -> 4.74 us  [mate_call(): pl.pallas_call(functools.partial(mate_kernel, count), out_shape=(shape_of...]
    ppermute x8 -> x10, waiting for transfers between devices: 0.02 us -> 1.75 us  [partner(): return lax.ppermute(value, axis, [(i, i ^ 1) for i in range(count)])]
    ppermute x8 -> x10, starting transfers between devices: 5.01 us -> 6.58 us  [partner(): return lax.ppermute(value, axis, [(i, i ^ 1) for i in range(count)])]
    pallas_call x1, Pallas kernels: 6.4 us -> 5.47 us  [own_call(): pl.pallas_call(functools.partial(own_kernel, chunks), out_shape=(shape_of...]
    ppermute x8 -> x9, starting transfers between devices: 8.75 us -> 8.13 us  [shifted(): lax.ppermute(value, axis, [(i, (i + 2 * shift) % count ^ flip) for i in r...]
  transfers between devices with their start and end apart: 16 -> 19, of which waited for: 5 -> 7; matrix products, arithmetic and copies ran while one was open for 0% -> 0% of each run, Pallas kernels for 42% -> 42%
where the time goes in v5:
time: 87.5 us; the launch traced here: 87.1 us
  Pallas kernels  43.9 us (50%)
  waiting for transfers between devices  20.7 us (24%)
  starting transfers between devices  14.7 us (17%)
  local copies, waits for them, and re-layouts  5.96 us (7%)
  between operations  1.6 us (2%)
    ppermute x9, waiting for transfers between devices, shifted(): lax.ppermute(value, axis, [(i, (i + 2 * shift) % count ^ flip) for i in r...  19 us
    pallas_call x1, Pallas kernels, late_rows(): pl.pallas_call(functools.partial(late_kernel, count, chunks, unit, pieces...  11.2 us
    ppermute x9, starting transfers between devices, shifted(): lax.ppermute(value, axis, [(i, (i + 2 * shift) % count ^ flip) for i in r...  8.13 us
    ppermute x10, starting transfers between devices, partner(): return lax.ppermute(value, axis, [(i, i ^ 1) for i in range(count)])  6.58 us
    pallas_call x1, Pallas kernels, own_call(): pl.pallas_call(functools.partial(own_kernel, chunks), out_shape=(shape_of...  5.47 us
    pallas_call x1, Pallas kernels, first_rows(): pl.pallas_call(functools.partial(first_kernel, count, chunks, unit), out_...  5.33 us
    unnamed x18, local copies, waits for them, and re-layouts  4.74 us
    pallas_call x1, Pallas kernels, mate_call(): pl.pallas_call(functools.partial(mate_kernel, count), out_shape=(shape_of...  4.74 us
  transfers between devices with their start and end apart: 19, of which 7 were waited for; matrix products, arithmetic and copies ran while one was open for 0% of the time, Pallas kernels for 42%

profile of v5, /device:TPU:0, one launch (start us, length us, event | category | flops | bytes accessed | tf_op | source)
XLA Modules:
  0.0 87.1 jit_solution(15800699931697394105)
XLA Ops:
  2.7 3.8 %pack_feet.1 = (bf16[9,16,128]{2,1,0:T(8,128)(2,1)S(1)}, bf16[152,16,128]{2,1,0:T(8,128)(2,1)S(1)}, bf16[151,16,128]{2,1,0:T(8,128)(2,1)S(1)}) custom-call(s32[8,64]{1,0:T(8,128)S(1)} %bitcast.77, s32[2,1024]{1,0:T(2,128)S(1)} %copy-done.2, f32[1,1024]{1,0:T(1,128)S(1)} %bitcast.81, bf16[64,16,1024]{2,1,0:T(8,128)(2,1)} %feet_ref.3), custom_call_target="tpu_custom_call" | custom-call | flops 2700000000 | bytes 1000000 | tf_op jit(solution)/shard_map/pack_feet/pallas_call | solution.py:156
  7.1 2.6 %collective-permute-start.12 = (bf16[152,16,128]{2,1,0:T(8,128)(2,1)S(1)}, bf16[152,16,128]{2,1,0:T(8,128)(2,1)S(1)}, u32[]{:S(2)}, u32[]{:S(2)}) collective-permute-start(bf16[152,16,128]{2,1,0:T(8,128)(2,1)S(1)} %get-tuple-element.123.refs_1_), channel_id=1, source_target_pairs={{0,2},{1,3},{2,0},{3,1},{4,6},{5,7},{6,4},{7,5},{8,10},{9,11},{10,... | collective-permute-start | bytes 1867784 | tf_op jit(solution)/shard_map/ppermute | solution.py:800
  10.1 3.7 %own_start.1 = (bf16[1024,1024]{1,0:T(8,128)(2,1)S(1)}, bf16[1024,1024]{1,0:T(8,128)(2,1)S(1)}, f32[8,1024]{1,0:T(8,128)S(1)}) custom-call(bf16[9,16,128]{2,1,0:T(8,128)(2,1)S(1)} %get-tuple-element.122.refs_0_, bf16[152,16,128]{2,1,0:T(8,128)(2,1)S(1)} %get-tuple-element.123.refs_1_, bf16[151,16,128]{2,1,0:T(8,128)(2,1)S(1)} %get-tuple-element.124.refs_2_), custom_call_target="tpu_custom_call" | custom-call | flops 3600000000 | bytes 1000000 | tf_op jit(solution)/shard_map/own_start/pallas_call | solution.py:345
  13.8 1.3 %copy-done.4 = bf16[1024,1024]{1,0:T(8,128)(2,1)} copy-done((bf16[1024,1024]{1,0:T(8,128)(2,1)}, bf16[1024,1024]{1,0:T(8,128)(2,1)S(1)}, u32[]{:S(2)}) %copy-start.4) | copy-done | bytes 2097176
  15.1 1.3 %copy-done.6 = bf16[1024,1024]{1,0:T(8,128)(2,1)} copy-done((bf16[1024,1024]{1,0:T(8,128)(2,1)}, bf16[1024,1024]{1,0:T(8,128)(2,1)S(1)}, u32[]{:S(2)}) %copy-start.6) | copy-done | bytes 2097176
  16.5 2.2 %pack_panel.1.refs_6_ = bf16[90,16,128]{2,1,0:T(8,128)(2,1)S(1)} custom-call(s32[8,64]{1,0:T(8,128)S(1)} %bitcast.78, s32[8,64]{1,0:T(8,128)S(1)} %bitcast.79, s32[128]{0:T(128)S(1)} %copy-done.9, s32[1]{0:T(128)} %bitcast.12.group_ref.refs_2_, s32[1]{0:T(128)} %bitcast.13.member_ref.refs_3_, bf16[64,16,1024]{2,1,0:T(8,128)(2,1)} %feet_ref.3), custom_call_target="tpu_custom_call" | custom-call | flops 1800000000 | bytes 1000000 | tf_op jit(solution)/shard_map/pack_panel/pallas_call | solution.py:205
  19.9 5.2 %collective-permute-done.11.refs_0_ = bf16[9,16,128]{2,1,0:T(8,128)(2,1)S(1)} collective-permute-done((bf16[9,16,128]{2,1,0:T(8,128)(2,1)S(1)}, bf16[9,16,128]{2,1,0:T(8,128)(2,1)S(1)}, u32[]{:S(2)}, u32[]{:S(2)}) %collective-permute-start.11) | collective-permute-done | bytes 36896 | tf_op jit(solution)/shard_map/ppermute | solution.py:800
  25.0 1.7 %collective-permute-start.13 = (bf16[151,16,128]{2,1,0:T(8,128)(2,1)S(1)}, bf16[151,16,128]{2,1,0:T(8,128)(2,1)S(1)}, u32[]{:S(2)}, u32[]{:S(2)}) collective-permute-start(bf16[151,16,128]{2,1,0:T(8,128)(2,1)S(1)} %get-tuple-element.124.refs_2_), channel_id=1, source_target_pairs={{0,2},{1,3},{2,0},{3,1},{4,6},{5,7},{6,4},{7,5},{8,10},{9,11},{10,... | collective-permute-start | bytes 1855496 | tf_op jit(solution)/shard_map/ppermute | solution.py:800
  26.8 2.7 %far_start.1.refs_4_.refs_12_ = bf16[1024,1024]{1,0:T(8,128)(2,1)S(1)} custom-call(bf16[9,16,128]{2,1,0:T(8,128)(2,1)S(1)} %collective-permute-done.11.refs_0_, f32[8,1024]{1,0:T(8,128)S(1)} %get-tuple-element.350.refs_1_.refs_5_.refs_4_), custom_call_target="tpu_custom_call" | custom-call | flops 3600000000 | bytes 1000000 | tf_op jit(solution)/shard_map/far_start/pallas_call | solution.py:451
  29.5 1.6 %collective-permute-start.7 = (bf16[90,16,128]{2,1,0:T(8,128)(2,1)S(1)}, bf16[90,16,128]{2,1,0:T(8,128)(2,1)S(1)}, u32[]{:S(2)}, u32[]{:S(2)}) collective-permute-start(bf16[90,16,128]{2,1,0:T(8,128)(2,1)S(1)} %pack_panel.1.refs_6_), channel_id=1, source_target_pairs={{0,8},{4,12},{8,16},{12,20},{16,24},{20,28},{24,0},{28,4},{1,9},{5... | collective-permute-start | bytes 1105928 | tf_op jit(solution)/shard_map/ppermute | solution.py:800
  31.6 5.5 %own_product.1 = (f32[1024,1024]{1,0:T(8,128)S(1)}, bf16[1024,1024]{1,0:T(8,128)(2,1)S(1)}, bf16[1024,1024]{1,0:T(8,128)(2,1)S(1)}) custom-call(bf16[9,16,128]{2,1,0:T(8,128)(2,1)S(1)} %collective-permute-done.20.refs_0_, bf16[152,16,128]{2,1,0:T(8,128)(2,1)S(1)} %collective-permute-done.21.refs_1_, ...), custom_call_target="tpu_custom_call" | custom-call | flops 5400000000 | bytes 1000000 | tf_op jit(solution)/shard_map/own_product/pallas_call | solution.py:397
  37.1 1.6 %collective-permute-start.17 = (bf16[90,16,128]{2,1,0:T(8,128)(2,1)S(1)}, bf16[90,16,128]{2,1,0:T(8,128)(2,1)S(1)}, u32[]{:S(2)}, u32[]{:S(2)}) collective-permute-start(bf16[90,16,128]{2,1,0:T(8,128)(2,1)S(1)} %pack_panel.1.refs_6_), channel_id=1, source_target_pairs={{0,4},{4,0},{8,12},{12,8},{16,20},{20,16},{24,28},{28,24},{1,5},{5... | collective-permute-start | bytes 1105928 | tf_op jit(solution)/shard_map/ppermute | solution.py:796
  38.7 2.5 %collective-permute-done.7.refs_8_ = bf16[90,16,128]{2,1,0:T(8,128)(2,1)S(1)} collective-permute-done((bf16[90,16,128]{2,1,0:T(8,128)(2,1)S(1)}, bf16[90,16,128]{2,1,0:T(8,128)(2,1)S(1)}, u32[]{:S(2)}, u32[]{:S(2)}) %collective-permute-start.7) | collective-permute-done | bytes 368672 | tf_op jit(solution)/shard_map/ppermute | solution.py:800
  41.2 4.7 %mate_product.1 = (f32[1024,1024]{1,0:T(8,128)S(1)}, bf16[1024,1024]{1,0:T(8,128)(2,1)S(1)}) custom-call(bf16[9,16,128]{2,1,0:T(8,128)(2,1)S(1)} %collective-permute-done.14.refs_0_.refs_2_.refs_3_, f32[1024,1024]{1,0:T(8,128)S(1)} %get-tuple-element.128.refs_1_, bf16[1024,1024]{1,0:T(8,128)(2,1)S(1)} %get-tuple-element.129.refs_2_, ...), custom_call_target="tpu_custom_call", output_to_operand_aliasing={{0}: (1, {})} | custom-call | flops 4499999744 | bytes 1000000 | tf_op jit(solution)/shard_map/mate_product/pallas_call | solution.py:482
  46.0 1.6 %collective-permute-start.18 = (bf16[90,16,128]{2,1,0:T(8,128)(2,1)S(1)}, bf16[90,16,128]{2,1,0:T(8,128)(2,1)S(1)}, u32[]{:S(2)}, u32[]{:S(2)}) collective-permute-start(bf16[90,16,128]{2,1,0:T(8,128)(2,1)S(1)} %collective-permute-done.7.refs_8_), channel_id=1, source_target_pairs={{0,4},{4,0},{8,12},{12,8},{16,20},{20,16},{24,28},{28,24},{1,5},{5... | collective-permute-start | bytes 1105928 | tf_op jit(solution)/shard_map/ppermute | solution.py:796
  47.5 4.4 %collective-permute-done.8.refs_10_ = bf16[90,16,128]{2,1,0:T(8,128)(2,1)S(1)} collective-permute-done((bf16[90,16,128]{2,1,0:T(8,128)(2,1)S(1)}, bf16[90,16,128]{2,1,0:T(8,128)(2,1)S(1)}, u32[]{:S(2)}, u32[]{:S(2)}) %collective-permute-start.8) | collective-permute-done | bytes 368672 | tf_op jit(solution)/shard_map/ppermute | solution.py:800
  52.0 1.5 %collective-permute-start.19 = (bf16[90,16,128]{2,1,0:T(8,128)(2,1)S(1)}, bf16[90,16,128]{2,1,0:T(8,128)(2,1)S(1)}, u32[]{:S(2)}, u32[]{:S(2)}) collective-permute-start(bf16[90,16,128]{2,1,0:T(8,128)(2,1)S(1)} %collective-permute-done.8.refs_10_), channel_id=1, source_target_pairs={{0,4},{4,0},{8,12},{12,8},{16,20},{20,16},{24,28},{28,24},{1,5},{5... | collective-permute-start | bytes 1105928 | tf_op jit(solution)/shard_map/ppermute | solution.py:796
  53.5 5.3 %first_rows.1 = (bf16[64,16,1024]{2,1,0:T(8,128)(2,1)S(1)}, s32[1]{0:T(128)}) custom-call(bf16[9,16,128]{2,1,0:T(8,128)(2,1)S(1)} %collective-permute-done.11.refs_0_, bf16[152,16,128]{2,1,0:T(8,128)(2,1)S(1)} %collective-permute-done.12.refs_1_, bf16[9,16,128]{2,1,0:T(8,128)(2,1)S(1)} %collective-permute-done.14.refs_0_.refs_2_.refs_3_, ...), custom_call_target="tpu_custom_call" | custom-call | flops 6300000256 | bytes 1000000 | tf_op jit(solution)/shard_map/first_rows/pallas_call | solution.py:572
  58.8 4.3 %collective-permute-done.9.refs_0_ = bf16[90,16,128]{2,1,0:T(8,128)(2,1)S(1)} collective-permute-done((bf16[90,16,128]{2,1,0:T(8,128)(2,1)S(1)}, bf16[90,16,128]{2,1,0:T(8,128)(2,1)S(1)}, u32[]{:S(2)}, u32[]{:S(2)}) %collective-permute-start.9) | collective-permute-done | bytes 368672 | tf_op jit(solution)/shard_map/ppermute | solution.py:800
  63.7 1.7 %collective-permute-done.19.refs_11_ = bf16[90,16,128]{2,1,0:T(8,128)(2,1)S(1)} collective-permute-done((bf16[90,16,128]{2,1,0:T(8,128)(2,1)S(1)}, bf16[90,16,128]{2,1,0:T(8,128)(2,1)S(1)}, u32[]{:S(2)}, u32[]{:S(2)}) %collective-permute-start.19) | collective-permute-done | bytes 368672 | tf_op jit(solution)/shard_map/ppermute | solution.py:796
  65.4 11.2 %late_rows.1 = (bf16[64,16,1024]{2,1,0:T(8,128)(2,1)}, bf16[16,64,1024]{2,1,0:T(8,128)(2,1)S(1)}, f32[64,96]{1,0:T(8,128)S(1)}, s32[1]{0:T(128)}) custom-call(bf16[9,16,128]{2,1,0:T(8,128)(2,1)S(1)} %collective-permute-done.11.refs_0_, bf16[152,16,128]{2,1,0:T(8,128)(2,1)S(1)} %collective-permute-done.12.refs_1_, ...), custom_call_target="tpu_custom_call" | custom-call | flops 8099999744 | bytes 1000000 | tf_op jit(solution)/shard_map/late_rows/pallas_call | solution.py:647
  76.6 3.7 %panel_last.1 = f32[72,128]{1,0:T(8,128)S(1)} custom-call(bf16[90,16,128]{2,1,0:T(8,128)(2,1)S(1)} %collective-permute-done.9.refs_0_, bf16[90,16,128]{2,1,0:T(8,128)(2,1)S(1)} %collective-permute-done.10.refs_1_, s32[1]{0:T(128)} %bitcast.12.group_ref.refs_2_, s32[1]{0:T(128)} %bitcast.13.member_ref.refs_3_, s32[1,128]{1,0:T(1,128)S(1)} %bitcast.98, ...), custom_call_target="tpu_custom_call" | custom-call | flops 2700000000 | bytes 1000000 | tf_op jit(solution)/shard_map/panel_last/pallas_call | solution.py:777
  80.4 1.1 %collective-permute-start.24 = (f32[72,128]{1,0:T(8,128)S(1)}, f32[72,128]{1,0:T(8,128)S(1)}, u32[]{:S(2)}, u32[]{:S(2)}) collective-permute-start(f32[72,128]{1,0:T(8,128)S(1)} %panel_last.1), channel_id=1, source_target_pairs={{0,2},{1,3},{2,0},{3,1},{4,6},{5,7},{6,4},{7,5},{8,10},{9,11},{10,... | collective-permute-start | bytes 110600 | tf_op jit(solution)/shard_map/ppermute | solution.py:800
  82.3 2.1 %collective-permute-done.24 = f32[72,128]{1,0:T(8,128)S(1)} collective-permute-done((f32[72,128]{1,0:T(8,128)S(1)}, f32[72,128]{1,0:T(8,128)S(1)}, u32[]{:S(2)}, u32[]{:S(2)}) %collective-permute-start.24) | collective-permute-done | bytes 36896 | tf_op jit(solution)/shard_map/ppermute | solution.py:800
  (47 shorter events, 8.1 us)
Async XLA Ops:
  6.5 25.1 %collective-permute-start.21 = (bf16[152,16,128]{2,1,0:T(8,128)(2,1)S(1)}, bf16[152,16,128]{2,1,0:T(8,128)(2,1)S(1)}, u32[]{:S(2)}, u32[]{:S(2)}) collective-permute-start(bf16[152,16,128]{2,1,0:T(8,128)(2,1)S(1)} %get-tuple-element.123.refs_1_), channel_id=1, source_target_pairs={{0,1},{1,0},{2,3},{3,2},{4,5},{5,4},{6,7},{7,6},{8,9},{9,8},{10,11... | collective-permute-start | bytes 1867784 | tf_op jit(solution)/shard_map/ppermute | solution.py:796
  7.1 24.0 %collective-permute-start.12 = (bf16[152,16,128]{2,1,0:T(8,128)(2,1)S(1)}, bf16[152,16,128]{2,1,0:T(8,128)(2,1)S(1)}, u32[]{:S(2)}, u32[]{:S(2)}) collective-permute-start(bf16[152,16,128]{2,1,0:T(8,128)(2,1)S(1)} %get-tuple-element.123.refs_1_), channel_id=1, source_target_pairs={{0,2},{1,3},{2,0},{3,1},{4,6},{5,7},{6,4},{7,5},{8,10},{9,11},{10,... | collective-permute-start | bytes 1867784 | tf_op jit(solution)/shard_map/ppermute | solution.py:800
  9.6 21.5 %collective-permute-start.22 = (bf16[151,16,128]{2,1,0:T(8,128)(2,1)S(1)}, bf16[151,16,128]{2,1,0:T(8,128)(2,1)S(1)}, u32[]{:S(2)}, u32[]{:S(2)}) collective-permute-start(bf16[151,16,128]{2,1,0:T(8,128)(2,1)S(1)} %get-tuple-element.124.refs_2_), channel_id=1, source_target_pairs={{0,1},{1,0},{2,3},{3,2},{4,5},{5,4},{6,7},{7,6},{8,9},{9,8},{10,11... | collective-permute-start | bytes 1855496 | tf_op jit(solution)/shard_map/ppermute | solution.py:796
  9.8 6.7 %copy-start.1 = (s32[64,8]{0,1:T(8,128)S(1)}, s32[64,8]{0,1:T(8,128)}, u32[]{:S(2)}) copy-start(s32[64,8]{0,1:T(8,128)} %param.14) | copy-start | bytes 6148
  9.8 6.7 %copy-start.9 = (s32[128]{0:T(128)S(1)}, s32[128]{0:T(128)}, u32[]{:S(2)}) copy-start(s32[128]{0:T(128)} %index_ref.1) | copy-start | bytes 1540
  9.8 15.3 %collective-permute-start.11 = (bf16[9,16,128]{2,1,0:T(8,128)(2,1)S(1)}, bf16[9,16,128]{2,1,0:T(8,128)(2,1)S(1)}, u32[]{:S(2)}, u32[]{:S(2)}) collective-permute-start(bf16[9,16,128]{2,1,0:T(8,128)(2,1)S(1)} %get-tuple-element.122.refs_0_), channel_id=1, source_target_pairs={{0,2},{1,3},{2,0},{3,1},{4,6},{5,7},{6,4},{7,5},{8,10},{9,11},{10,... | collective-permute-start | bytes 110600 | tf_op jit(solution)/shard_map/ppermute | solution.py:800
  15.1 1.4 %copy-start.6 = (bf16[1024,1024]{1,0:T(8,128)(2,1)}, bf16[1024,1024]{1,0:T(8,128)(2,1)S(1)}, u32[]{:S(2)}) copy-start(bf16[1024,1024]{1,0:T(8,128)(2,1)S(1)} %get-tuple-element.127.refs_4_) | copy-start | bytes 6291460
  19.7 9.8 %collective-permute-start.20 = (bf16[9,16,128]{2,1,0:T(8,128)(2,1)S(1)}, bf16[9,16,128]{2,1,0:T(8,128)(2,1)S(1)}, u32[]{:S(2)}, u32[]{:S(2)}) collective-permute-start(bf16[9,16,128]{2,1,0:T(8,128)(2,1)S(1)} %get-tuple-element.122.refs_0_), channel_id=1, source_target_pairs={{0,1},{1,0},{2,3},{3,2},{4,5},{5,4},{6,7},{7,6},{8,9},{9,8},{10,11... | collective-permute-start | bytes 110600 | tf_op jit(solution)/shard_map/ppermute | solution.py:796
  25.0 16.1 %collective-permute-start.13 = (bf16[151,16,128]{2,1,0:T(8,128)(2,1)S(1)}, bf16[151,16,128]{2,1,0:T(8,128)(2,1)S(1)}, u32[]{:S(2)}, u32[]{:S(2)}) collective-permute-start(bf16[151,16,128]{2,1,0:T(8,128)(2,1)S(1)} %get-tuple-element.124.refs_2_), channel_id=1, source_target_pairs={{0,2},{1,3},{2,0},{3,1},{4,6},{5,7},{6,4},{7,5},{8,10},{9,11},{10,... | collective-permute-start | bytes 1855496 | tf_op jit(solution)/shard_map/ppermute | solution.py:800
  26.8 4.8 %copy-start.5 = (bf16[1024,1024]{1,0:T(8,128)(2,1)S(1)}, bf16[1024,1024]{1,0:T(8,128)(2,1)}, u32[]{:S(2)}) copy-start(bf16[1024,1024]{1,0:T(8,128)(2,1)} %copy-done.4) | copy-start | bytes 6291460
  26.8 4.8 %copy-start.7 = (bf16[1024,1024]{1,0:T(8,128)(2,1)S(1)}, bf16[1024,1024]{1,0:T(8,128)(2,1)}, u32[]{:S(2)}) copy-start(bf16[1024,1024]{1,0:T(8,128)(2,1)} %copy-done.6) | copy-start | bytes 6291460
  29.5 11.7 %collective-permute-start.7 = (bf16[90,16,128]{2,1,0:T(8,128)(2,1)S(1)}, bf16[90,16,128]{2,1,0:T(8,128)(2,1)S(1)}, u32[]{:S(2)}, u32[]{:S(2)}) collective-permute-start(bf16[90,16,128]{2,1,0:T(8,128)(2,1)S(1)} %pack_panel.1.refs_6_), channel_id=1, source_target_pairs={{0,8},{4,12},{8,16},{12,20},{16,24},{20,28},{24,0},{28,4},{1,9},{5... | collective-permute-start | bytes 1105928 | tf_op jit(solution)/shard_map/ppermute | solution.py:800
  31.1 10.1 %collective-permute-start.14 = (bf16[9,16,128]{2,1,0:T(8,128)(2,1)S(1)}, bf16[9,16,128]{2,1,0:T(8,128)(2,1)S(1)}, u32[]{:S(2)}, u32[]{:S(2)}) collective-permute-start(bf16[9,16,128]{2,1,0:T(8,128)(2,1)S(1)} %collective-permute-done.11.refs_0_), channel_id=1, source_target_pairs={{0,1},{1,0},{2,3},{3,2},{4,5},{5,4},{6,7},{7,6},{8,9},{9,8},{10,11... | collective-permute-start | bytes 110600 | tf_op jit(solution)/shard_map/ppermute | solution.py:796
  31.1 22.4 %collective-permute-start.15 = (bf16[152,16,128]{2,1,0:T(8,128)(2,1)S(1)}, bf16[152,16,128]{2,1,0:T(8,128)(2,1)S(1)}, u32[]{:S(2)}, u32[]{:S(2)}) collective-permute-start(bf16[152,16,128]{2,1,0:T(8,128)(2,1)S(1)} %collective-permute-done.12.refs_1_), channel_id=1, source_target_pairs={{0,1},{1,0},{2,3},{3,2},{4,5},{5,4},{6,7},{7,6},{8,9},{9,8},{10,11... | collective-permute-start | bytes 1867784 | tf_op jit(solution)/shard_map/ppermute | solution.py:796
  37.1 26.5 %collective-permute-start.17 = (bf16[90,16,128]{2,1,0:T(8,128)(2,1)S(1)}, bf16[90,16,128]{2,1,0:T(8,128)(2,1)S(1)}, u32[]{:S(2)}, u32[]{:S(2)}) collective-permute-start(bf16[90,16,128]{2,1,0:T(8,128)(2,1)S(1)} %pack_panel.1.refs_6_), channel_id=1, source_target_pairs={{0,4},{4,0},{8,12},{12,8},{16,20},{20,16},{24,28},{28,24},{1,5},{5... | collective-permute-start | bytes 1105928 | tf_op jit(solution)/shard_map/ppermute | solution.py:796
  41.2 10.8 %collective-permute-start.8 = (bf16[90,16,128]{2,1,0:T(8,128)(2,1)S(1)}, bf16[90,16,128]{2,1,0:T(8,128)(2,1)S(1)}, u32[]{:S(2)}, u32[]{:S(2)}) collective-permute-start(bf16[90,16,128]{2,1,0:T(8,128)(2,1)S(1)} %collective-permute-done.7.refs_8_), channel_id=1, source_target_pairs={{0,8},{4,12},{8,16},{12,20},{16,24},{20,28},{24,0},{28,4},{1,9},{5... | collective-permute-start | bytes 1105928 | tf_op jit(solution)/shard_map/ppermute | solution.py:800
  41.2 24.2 %collective-permute-start.16 = (bf16[151,16,128]{2,1,0:T(8,128)(2,1)S(1)}, bf16[151,16,128]{2,1,0:T(8,128)(2,1)S(1)}, u32[]{:S(2)}, u32[]{:S(2)}) collective-permute-start(bf16[151,16,128]{2,1,0:T(8,128)(2,1)S(1)} %collective-permute-done.13.refs_2_), channel_id=1, source_target_pairs={{0,1},{1,0},{2,3},{3,2},{4,5},{5,4},{6,7},{7,6},{8,9},{9,8},{10,11... | collective-permute-start | bytes 1855496 | tf_op jit(solution)/shard_map/ppermute | solution.py:796
  46.0 17.7 %collective-permute-start.18 = (bf16[90,16,128]{2,1,0:T(8,128)(2,1)S(1)}, bf16[90,16,128]{2,1,0:T(8,128)(2,1)S(1)}, u32[]{:S(2)}, u32[]{:S(2)}) collective-permute-start(bf16[90,16,128]{2,1,0:T(8,128)(2,1)S(1)} %collective-permute-done.7.refs_8_), channel_id=1, source_target_pairs={{0,4},{4,0},{8,12},{12,8},{16,20},{20,16},{24,28},{28,24},{1,5},{5... | collective-permute-start | bytes 1105928 | tf_op jit(solution)/shard_map/ppermute | solution.py:796
  52.0 13.4 %collective-permute-start.19 = (bf16[90,16,128]{2,1,0:T(8,128)(2,1)S(1)}, bf16[90,16,128]{2,1,0:T(8,128)(2,1)S(1)}, u32[]{:S(2)}, u32[]{:S(2)}) collective-permute-start(bf16[90,16,128]{2,1,0:T(8,128)(2,1)S(1)} %collective-permute-done.8.refs_10_), channel_id=1, source_target_pairs={{0,4},{4,0},{8,12},{12,8},{16,20},{20,16},{24,28},{28,24},{1,5},{5... | collective-permute-start | bytes 1105928 | tf_op jit(solution)/shard_map/ppermute | solution.py:796
  53.5 9.7 %collective-permute-start.9 = (bf16[90,16,128]{2,1,0:T(8,128)(2,1)S(1)}, bf16[90,16,128]{2,1,0:T(8,128)(2,1)S(1)}, u32[]{:S(2)}, u32[]{:S(2)}) collective-permute-start(bf16[90,16,128]{2,1,0:T(8,128)(2,1)S(1)} %collective-permute-done.8.refs_10_), channel_id=1, source_target_pairs={{0,8},{4,12},{8,16},{12,20},{16,24},{20,28},{24,0},{28,4},{1,9},{5... | collective-permute-start | bytes 1105928 | tf_op jit(solution)/shard_map/ppermute | solution.py:800
  63.1 13.5 %collective-permute-start.10 = (bf16[90,16,128]{2,1,0:T(8,128)(2,1)S(1)}, bf16[90,16,128]{2,1,0:T(8,128)(2,1)S(1)}, u32[]{:S(2)}, u32[]{:S(2)}) collective-permute-start(bf16[90,16,128]{2,1,0:T(8,128)(2,1)S(1)} %collective-permute-done.9.refs_0_), channel_id=1, source_target_pairs={{0,4},{4,0},{8,12},{12,8},{16,20},{20,16},{24,28},{28,24},{1,5},{5... | collective-permute-start | bytes 1105928 | tf_op jit(solution)/shard_map/ppermute | solution.py:796
  80.3 2.0 %collective-permute-start.23 = (f32[72,128]{1,0:T(8,128)S(1)}, f32[72,128]{1,0:T(8,128)S(1)}, u32[]{:S(2)}, u32[]{:S(2)}) collective-permute-start(f32[72,128]{1,0:T(8,128)S(1)} %panel_last.1), channel_id=1, source_target_pairs={{0,1},{1,0},{2,3},{3,2},{4,5},{5,4},{6,7},{7,6},{8,9},{9,8},{10,11... | collective-permute-start | bytes 110600 | tf_op jit(solution)/shard_map/ppermute | solution.py:800
  80.4 4.0 %collective-permute-start.24 = (f32[72,128]{1,0:T(8,128)S(1)}, f32[72,128]{1,0:T(8,128)S(1)}, u32[]{:S(2)}, u32[]{:S(2)}) collective-permute-start(f32[72,128]{1,0:T(8,128)S(1)} %panel_last.1), channel_id=1, source_target_pairs={{0,2},{1,3},{2,0},{3,1},{4,6},{5,7},{6,4},{7,5},{8,10},{9,11},{10,... | collective-permute-start | bytes 110600 | tf_op jit(solution)/shard_map/ppermute | solution.py:800
  81.5 3.4 %collective-permute-start.25 = (f32[72,128]{1,0:T(8,128)S(1)}, f32[72,128]{1,0:T(8,128)S(1)}, u32[]{:S(2)}, u32[]{:S(2)}) collective-permute-start(f32[72,128]{1,0:T(8,128)S(1)} %panel_last.1), channel_id=1, source_target_pairs={{0,3},{1,2},{2,1},{3,0},{4,7},{5,6},{6,5},{7,4},{8,11},{9,10},{10,... | collective-permute-start | bytes 110600 | tf_op jit(solution)/shard_map/ppermute | solution.py:800
  (4 other events, 3.4 us)

commit v6 on v5

--- a/solution.py
+++ b/solution.py
@@ -241,12 +241,6 @@
     buf[0] = jnp.zeros(buf.shape[1:], buf.dtype)
 
 
-def copy_in(src, dst, sem):
-    copy = pltpu.make_async_copy(src, dst, sem)
-    copy.start()
-    copy.wait()
-
-
 def split(number, size):
     if size & (size - 1):
         return lax.div(number, size), lax.rem(number, size)
@@ -315,12 +309,13 @@
     blocks = cells // lanes
     rows = dense.shape[0] // times
     copies = fetch(msg, buf, sem)
-    for copy in copies:
-        copy.wait()
-    read_info(buf, blocks, info_ref, turned)
+    copies[0].wait()
     read_head(buf, rows, blocks, bits_v)
     copy = pltpu.make_async_copy(bits_v, bits_s, sem.at[chunks])
     copy.start()
+    read_info(buf, blocks, info_ref, turned)
+    for other in copies[1:]:
+        other.wait()
     half = cells // 2
     fine = math.gcd(4, rows // 2)
 
@@ -374,11 +369,15 @@
     tall = min(256, rows * times)
     steps = rows * times // tall
     part = cells // steps
-    for copy in fetch(msg, buf, sem):
+    copies = fetch(msg, buf, sem)
+    copies[0].wait()
+    read_head(buf, rows, blocks, bits_v)
+    bits_copy = pltpu.make_async_copy(bits_v, bits_s, sem.at[chunks])
+    bits_copy.start()
+    read_info(buf, blocks, None, turned)
+    for copy in copies[1:]:
         copy.wait()
-    read_info(buf, blocks, None, turned)
-    read_head(buf, rows, blocks, bits_v)
-    copy_in(bits_v, bits_s, sem.at[chunks])
+    bits_copy.wait()
 
     @pl.loop(0, steps)
     def _(u):
@@ -532,10 +531,14 @@
     limit = sum(chunk.shape[0] for chunk in msgs[0])
     copies = [fetch(msgs[k], bufs.at[k], sem.at[k]) for k in range(count)]
     for k in range(count):
-        for copy in copies[k]:
+        copies[k][0].wait()
+        read_head(bufs.at[k], rows, blocks, bits_v.at[k])
+    bits_copy = pltpu.make_async_copy(bits_v, bits_s, sem.at[count, 0])
+    bits_copy.start()
+    for k in range(count):
+        for copy in copies[k][1:]:
             copy.wait()
-        read_head(bufs.at[k], rows, blocks, bits_v.at[k])
-    copy_in(bits_v, bits_s, sem.at[count, 0])
+    bits_copy.wait()
     ready = jnp.int32(0)
     for u in range(rows // unit):
         whole = jnp.int32(1)
@@ -596,8 +599,7 @@
     for copy in panel_copies:
         copy.start()
     for k in range(count):
-        for copy in copies[k]:
-            copy.wait()
+        copies[k][0].wait()
         read_head(bufs.at[k], rows, blocks, bits_v.at[k])
     for k, copy in enumerate(panel_copies):
         copy.wait()
@@ -617,6 +619,9 @@
         return 0
 
     lax.fori_loop(0, first, carry_over, 0)
+    for k in range(count):
+        for copy in copies[k][1:]:
+            copy.wait()
     bits_copy.wait()
     place(jnp.minimum(first, rows // unit - 1), 0, count // 2, unit, bufs, bits_s, dense_a, cells)
 
@@ -804,13 +809,13 @@
     return with_layout_constraint(value, Layout(tuple(range(value.ndim))))
 
 
-def add_cells(part, cells):
-    total = part
-    for shift in range(cells // 2):
-        for flip in range(2):
-            if shift or flip:
-                total = total + shifted(part, "cell", cells, shift, flip)
-    return total
+def cell_parts(part, cells):
+    moves = [(shift, flip) for shift in range(cells // 2) for flip in range(2)]
+    return [part] + [shifted(part, "cell", cells, shift, flip) for shift, flip in moves[1:]]
+
+
+def add_up(parts):
+    return functools.reduce(jnp.add, parts)
 
 
 def dense_way(cells, observers, footprint, block_mask, own, time_cov, mine, sources):
@@ -846,7 +851,7 @@
     _, parts = lax.scan(meet, jnp.take(feet, mine, axis=0), None, length=observers // 2)
     parts = parts.transpose(1, 0, 2).reshape(obs_rows, observers, -1)
     ordered = jnp.zeros_like(parts).at[:, sources].set(parts)
-    return cov_product, add_cells(ordered.reshape(obs_rows, -1), cells)
+    return cov_product, add_up(cell_parts(ordered.reshape(obs_rows, -1), cells))
 
 
 def body(cells, observers, footprint, block_mask, cell_coords, cell_sigma, time_cov, error_var, panel_index):
@@ -893,7 +898,9 @@
     part = panel_last(messages[cut:], turned, each, group, member, panel_index, error_var, before, over)
 
     part, late_group, late_mask = lax.optimization_barrier((part, group, mask))
-    total = add_cells(part, cells)
+    parts = cell_parts(part, cells)
+    total = add_up([value[:obs_rows] for value in parts])
+    over = add_up([value[obs_rows, 0] for value in parts])
 
     def again(carry):
         wanted = carry[0]
@@ -908,7 +915,7 @@
         on_diagonal = (positions[:, None] == panel_index[None, :]).astype(F32)
         return jnp.bool_(False), cov_product, row_major(total + error_var[:, None] * on_diagonal)
 
-    carry = (total[obs_rows, 0] > 0, cov_product, row_major(total[:obs_rows]))
+    carry = (over > 0, cov_product, row_major(total))
     return lax.while_loop(lambda carry: carry[0], again, carry)[1:]
 
 

time: 87.5 us -> 88.2 us (level)
  waiting for transfers between devices: 20.7 us -> 18.2 us
  between operations: 1.6 us -> 3.44 us
  local copies, waits for them, and re-layouts: 5.96 us -> 6.94 us
    ppermute x9, waiting for transfers between devices: 19 us -> 16.4 us  [shifted(): lax.ppermute(value, axis, [(i, (i + 2 * shift) % count ^ flip) for i in r...]
    slice x2 -> x4, local copies, waits for them, and re-layouts: 1.14 us -> 2.11 us  [body(): over = add_up([value[obs_rows, 0] for value in parts])]
  transfers between devices with their start and end apart: 19 -> 19, of which waited for: 7 -> 5; matrix products, arithmetic and copies ran while one was open for 0% -> 2% of each run, Pallas kernels for 42% -> 41%
where the time goes in v6:
time: 88.2 us; the launch traced here: 87.7 us
  Pallas kernels  43.8 us (50%)
  waiting for transfers between devices  18.2 us (21%)
  starting transfers between devices  14.7 us (17%)
  local copies, waits for them, and re-layouts  6.94 us (8%)
  between operations  3.44 us (4%)
    ppermute x9, waiting for transfers between devices, shifted(): lax.ppermute(value, axis, [(i, (i + 2 * shift) % count ^ flip) for i in r...  16.4 us
    pallas_call x1, Pallas kernels, late_rows(): pl.pallas_call(functools.partial(late_kernel, count, chunks, unit, pieces...  11.2 us
    ppermute x9, starting transfers between devices, shifted(): lax.ppermute(value, axis, [(i, (i + 2 * shift) % count ^ flip) for i in r...  8.13 us
    ppermute x10, starting transfers between devices, partner(): return lax.ppermute(value, axis, [(i, i ^ 1) for i in range(count)])  6.6 us
    pallas_call x1, Pallas kernels, own_call(): pl.pallas_call(functools.partial(own_kernel, chunks), out_shape=(shape_of...  5.46 us
    pallas_call x1, Pallas kernels, first_rows(): pl.pallas_call(functools.partial(first_kernel, count, chunks, unit), out_...  5.31 us
    unnamed x18, local copies, waits for them, and re-layouts  4.74 us
    pallas_call x1, Pallas kernels, mate_call(): pl.pallas_call(functools.partial(mate_kernel, count), out_shape=(shape_of...  4.74 us
  transfers between devices with their start and end apart: 19, of which 5 were waited for; matrix products, arithmetic and copies ran while one was open for 2% of the time, Pallas kernels for 41%

profile of v6, /device:TPU:0, one launch (start us, length us, event | category | flops | bytes accessed | tf_op | source)
XLA Modules:
  0.0 87.7 jit_solution(373706935588704782)
XLA Ops:
  2.7 3.8 %pack_feet.1 = (bf16[9,16,128]{2,1,0:T(8,128)(2,1)S(1)}, bf16[152,16,128]{2,1,0:T(8,128)(2,1)S(1)}, bf16[151,16,128]{2,1,0:T(8,128)(2,1)S(1)}) custom-call(s32[8,64]{1,0:T(8,128)S(1)} %bitcast.77, s32[2,1024]{1,0:T(2,128)S(1)} %copy-done.2, f32[1,1024]{1,0:T(1,128)S(1)} %bitcast.81, bf16[64,16,1024]{2,1,0:T(8,128)(2,1)} %feet_ref.3), custom_call_target="tpu_custom_call" | custom-call | flops 2700000000 | bytes 1000000 | tf_op jit(solution)/shard_map/pack_feet/pallas_call | solution.py:156
  7.1 2.6 %collective-permute-start.12 = (bf16[152,16,128]{2,1,0:T(8,128)(2,1)S(1)}, bf16[152,16,128]{2,1,0:T(8,128)(2,1)S(1)}, u32[]{:S(2)}, u32[]{:S(2)}) collective-permute-start(bf16[152,16,128]{2,1,0:T(8,128)(2,1)S(1)} %get-tuple-element.123.refs_1_), channel_id=1, source_target_pairs={{0,2},{1,3},{2,0},{3,1},{4,6},{5,7},{6,4},{7,5},{8,10},{9,11},{10,... | collective-permute-start | bytes 1867784 | tf_op jit(solution)/shard_map/ppermute | solution.py:805
  10.1 3.7 %own_start.1 = (bf16[1024,1024]{1,0:T(8,128)(2,1)S(1)}, bf16[1024,1024]{1,0:T(8,128)(2,1)S(1)}, f32[8,1024]{1,0:T(8,128)S(1)}) custom-call(bf16[9,16,128]{2,1,0:T(8,128)(2,1)S(1)} %get-tuple-element.122.refs_0_, bf16[152,16,128]{2,1,0:T(8,128)(2,1)S(1)} %get-tuple-element.123.refs_1_, bf16[151,16,128]{2,1,0:T(8,128)(2,1)S(1)} %get-tuple-element.124.refs_2_), custom_call_target="tpu_custom_call" | custom-call | flops 3600000000 | bytes 1000000 | tf_op jit(solution)/shard_map/own_start/pallas_call | solution.py:340
  13.8 1.3 %copy-done.4 = bf16[1024,1024]{1,0:T(8,128)(2,1)} copy-done((bf16[1024,1024]{1,0:T(8,128)(2,1)}, bf16[1024,1024]{1,0:T(8,128)(2,1)S(1)}, u32[]{:S(2)}) %copy-start.4) | copy-done | bytes 2097176
  15.1 1.3 %copy-done.6 = bf16[1024,1024]{1,0:T(8,128)(2,1)} copy-done((bf16[1024,1024]{1,0:T(8,128)(2,1)}, bf16[1024,1024]{1,0:T(8,128)(2,1)S(1)}, u32[]{:S(2)}) %copy-start.6) | copy-done | bytes 2097176
  16.5 2.2 %pack_panel.1.refs_6_ = bf16[90,16,128]{2,1,0:T(8,128)(2,1)S(1)} custom-call(s32[8,64]{1,0:T(8,128)S(1)} %bitcast.78, s32[8,64]{1,0:T(8,128)S(1)} %bitcast.79, s32[128]{0:T(128)S(1)} %copy-done.9, s32[1]{0:T(128)} %bitcast.12.group_ref.refs_2_, s32[1]{0:T(128)} %bitcast.13.member_ref.refs_3_, bf16[64,16,1024]{2,1,0:T(8,128)(2,1)} %feet_ref.3), custom_call_target="tpu_custom_call" | custom-call | flops 1800000000 | bytes 1000000 | tf_op jit(solution)/shard_map/pack_panel/pallas_call | solution.py:205
  18.7 1.0 %mixing.1.refs_7_.refs_15_ = bf16[256,768]{1,0:T(8,128)(2,1)S(1)} custom-call(f32[16,16]{1,0:T(8,128)} %time_ref.1), custom_call_target="tpu_custom_call" | custom-call | flops 900000000 | bytes 1000000 | tf_op jit(solution)/shard_map/mixing/pallas_call | solution.py:697
  19.9 5.2 %collective-permute-done.11.refs_0_ = bf16[9,16,128]{2,1,0:T(8,128)(2,1)S(1)} collective-permute-done((bf16[9,16,128]{2,1,0:T(8,128)(2,1)S(1)}, bf16[9,16,128]{2,1,0:T(8,128)(2,1)S(1)}, u32[]{:S(2)}, u32[]{:S(2)}) %collective-permute-start.11) | collective-permute-done | bytes 36896 | tf_op jit(solution)/shard_map/ppermute | solution.py:805
  25.0 1.7 %collective-permute-start.13 = (bf16[151,16,128]{2,1,0:T(8,128)(2,1)S(1)}, bf16[151,16,128]{2,1,0:T(8,128)(2,1)S(1)}, u32[]{:S(2)}, u32[]{:S(2)}) collective-permute-start(bf16[151,16,128]{2,1,0:T(8,128)(2,1)S(1)} %get-tuple-element.124.refs_2_), channel_id=1, source_target_pairs={{0,2},{1,3},{2,0},{3,1},{4,6},{5,7},{6,4},{7,5},{8,10},{9,11},{10,... | collective-permute-start | bytes 1855496 | tf_op jit(solution)/shard_map/ppermute | solution.py:805
  26.8 2.7 %far_start.1.refs_4_.refs_12_ = bf16[1024,1024]{1,0:T(8,128)(2,1)S(1)} custom-call(bf16[9,16,128]{2,1,0:T(8,128)(2,1)S(1)} %collective-permute-done.11.refs_0_, f32[8,1024]{1,0:T(8,128)S(1)} %get-tuple-element.350.refs_1_.refs_5_.refs_4_), custom_call_target="tpu_custom_call" | custom-call | flops 3600000000 | bytes 1000000 | tf_op jit(solution)/shard_map/far_start/pallas_call | solution.py:450
  29.5 1.6 %collective-permute-start.7 = (bf16[90,16,128]{2,1,0:T(8,128)(2,1)S(1)}, bf16[90,16,128]{2,1,0:T(8,128)(2,1)S(1)}, u32[]{:S(2)}, u32[]{:S(2)}) collective-permute-start(bf16[90,16,128]{2,1,0:T(8,128)(2,1)S(1)} %pack_panel.1.refs_6_), channel_id=1, source_target_pairs={{0,8},{4,12},{8,16},{12,20},{16,24},{20,28},{24,0},{28,4},{1,9},{5... | collective-permute-start | bytes 1105928 | tf_op jit(solution)/shard_map/ppermute | solution.py:805
  31.6 5.5 %own_product.1 = (f32[1024,1024]{1,0:T(8,128)S(1)}, bf16[1024,1024]{1,0:T(8,128)(2,1)S(1)}, bf16[1024,1024]{1,0:T(8,128)(2,1)S(1)}) custom-call(bf16[9,16,128]{2,1,0:T(8,128)(2,1)S(1)} %collective-permute-done.20.refs_0_, bf16[152,16,128]{2,1,0:T(8,128)(2,1)S(1)} %collective-permute-done.21.refs_1_, ...), custom_call_target="tpu_custom_call" | custom-call | flops 5400000000 | bytes 1000000 | tf_op jit(solution)/shard_map/own_product/pallas_call | solution.py:396
  37.1 1.6 %collective-permute-start.17 = (bf16[90,16,128]{2,1,0:T(8,128)(2,1)S(1)}, bf16[90,16,128]{2,1,0:T(8,128)(2,1)S(1)}, u32[]{:S(2)}, u32[]{:S(2)}) collective-permute-start(bf16[90,16,128]{2,1,0:T(8,128)(2,1)S(1)} %pack_panel.1.refs_6_), channel_id=1, source_target_pairs={{0,4},{4,0},{8,12},{12,8},{16,20},{20,16},{24,28},{28,24},{1,5},{5... | collective-permute-start | bytes 1105928 | tf_op jit(solution)/shard_map/ppermute | solution.py:801
  38.7 2.5 %collective-permute-done.7.refs_8_ = bf16[90,16,128]{2,1,0:T(8,128)(2,1)S(1)} collective-permute-done((bf16[90,16,128]{2,1,0:T(8,128)(2,1)S(1)}, bf16[90,16,128]{2,1,0:T(8,128)(2,1)S(1)}, u32[]{:S(2)}, u32[]{:S(2)}) %collective-permute-start.7) | collective-permute-done | bytes 368672 | tf_op jit(solution)/shard_map/ppermute | solution.py:805
  41.2 4.7 %mate_product.1 = (f32[1024,1024]{1,0:T(8,128)S(1)}, bf16[1024,1024]{1,0:T(8,128)(2,1)S(1)}) custom-call(bf16[9,16,128]{2,1,0:T(8,128)(2,1)S(1)} %collective-permute-done.14.refs_0_.refs_2_.refs_3_, f32[1024,1024]{1,0:T(8,128)S(1)} %get-tuple-element.128.refs_1_, bf16[1024,1024]{1,0:T(8,128)(2,1)S(1)} %get-tuple-element.129.refs_2_, ...), custom_call_target="tpu_custom_call", output_to_operand_aliasing={{0}: (1, {})} | custom-call | flops 4499999744 | bytes 1000000 | tf_op jit(solution)/shard_map/mate_product/pallas_call | solution.py:481
  46.0 1.6 %collective-permute-start.18 = (bf16[90,16,128]{2,1,0:T(8,128)(2,1)S(1)}, bf16[90,16,128]{2,1,0:T(8,128)(2,1)S(1)}, u32[]{:S(2)}, u32[]{:S(2)}) collective-permute-start(bf16[90,16,128]{2,1,0:T(8,128)(2,1)S(1)} %collective-permute-done.7.refs_8_), channel_id=1, source_target_pairs={{0,4},{4,0},{8,12},{12,8},{16,20},{20,16},{24,28},{28,24},{1,5},{5... | collective-permute-start | bytes 1105928 | tf_op jit(solution)/shard_map/ppermute | solution.py:801
  47.5 4.4 %collective-permute-done.8.refs_10_ = bf16[90,16,128]{2,1,0:T(8,128)(2,1)S(1)} collective-permute-done((bf16[90,16,128]{2,1,0:T(8,128)(2,1)S(1)}, bf16[90,16,128]{2,1,0:T(8,128)(2,1)S(1)}, u32[]{:S(2)}, u32[]{:S(2)}) %collective-permute-start.8) | collective-permute-done | bytes 368672 | tf_op jit(solution)/shard_map/ppermute | solution.py:805
  52.0 1.5 %collective-permute-start.19 = (bf16[90,16,128]{2,1,0:T(8,128)(2,1)S(1)}, bf16[90,16,128]{2,1,0:T(8,128)(2,1)S(1)}, u32[]{:S(2)}, u32[]{:S(2)}) collective-permute-start(bf16[90,16,128]{2,1,0:T(8,128)(2,1)S(1)} %collective-permute-done.8.refs_10_), channel_id=1, source_target_pairs={{0,4},{4,0},{8,12},{12,8},{16,20},{20,16},{24,28},{28,24},{1,5},{5... | collective-permute-start | bytes 1105928 | tf_op jit(solution)/shard_map/ppermute | solution.py:801
  53.5 5.3 %first_rows.1 = (bf16[64,16,1024]{2,1,0:T(8,128)(2,1)S(1)}, s32[1]{0:T(128)}) custom-call(bf16[9,16,128]{2,1,0:T(8,128)(2,1)S(1)} %collective-permute-done.11.refs_0_, bf16[152,16,128]{2,1,0:T(8,128)(2,1)S(1)} %collective-permute-done.12.refs_1_, bf16[9,16,128]{2,1,0:T(8,128)(2,1)S(1)} %collective-permute-done.14.refs_0_.refs_2_.refs_3_, ...), custom_call_target="tpu_custom_call" | custom-call | flops 6300000256 | bytes 1000000 | tf_op jit(solution)/shard_map/first_rows/pallas_call | solution.py:575
  58.8 4.3 %collective-permute-done.9.refs_0_ = bf16[90,16,128]{2,1,0:T(8,128)(2,1)S(1)} collective-permute-done((bf16[90,16,128]{2,1,0:T(8,128)(2,1)S(1)}, bf16[90,16,128]{2,1,0:T(8,128)(2,1)S(1)}, u32[]{:S(2)}, u32[]{:S(2)}) %collective-permute-start.9) | collective-permute-done | bytes 368672 | tf_op jit(solution)/shard_map/ppermute | solution.py:805
  63.7 1.7 %collective-permute-done.19.refs_11_ = bf16[90,16,128]{2,1,0:T(8,128)(2,1)S(1)} collective-permute-done((bf16[90,16,128]{2,1,0:T(8,128)(2,1)S(1)}, bf16[90,16,128]{2,1,0:T(8,128)(2,1)S(1)}, u32[]{:S(2)}, u32[]{:S(2)}) %collective-permute-start.19) | collective-permute-done | bytes 368672 | tf_op jit(solution)/shard_map/ppermute | solution.py:801
  65.4 11.2 %late_rows.1 = (bf16[64,16,1024]{2,1,0:T(8,128)(2,1)}, bf16[16,64,1024]{2,1,0:T(8,128)(2,1)S(1)}, f32[64,96]{1,0:T(8,128)S(1)}, s32[1]{0:T(128)}) custom-call(bf16[9,16,128]{2,1,0:T(8,128)(2,1)S(1)} %collective-permute-done.11.refs_0_, bf16[152,16,128]{2,1,0:T(8,128)(2,1)S(1)} %collective-permute-done.12.refs_1_, ...), custom_call_target="tpu_custom_call" | custom-call | flops 8099999744 | bytes 1000000 | tf_op jit(solution)/shard_map/late_rows/pallas_call | solution.py:652
  76.6 3.7 %panel_last.1 = f32[72,128]{1,0:T(8,128)S(1)} custom-call(bf16[90,16,128]{2,1,0:T(8,128)(2,1)S(1)} %collective-permute-done.9.refs_0_, bf16[90,16,128]{2,1,0:T(8,128)(2,1)S(1)} %collective-permute-done.10.refs_1_, s32[1]{0:T(128)} %bitcast.12.group_ref.refs_2_, s32[1]{0:T(128)} %bitcast.13.member_ref.refs_3_, s32[1,128]{1,0:T(1,128)S(1)} %bitcast.98, ...), custom_call_target="tpu_custom_call" | custom-call | flops 2700000000 | bytes 1000000 | tf_op jit(solution)/shard_map/panel_last/pallas_call | solution.py:782
  80.4 1.1 %collective-permute-start.24 = (f32[72,128]{1,0:T(8,128)S(1)}, f32[72,128]{1,0:T(8,128)S(1)}, u32[]{:S(2)}, u32[]{:S(2)}) collective-permute-start(f32[72,128]{1,0:T(8,128)S(1)} %panel_last.1), channel_id=1, source_target_pairs={{0,2},{1,3},{2,0},{3,1},{4,6},{5,7},{6,4},{7,5},{8,10},{9,11},{10,... | collective-permute-start | bytes 110600 | tf_op jit(solution)/shard_map/ppermute | solution.py:805
  (49 shorter events, 8.0 us)
Async XLA Ops:
  6.5 25.1 %collective-permute-start.21 = (bf16[152,16,128]{2,1,0:T(8,128)(2,1)S(1)}, bf16[152,16,128]{2,1,0:T(8,128)(2,1)S(1)}, u32[]{:S(2)}, u32[]{:S(2)}) collective-permute-start(bf16[152,16,128]{2,1,0:T(8,128)(2,1)S(1)} %get-tuple-element.123.refs_1_), channel_id=1, source_target_pairs={{0,1},{1,0},{2,3},{3,2},{4,5},{5,4},{6,7},{7,6},{8,9},{9,8},{10,11... | collective-permute-start | bytes 1867784 | tf_op jit(solution)/shard_map/ppermute | solution.py:801
  7.1 24.0 %collective-permute-start.12 = (bf16[152,16,128]{2,1,0:T(8,128)(2,1)S(1)}, bf16[152,16,128]{2,1,0:T(8,128)(2,1)S(1)}, u32[]{:S(2)}, u32[]{:S(2)}) collective-permute-start(bf16[152,16,128]{2,1,0:T(8,128)(2,1)S(1)} %get-tuple-element.123.refs_1_), channel_id=1, source_target_pairs={{0,2},{1,3},{2,0},{3,1},{4,6},{5,7},{6,4},{7,5},{8,10},{9,11},{10,... | collective-permute-start | bytes 1867784 | tf_op jit(solution)/shard_map/ppermute | solution.py:805
  9.6 21.5 %collective-permute-start.22 = (bf16[151,16,128]{2,1,0:T(8,128)(2,1)S(1)}, bf16[151,16,128]{2,1,0:T(8,128)(2,1)S(1)}, u32[]{:S(2)}, u32[]{:S(2)}) collective-permute-start(bf16[151,16,128]{2,1,0:T(8,128)(2,1)S(1)} %get-tuple-element.124.refs_2_), channel_id=1, source_target_pairs={{0,1},{1,0},{2,3},{3,2},{4,5},{5,4},{6,7},{7,6},{8,9},{9,8},{10,11... | collective-permute-start | bytes 1855496 | tf_op jit(solution)/shard_map/ppermute | solution.py:801
  9.8 6.7 %copy-start.1 = (s32[64,8]{0,1:T(8,128)S(1)}, s32[64,8]{0,1:T(8,128)}, u32[]{:S(2)}) copy-start(s32[64,8]{0,1:T(8,128)} %param.14) | copy-start | bytes 6148
  9.8 6.7 %copy-start.9 = (s32[128]{0:T(128)S(1)}, s32[128]{0:T(128)}, u32[]{:S(2)}) copy-start(s32[128]{0:T(128)} %index_ref.1) | copy-start | bytes 1540
  9.8 15.3 %collective-permute-start.11 = (bf16[9,16,128]{2,1,0:T(8,128)(2,1)S(1)}, bf16[9,16,128]{2,1,0:T(8,128)(2,1)S(1)}, u32[]{:S(2)}, u32[]{:S(2)}) collective-permute-start(bf16[9,16,128]{2,1,0:T(8,128)(2,1)S(1)} %get-tuple-element.122.refs_0_), channel_id=1, source_target_pairs={{0,2},{1,3},{2,0},{3,1},{4,6},{5,7},{6,4},{7,5},{8,10},{9,11},{10,... | collective-permute-start | bytes 110600 | tf_op jit(solution)/shard_map/ppermute | solution.py:805
  15.1 1.4 %copy-start.6 = (bf16[1024,1024]{1,0:T(8,128)(2,1)}, bf16[1024,1024]{1,0:T(8,128)(2,1)S(1)}, u32[]{:S(2)}) copy-start(bf16[1024,1024]{1,0:T(8,128)(2,1)S(1)} %get-tuple-element.127.refs_4_) | copy-start | bytes 6291460
  19.7 9.8 %collective-permute-start.20 = (bf16[9,16,128]{2,1,0:T(8,128)(2,1)S(1)}, bf16[9,16,128]{2,1,0:T(8,128)(2,1)S(1)}, u32[]{:S(2)}, u32[]{:S(2)}) collective-permute-start(bf16[9,16,128]{2,1,0:T(8,128)(2,1)S(1)} %get-tuple-element.122.refs_0_), channel_id=1, source_target_pairs={{0,1},{1,0},{2,3},{3,2},{4,5},{5,4},{6,7},{7,6},{8,9},{9,8},{10,11... | collective-permute-start | bytes 110600 | tf_op jit(solution)/shard_map/ppermute | solution.py:801
  25.0 16.1 %collective-permute-start.13 = (bf16[151,16,128]{2,1,0:T(8,128)(2,1)S(1)}, bf16[151,16,128]{2,1,0:T(8,128)(2,1)S(1)}, u32[]{:S(2)}, u32[]{:S(2)}) collective-permute-start(bf16[151,16,128]{2,1,0:T(8,128)(2,1)S(1)} %get-tuple-element.124.refs_2_), channel_id=1, source_target_pairs={{0,2},{1,3},{2,0},{3,1},{4,6},{5,7},{6,4},{7,5},{8,10},{9,11},{10,... | collective-permute-start | bytes 1855496 | tf_op jit(solution)/shard_map/ppermute | solution.py:805
  26.8 4.8 %copy-start.5 = (bf16[1024,1024]{1,0:T(8,128)(2,1)S(1)}, bf16[1024,1024]{1,0:T(8,128)(2,1)}, u32[]{:S(2)}) copy-start(bf16[1024,1024]{1,0:T(8,128)(2,1)} %copy-done.4) | copy-start | bytes 6291460
  26.8 4.8 %copy-start.7 = (bf16[1024,1024]{1,0:T(8,128)(2,1)S(1)}, bf16[1024,1024]{1,0:T(8,128)(2,1)}, u32[]{:S(2)}) copy-start(bf16[1024,1024]{1,0:T(8,128)(2,1)} %copy-done.6) | copy-start | bytes 6291460
  29.5 11.7 %collective-permute-start.7 = (bf16[90,16,128]{2,1,0:T(8,128)(2,1)S(1)}, bf16[90,16,128]{2,1,0:T(8,128)(2,1)S(1)}, u32[]{:S(2)}, u32[]{:S(2)}) collective-permute-start(bf16[90,16,128]{2,1,0:T(8,128)(2,1)S(1)} %pack_panel.1.refs_6_), channel_id=1, source_target_pairs={{0,8},{4,12},{8,16},{12,20},{16,24},{20,28},{24,0},{28,4},{1,9},{5... | collective-permute-start | bytes 1105928 | tf_op jit(solution)/shard_map/ppermute | solution.py:805
  31.1 10.1 %collective-permute-start.14 = (bf16[9,16,128]{2,1,0:T(8,128)(2,1)S(1)}, bf16[9,16,128]{2,1,0:T(8,128)(2,1)S(1)}, u32[]{:S(2)}, u32[]{:S(2)}) collective-permute-start(bf16[9,16,128]{2,1,0:T(8,128)(2,1)S(1)} %collective-permute-done.11.refs_0_), channel_id=1, source_target_pairs={{0,1},{1,0},{2,3},{3,2},{4,5},{5,4},{6,7},{7,6},{8,9},{9,8},{10,11... | collective-permute-start | bytes 110600 | tf_op jit(solution)/shard_map/ppermute | solution.py:801
  31.1 22.4 %collective-permute-start.15 = (bf16[152,16,128]{2,1,0:T(8,128)(2,1)S(1)}, bf16[152,16,128]{2,1,0:T(8,128)(2,1)S(1)}, u32[]{:S(2)}, u32[]{:S(2)}) collective-permute-start(bf16[152,16,128]{2,1,0:T(8,128)(2,1)S(1)} %collective-permute-done.12.refs_1_), channel_id=1, source_target_pairs={{0,1},{1,0},{2,3},{3,2},{4,5},{5,4},{6,7},{7,6},{8,9},{9,8},{10,11... | collective-permute-start | bytes 1867784 | tf_op jit(solution)/shard_map/ppermute | solution.py:801
  37.1 26.5 %collective-permute-start.17 = (bf16[90,16,128]{2,1,0:T(8,128)(2,1)S(1)}, bf16[90,16,128]{2,1,0:T(8,128)(2,1)S(1)}, u32[]{:S(2)}, u32[]{:S(2)}) collective-permute-start(bf16[90,16,128]{2,1,0:T(8,128)(2,1)S(1)} %pack_panel.1.refs_6_), channel_id=1, source_target_pairs={{0,4},{4,0},{8,12},{12,8},{16,20},{20,16},{24,28},{28,24},{1,5},{5... | collective-permute-start | bytes 1105928 | tf_op jit(solution)/shard_map/ppermute | solution.py:801
  41.2 10.8 %collective-permute-start.8 = (bf16[90,16,128]{2,1,0:T(8,128)(2,1)S(1)}, bf16[90,16,128]{2,1,0:T(8,128)(2,1)S(1)}, u32[]{:S(2)}, u32[]{:S(2)}) collective-permute-start(bf16[90,16,128]{2,1,0:T(8,128)(2,1)S(1)} %collective-permute-done.7.refs_8_), channel_id=1, source_target_pairs={{0,8},{4,12},{8,16},{12,20},{16,24},{20,28},{24,0},{28,4},{1,9},{5... | collective-permute-start | bytes 1105928 | tf_op jit(solution)/shard_map/ppermute | solution.py:805
  41.2 24.2 %collective-permute-start.16 = (bf16[151,16,128]{2,1,0:T(8,128)(2,1)S(1)}, bf16[151,16,128]{2,1,0:T(8,128)(2,1)S(1)}, u32[]{:S(2)}, u32[]{:S(2)}) collective-permute-start(bf16[151,16,128]{2,1,0:T(8,128)(2,1)S(1)} %collective-permute-done.13.refs_2_), channel_id=1, source_target_pairs={{0,1},{1,0},{2,3},{3,2},{4,5},{5,4},{6,7},{7,6},{8,9},{9,8},{10,11... | collective-permute-start | bytes 1855496 | tf_op jit(solution)/shard_map/ppermute | solution.py:801
  46.0 17.7 %collective-permute-start.18 = (bf16[90,16,128]{2,1,0:T(8,128)(2,1)S(1)}, bf16[90,16,128]{2,1,0:T(8,128)(2,1)S(1)}, u32[]{:S(2)}, u32[]{:S(2)}) collective-permute-start(bf16[90,16,128]{2,1,0:T(8,128)(2,1)S(1)} %collective-permute-done.7.refs_8_), channel_id=1, source_target_pairs={{0,4},{4,0},{8,12},{12,8},{16,20},{20,16},{24,28},{28,24},{1,5},{5... | collective-permute-start | bytes 1105928 | tf_op jit(solution)/shard_map/ppermute | solution.py:801
  52.0 13.4 %collective-permute-start.19 = (bf16[90,16,128]{2,1,0:T(8,128)(2,1)S(1)}, bf16[90,16,128]{2,1,0:T(8,128)(2,1)S(1)}, u32[]{:S(2)}, u32[]{:S(2)}) collective-permute-start(bf16[90,16,128]{2,1,0:T(8,128)(2,1)S(1)} %collective-permute-done.8.refs_10_), channel_id=1, source_target_pairs={{0,4},{4,0},{8,12},{12,8},{16,20},{20,16},{24,28},{28,24},{1,5},{5... | collective-permute-start | bytes 1105928 | tf_op jit(solution)/shard_map/ppermute | solution.py:801
  53.5 9.7 %collective-permute-start.9 = (bf16[90,16,128]{2,1,0:T(8,128)(2,1)S(1)}, bf16[90,16,128]{2,1,0:T(8,128)(2,1)S(1)}, u32[]{:S(2)}, u32[]{:S(2)}) collective-permute-start(bf16[90,16,128]{2,1,0:T(8,128)(2,1)S(1)} %collective-permute-done.8.refs_10_), channel_id=1, source_target_pairs={{0,8},{4,12},{8,16},{12,20},{16,24},{20,28},{24,0},{28,4},{1,9},{5... | collective-permute-start | bytes 1105928 | tf_op jit(solution)/shard_map/ppermute | solution.py:805
  63.1 13.4 %collective-permute-start.10 = (bf16[90,16,128]{2,1,0:T(8,128)(2,1)S(1)}, bf16[90,16,128]{2,1,0:T(8,128)(2,1)S(1)}, u32[]{:S(2)}, u32[]{:S(2)}) collective-permute-start(bf16[90,16,128]{2,1,0:T(8,128)(2,1)S(1)} %collective-permute-done.9.refs_0_), channel_id=1, source_target_pairs={{0,4},{4,0},{8,12},{12,8},{16,20},{20,16},{24,28},{28,24},{1,5},{5... | collective-permute-start | bytes 1105928 | tf_op jit(solution)/shard_map/ppermute | solution.py:801
  80.3 2.5 %collective-permute-start.23 = (f32[72,128]{1,0:T(8,128)S(1)}, f32[72,128]{1,0:T(8,128)S(1)}, u32[]{:S(2)}, u32[]{:S(2)}) collective-permute-start(f32[72,128]{1,0:T(8,128)S(1)} %panel_last.1), channel_id=1, source_target_pairs={{0,1},{1,0},{2,3},{3,2},{4,5},{5,4},{6,7},{7,6},{8,9},{9,8},{10,11... | collective-permute-start | bytes 110600 | tf_op jit(solution)/shard_map/ppermute | solution.py:805
  80.4 4.3 %collective-permute-start.24 = (f32[72,128]{1,0:T(8,128)S(1)}, f32[72,128]{1,0:T(8,128)S(1)}, u32[]{:S(2)}, u32[]{:S(2)}) collective-permute-start(f32[72,128]{1,0:T(8,128)S(1)} %panel_last.1), channel_id=1, source_target_pairs={{0,2},{1,3},{2,0},{3,1},{4,6},{5,7},{6,4},{7,5},{8,10},{9,11},{10,... | collective-permute-start | bytes 110600 | tf_op jit(solution)/shard_map/ppermute | solution.py:805
  81.5 4.4 %collective-permute-start.25 = (f32[72,128]{1,0:T(8,128)S(1)}, f32[72,128]{1,0:T(8,128)S(1)}, u32[]{:S(2)}, u32[]{:S(2)}) collective-permute-start(f32[72,128]{1,0:T(8,128)S(1)} %panel_last.1), channel_id=1, source_target_pairs={{0,3},{1,2},{2,1},{3,0},{4,7},{5,6},{6,5},{7,4},{8,11},{9,10},{10,... | collective-permute-start | bytes 110600 | tf_op jit(solution)/shard_map/ppermute | solution.py:805
  (4 other events, 3.4 us)

commit v7 on v6

--- a/solution.py
+++ b/solution.py
@@ -797,6 +797,26 @@
     )(*msgs, group[None], member[None], panel_index[None, :], error_var[None, :], turned, before, over)
 
 
+def finish_kernel(*refs):
+    *parts, out_ref, over_ref = refs
+    rows = out_ref.shape[0]
+    total = functools.reduce(jnp.add, [part[...] for part in parts])
+    out_ref[...] = total[:rows]
+    over_ref[0] = jnp.max(total[rows:]).astype(I32)
+
+
+def finish(parts, rows):
+    return pl.pallas_call(
+        finish_kernel,
+        out_shape=(shape_of((rows, parts[0].shape[1]), F32), shape_of((1,), I32)),
+        in_specs=[VMEM] * len(parts),
+        out_specs=(VMEM, SMEM),
+        compiler_params=params(8),
+        cost_estimate=cost(1),
+        name="finish",
+    )(*parts)
+
+
 def partner(value, axis, count):
     return lax.ppermute(value, axis, [(i, i ^ 1) for i in range(count)])
 
@@ -898,9 +918,7 @@
     part = panel_last(messages[cut:], turned, each, group, member, panel_index, error_var, before, over)
 
     part, late_group, late_mask = lax.optimization_barrier((part, group, mask))
-    parts = cell_parts(part, cells)
-    total = add_up([value[:obs_rows] for value in parts])
-    over = add_up([value[obs_rows, 0] for value in parts])
+    total, over = finish(cell_parts(part, cells), obs_rows)
 
     def again(carry):
         wanted = carry[0]
@@ -915,7 +933,7 @@
         on_diagonal = (positions[:, None] == panel_index[None, :]).astype(F32)
         return jnp.bool_(False), cov_product, row_major(total + error_var[:, None] * on_diagonal)
 
-    carry = (over > 0, cov_product, row_major(total))
+    carry = (over[0] > 0, cov_product, total)
     return lax.while_loop(lambda carry: carry[0], again, carry)[1:]
 
 

time: 88.2 us -> 87 us (0.986)
  waiting for transfers between devices: 18.2 us -> 20.8 us
  local copies, waits for them, and re-layouts: 6.94 us -> 4.82 us
  between operations: 3.44 us -> 1.61 us
    ppermute x9, waiting for transfers between devices: 16.4 us -> 19 us  [shifted(): lax.ppermute(value, axis, [(i, (i + 2 * shift) % count ^ flip) for i in r...]
    slice x4 -> x0, local copies, waits for them, and re-layouts: 2.11 us -> none  [body(): over = add_up([value[obs_rows, 0] for value in parts])]
  transfers between devices with their start and end apart: 19 -> 19, of which waited for: 5 -> 7; matrix products, arithmetic and copies ran while one was open for 2% -> 0% of each run, Pallas kernels for 41% -> 42%
where the time goes in v7:
time: 87 us; the launch traced here: 86.6 us
  Pallas kernels  44.4 us (51%)
  waiting for transfers between devices  20.8 us (24%)
  starting transfers between devices  14.7 us (17%)
  local copies, waits for them, and re-layouts  4.82 us (6%)
  between operations  1.61 us (2%)
    ppermute x9, waiting for transfers between devices, shifted(): lax.ppermute(value, axis, [(i, (i + 2 * shift) % count ^ flip) for i in r...  19 us
    pallas_call x1, Pallas kernels, late_rows(): pl.pallas_call(functools.partial(late_kernel, count, chunks, unit, pieces...  11.1 us
    ppermute x9, starting transfers between devices, shifted(): lax.ppermute(value, axis, [(i, (i + 2 * shift) % count ^ flip) for i in r...  8.13 us
    ppermute x10, starting transfers between devices, partner(): return lax.ppermute(value, axis, [(i, i ^ 1) for i in range(count)])  6.61 us
    pallas_call x1, Pallas kernels, own_call(): pl.pallas_call(functools.partial(own_kernel, chunks), out_shape=(shape_of...  5.46 us
    pallas_call x1, Pallas kernels, first_rows(): pl.pallas_call(functools.partial(first_kernel, count, chunks, unit), out_...  5.31 us
    pallas_call x1, Pallas kernels, mate_call(): pl.pallas_call(functools.partial(mate_kernel, count), out_shape=(shape_of...  4.74 us
    unnamed x18, local copies, waits for them, and re-layouts  4.74 us
  transfers between devices with their start and end apart: 19, of which 7 were waited for; matrix products, arithmetic and copies ran while one was open for 0% of the time, Pallas kernels for 42%

profile of v7, /device:TPU:0, one launch (start us, length us, event | category | flops | bytes accessed | tf_op | source)
XLA Modules:
  0.0 86.6 jit_solution(2307930587751930869)
XLA Ops:
  2.7 3.8 %pack_feet.1 = (bf16[9,16,128]{2,1,0:T(8,128)(2,1)S(1)}, bf16[152,16,128]{2,1,0:T(8,128)(2,1)S(1)}, bf16[151,16,128]{2,1,0:T(8,128)(2,1)S(1)}) custom-call(s32[8,64]{1,0:T(8,128)S(1)} %bitcast.77, s32[2,1024]{1,0:T(2,128)S(1)} %copy-done.2, f32[1,1024]{1,0:T(1,128)S(1)} %bitcast.81, bf16[64,16,1024]{2,1,0:T(8,128)(2,1)} %feet_ref.3), custom_call_target="tpu_custom_call" | custom-call | flops 2700000000 | bytes 1000000 | tf_op jit(solution)/shard_map/pack_feet/pallas_call | solution.py:156
  7.1 2.6 %collective-permute-start.12 = (bf16[152,16,128]{2,1,0:T(8,128)(2,1)S(1)}, bf16[152,16,128]{2,1,0:T(8,128)(2,1)S(1)}, u32[]{:S(2)}, u32[]{:S(2)}) collective-permute-start(bf16[152,16,128]{2,1,0:T(8,128)(2,1)S(1)} %get-tuple-element.125.refs_1_), channel_id=1, source_target_pairs={{0,2},{1,3},{2,0},{3,1},{4,6},{5,7},{6,4},{7,5},{8,10},{9,11},{10,... | collective-permute-start | bytes 1867784 | tf_op jit(solution)/shard_map/ppermute | solution.py:825
  10.1 3.7 %own_start.1 = (bf16[1024,1024]{1,0:T(8,128)(2,1)S(1)}, bf16[1024,1024]{1,0:T(8,128)(2,1)S(1)}, f32[8,1024]{1,0:T(8,128)S(1)}) custom-call(bf16[9,16,128]{2,1,0:T(8,128)(2,1)S(1)} %get-tuple-element.124.refs_0_, bf16[152,16,128]{2,1,0:T(8,128)(2,1)S(1)} %get-tuple-element.125.refs_1_, bf16[151,16,128]{2,1,0:T(8,128)(2,1)S(1)} %get-tuple-element.126.refs_2_), custom_call_target="tpu_custom_call" | custom-call | flops 3600000000 | bytes 1000000 | tf_op jit(solution)/shard_map/own_start/pallas_call | solution.py:340
  13.8 1.3 %copy-done.4 = bf16[1024,1024]{1,0:T(8,128)(2,1)} copy-done((bf16[1024,1024]{1,0:T(8,128)(2,1)}, bf16[1024,1024]{1,0:T(8,128)(2,1)S(1)}, u32[]{:S(2)}) %copy-start.4) | copy-done | bytes 2097176
  15.1 1.3 %copy-done.6 = bf16[1024,1024]{1,0:T(8,128)(2,1)} copy-done((bf16[1024,1024]{1,0:T(8,128)(2,1)}, bf16[1024,1024]{1,0:T(8,128)(2,1)S(1)}, u32[]{:S(2)}) %copy-start.6) | copy-done | bytes 2097176
  16.4 2.2 %pack_panel.1.refs_6_ = bf16[90,16,128]{2,1,0:T(8,128)(2,1)S(1)} custom-call(s32[8,64]{1,0:T(8,128)S(1)} %bitcast.78, s32[8,64]{1,0:T(8,128)S(1)} %bitcast.79, s32[128]{0:T(128)S(1)} %copy-done.9, s32[1]{0:T(128)} %bitcast.12.group_ref.refs_2_, s32[1]{0:T(128)} %bitcast.13.member_ref.refs_3_, bf16[64,16,1024]{2,1,0:T(8,128)(2,1)} %feet_ref.3), custom_call_target="tpu_custom_call" | custom-call | flops 1800000000 | bytes 1000000 | tf_op jit(solution)/shard_map/pack_panel/pallas_call | solution.py:205
  19.9 5.2 %collective-permute-done.11.refs_0_ = bf16[9,16,128]{2,1,0:T(8,128)(2,1)S(1)} collective-permute-done((bf16[9,16,128]{2,1,0:T(8,128)(2,1)S(1)}, bf16[9,16,128]{2,1,0:T(8,128)(2,1)S(1)}, u32[]{:S(2)}, u32[]{:S(2)}) %collective-permute-start.11) | collective-permute-done | bytes 36896 | tf_op jit(solution)/shard_map/ppermute | solution.py:825
  25.0 1.7 %collective-permute-start.13 = (bf16[151,16,128]{2,1,0:T(8,128)(2,1)S(1)}, bf16[151,16,128]{2,1,0:T(8,128)(2,1)S(1)}, u32[]{:S(2)}, u32[]{:S(2)}) collective-permute-start(bf16[151,16,128]{2,1,0:T(8,128)(2,1)S(1)} %get-tuple-element.126.refs_2_), channel_id=1, source_target_pairs={{0,2},{1,3},{2,0},{3,1},{4,6},{5,7},{6,4},{7,5},{8,10},{9,11},{10,... | collective-permute-start | bytes 1855496 | tf_op jit(solution)/shard_map/ppermute | solution.py:825
  26.8 2.7 %far_start.1.refs_4_.refs_12_ = bf16[1024,1024]{1,0:T(8,128)(2,1)S(1)} custom-call(bf16[9,16,128]{2,1,0:T(8,128)(2,1)S(1)} %collective-permute-done.11.refs_0_, f32[8,1024]{1,0:T(8,128)S(1)} %get-tuple-element.354.refs_1_.refs_5_.refs_4_), custom_call_target="tpu_custom_call" | custom-call | flops 3600000000 | bytes 1000000 | tf_op jit(solution)/shard_map/far_start/pallas_call | solution.py:450
  29.5 1.6 %collective-permute-start.7 = (bf16[90,16,128]{2,1,0:T(8,128)(2,1)S(1)}, bf16[90,16,128]{2,1,0:T(8,128)(2,1)S(1)}, u32[]{:S(2)}, u32[]{:S(2)}) collective-permute-start(bf16[90,16,128]{2,1,0:T(8,128)(2,1)S(1)} %pack_panel.1.refs_6_), channel_id=1, source_target_pairs={{0,8},{4,12},{8,16},{12,20},{16,24},{20,28},{24,0},{28,4},{1,9},{5... | collective-permute-start | bytes 1105928 | tf_op jit(solution)/shard_map/ppermute | solution.py:825
  31.6 5.5 %own_product.1 = (f32[1024,1024]{1,0:T(8,128)S(1)}, bf16[1024,1024]{1,0:T(8,128)(2,1)S(1)}, bf16[1024,1024]{1,0:T(8,128)(2,1)S(1)}) custom-call(bf16[9,16,128]{2,1,0:T(8,128)(2,1)S(1)} %collective-permute-done.20.refs_0_, bf16[152,16,128]{2,1,0:T(8,128)(2,1)S(1)} %collective-permute-done.21.refs_1_, ...), custom_call_target="tpu_custom_call" | custom-call | flops 5400000000 | bytes 1000000 | tf_op jit(solution)/shard_map/own_product/pallas_call | solution.py:396
  37.1 1.6 %collective-permute-start.17 = (bf16[90,16,128]{2,1,0:T(8,128)(2,1)S(1)}, bf16[90,16,128]{2,1,0:T(8,128)(2,1)S(1)}, u32[]{:S(2)}, u32[]{:S(2)}) collective-permute-start(bf16[90,16,128]{2,1,0:T(8,128)(2,1)S(1)} %pack_panel.1.refs_6_), channel_id=1, source_target_pairs={{0,4},{4,0},{8,12},{12,8},{16,20},{20,16},{24,28},{28,24},{1,5},{5... | collective-permute-start | bytes 1105928 | tf_op jit(solution)/shard_map/ppermute | solution.py:821
  38.7 2.5 %collective-permute-done.7.refs_8_ = bf16[90,16,128]{2,1,0:T(8,128)(2,1)S(1)} collective-permute-done((bf16[90,16,128]{2,1,0:T(8,128)(2,1)S(1)}, bf16[90,16,128]{2,1,0:T(8,128)(2,1)S(1)}, u32[]{:S(2)}, u32[]{:S(2)}) %collective-permute-start.7) | collective-permute-done | bytes 368672 | tf_op jit(solution)/shard_map/ppermute | solution.py:825
  41.2 4.7 %mate_product.1 = (f32[1024,1024]{1,0:T(8,128)S(1)}, bf16[1024,1024]{1,0:T(8,128)(2,1)S(1)}) custom-call(bf16[9,16,128]{2,1,0:T(8,128)(2,1)S(1)} %collective-permute-done.14.refs_0_.refs_2_.refs_3_, f32[1024,1024]{1,0:T(8,128)S(1)} %get-tuple-element.130.refs_1_, bf16[1024,1024]{1,0:T(8,128)(2,1)S(1)} %get-tuple-element.131.refs_2_, ...), custom_call_target="tpu_custom_call", output_to_operand_aliasing={{0}: (1, {})} | custom-call | flops 4499999744 | bytes 1000000 | tf_op jit(solution)/shard_map/mate_product/pallas_call | solution.py:481
  46.0 1.6 %collective-permute-start.18 = (bf16[90,16,128]{2,1,0:T(8,128)(2,1)S(1)}, bf16[90,16,128]{2,1,0:T(8,128)(2,1)S(1)}, u32[]{:S(2)}, u32[]{:S(2)}) collective-permute-start(bf16[90,16,128]{2,1,0:T(8,128)(2,1)S(1)} %collective-permute-done.7.refs_8_), channel_id=1, source_target_pairs={{0,4},{4,0},{8,12},{12,8},{16,20},{20,16},{24,28},{28,24},{1,5},{5... | collective-permute-start | bytes 1105928 | tf_op jit(solution)/shard_map/ppermute | solution.py:821
  47.5 4.4 %collective-permute-done.8.refs_10_ = bf16[90,16,128]{2,1,0:T(8,128)(2,1)S(1)} collective-permute-done((bf16[90,16,128]{2,1,0:T(8,128)(2,1)S(1)}, bf16[90,16,128]{2,1,0:T(8,128)(2,1)S(1)}, u32[]{:S(2)}, u32[]{:S(2)}) %collective-permute-start.8) | collective-permute-done | bytes 368672 | tf_op jit(solution)/shard_map/ppermute | solution.py:825
  52.0 1.5 %collective-permute-start.19 = (bf16[90,16,128]{2,1,0:T(8,128)(2,1)S(1)}, bf16[90,16,128]{2,1,0:T(8,128)(2,1)S(1)}, u32[]{:S(2)}, u32[]{:S(2)}) collective-permute-start(bf16[90,16,128]{2,1,0:T(8,128)(2,1)S(1)} %collective-permute-done.8.refs_10_), channel_id=1, source_target_pairs={{0,4},{4,0},{8,12},{12,8},{16,20},{20,16},{24,28},{28,24},{1,5},{5... | collective-permute-start | bytes 1105928 | tf_op jit(solution)/shard_map/ppermute | solution.py:821
  53.5 5.3 %first_rows.1 = (bf16[64,16,1024]{2,1,0:T(8,128)(2,1)S(1)}, s32[1]{0:T(128)}) custom-call(bf16[9,16,128]{2,1,0:T(8,128)(2,1)S(1)} %collective-permute-done.11.refs_0_, bf16[152,16,128]{2,1,0:T(8,128)(2,1)S(1)} %collective-permute-done.12.refs_1_, bf16[9,16,128]{2,1,0:T(8,128)(2,1)S(1)} %collective-permute-done.14.refs_0_.refs_2_.refs_3_, ...), custom_call_target="tpu_custom_call" | custom-call | flops 6300000256 | bytes 1000000 | tf_op jit(solution)/shard_map/first_rows/pallas_call | solution.py:575
  58.8 4.3 %collective-permute-done.9.refs_0_ = bf16[90,16,128]{2,1,0:T(8,128)(2,1)S(1)} collective-permute-done((bf16[90,16,128]{2,1,0:T(8,128)(2,1)S(1)}, bf16[90,16,128]{2,1,0:T(8,128)(2,1)S(1)}, u32[]{:S(2)}, u32[]{:S(2)}) %collective-permute-start.9) | collective-permute-done | bytes 368672 | tf_op jit(solution)/shard_map/ppermute | solution.py:825
  63.7 1.7 %collective-permute-done.19.refs_11_ = bf16[90,16,128]{2,1,0:T(8,128)(2,1)S(1)} collective-permute-done((bf16[90,16,128]{2,1,0:T(8,128)(2,1)S(1)}, bf16[90,16,128]{2,1,0:T(8,128)(2,1)S(1)}, u32[]{:S(2)}, u32[]{:S(2)}) %collective-permute-start.19) | collective-permute-done | bytes 368672 | tf_op jit(solution)/shard_map/ppermute | solution.py:821
  65.4 11.1 %late_rows.1 = (bf16[64,16,1024]{2,1,0:T(8,128)(2,1)}, bf16[16,64,1024]{2,1,0:T(8,128)(2,1)S(1)}, f32[64,96]{1,0:T(8,128)S(1)}, s32[1]{0:T(128)}) custom-call(bf16[9,16,128]{2,1,0:T(8,128)(2,1)S(1)} %collective-permute-done.11.refs_0_, bf16[152,16,128]{2,1,0:T(8,128)(2,1)S(1)} %collective-permute-done.12.refs_1_, ...), custom_call_target="tpu_custom_call" | custom-call | flops 8099999744 | bytes 1000000 | tf_op jit(solution)/shard_map/late_rows/pallas_call | solution.py:652
  76.5 3.8 %panel_last.1.refs_0_ = f32[72,128]{1,0:T(8,128)S(1)} custom-call(bf16[90,16,128]{2,1,0:T(8,128)(2,1)S(1)} %collective-permute-done.9.refs_0_, bf16[90,16,128]{2,1,0:T(8,128)(2,1)S(1)} %collective-permute-done.10.refs_1_, s32[1]{0:T(128)} %bitcast.12.group_ref.refs_2_, s32[1]{0:T(128)} %bitcast.13.member_ref.refs_3_, s32[1,128]{1,0:T(1,128)S(1)} %bitcast.98, ...), custom_call_target="tpu_custom_call" | custom-call | flops 2700000000 | bytes 1000000 | tf_op jit(solution)/shard_map/panel_last/pallas_call | solution.py:782
  80.4 1.1 %collective-permute-start.24 = (f32[72,128]{1,0:T(8,128)S(1)}, f32[72,128]{1,0:T(8,128)S(1)}, u32[]{:S(2)}, u32[]{:S(2)}) collective-permute-start(f32[72,128]{1,0:T(8,128)S(1)} %panel_last.1.refs_0_), channel_id=1, source_target_pairs={{0,2},{1,3},{2,0},{3,1},{4,6},{5,7},{6,4},{7,5},{8,10},{9,11},{10,... | collective-permute-start | bytes 110600 | tf_op jit(solution)/shard_map/ppermute | solution.py:825
  82.3 2.1 %collective-permute-done.24.refs_2_ = f32[72,128]{1,0:T(8,128)S(1)} collective-permute-done((f32[72,128]{1,0:T(8,128)S(1)}, f32[72,128]{1,0:T(8,128)S(1)}, u32[]{:S(2)}, u32[]{:S(2)}) %collective-permute-start.24) | collective-permute-done | bytes 36896 | tf_op jit(solution)/shard_map/ppermute | solution.py:825
  (45 shorter events, 7.6 us)
Async XLA Ops:
  6.5 25.1 %collective-permute-start.21 = (bf16[152,16,128]{2,1,0:T(8,128)(2,1)S(1)}, bf16[152,16,128]{2,1,0:T(8,128)(2,1)S(1)}, u32[]{:S(2)}, u32[]{:S(2)}) collective-permute-start(bf16[152,16,128]{2,1,0:T(8,128)(2,1)S(1)} %get-tuple-element.125.refs_1_), channel_id=1, source_target_pairs={{0,1},{1,0},{2,3},{3,2},{4,5},{5,4},{6,7},{7,6},{8,9},{9,8},{10,11... | collective-permute-start | bytes 1867784 | tf_op jit(solution)/shard_map/ppermute | solution.py:821
  7.1 24.0 %collective-permute-start.12 = (bf16[152,16,128]{2,1,0:T(8,128)(2,1)S(1)}, bf16[152,16,128]{2,1,0:T(8,128)(2,1)S(1)}, u32[]{:S(2)}, u32[]{:S(2)}) collective-permute-start(bf16[152,16,128]{2,1,0:T(8,128)(2,1)S(1)} %get-tuple-element.125.refs_1_), channel_id=1, source_target_pairs={{0,2},{1,3},{2,0},{3,1},{4,6},{5,7},{6,4},{7,5},{8,10},{9,11},{10,... | collective-permute-start | bytes 1867784 | tf_op jit(solution)/shard_map/ppermute | solution.py:825
  9.6 21.5 %collective-permute-start.22 = (bf16[151,16,128]{2,1,0:T(8,128)(2,1)S(1)}, bf16[151,16,128]{2,1,0:T(8,128)(2,1)S(1)}, u32[]{:S(2)}, u32[]{:S(2)}) collective-permute-start(bf16[151,16,128]{2,1,0:T(8,128)(2,1)S(1)} %get-tuple-element.126.refs_2_), channel_id=1, source_target_pairs={{0,1},{1,0},{2,3},{3,2},{4,5},{5,4},{6,7},{7,6},{8,9},{9,8},{10,11... | collective-permute-start | bytes 1855496 | tf_op jit(solution)/shard_map/ppermute | solution.py:821
  9.8 6.7 %copy-start.1 = (s32[64,8]{0,1:T(8,128)S(1)}, s32[64,8]{0,1:T(8,128)}, u32[]{:S(2)}) copy-start(s32[64,8]{0,1:T(8,128)} %param.14) | copy-start | bytes 6148
  9.8 6.7 %copy-start.9 = (s32[128]{0:T(128)S(1)}, s32[128]{0:T(128)}, u32[]{:S(2)}) copy-start(s32[128]{0:T(128)} %index_ref.1) | copy-start | bytes 1540
  9.8 15.3 %collective-permute-start.11 = (bf16[9,16,128]{2,1,0:T(8,128)(2,1)S(1)}, bf16[9,16,128]{2,1,0:T(8,128)(2,1)S(1)}, u32[]{:S(2)}, u32[]{:S(2)}) collective-permute-start(bf16[9,16,128]{2,1,0:T(8,128)(2,1)S(1)} %get-tuple-element.124.refs_0_), channel_id=1, source_target_pairs={{0,2},{1,3},{2,0},{3,1},{4,6},{5,7},{6,4},{7,5},{8,10},{9,11},{10,... | collective-permute-start | bytes 110600 | tf_op jit(solution)/shard_map/ppermute | solution.py:825
  15.1 1.3 %copy-start.6 = (bf16[1024,1024]{1,0:T(8,128)(2,1)}, bf16[1024,1024]{1,0:T(8,128)(2,1)S(1)}, u32[]{:S(2)}) copy-start(bf16[1024,1024]{1,0:T(8,128)(2,1)S(1)} %get-tuple-element.129.refs_4_) | copy-start | bytes 6291460
  19.7 9.8 %collective-permute-start.20 = (bf16[9,16,128]{2,1,0:T(8,128)(2,1)S(1)}, bf16[9,16,128]{2,1,0:T(8,128)(2,1)S(1)}, u32[]{:S(2)}, u32[]{:S(2)}) collective-permute-start(bf16[9,16,128]{2,1,0:T(8,128)(2,1)S(1)} %get-tuple-element.124.refs_0_), channel_id=1, source_target_pairs={{0,1},{1,0},{2,3},{3,2},{4,5},{5,4},{6,7},{7,6},{8,9},{9,8},{10,11... | collective-permute-start | bytes 110600 | tf_op jit(solution)/shard_map/ppermute | solution.py:821
  25.0 16.1 %collective-permute-start.13 = (bf16[151,16,128]{2,1,0:T(8,128)(2,1)S(1)}, bf16[151,16,128]{2,1,0:T(8,128)(2,1)S(1)}, u32[]{:S(2)}, u32[]{:S(2)}) collective-permute-start(bf16[151,16,128]{2,1,0:T(8,128)(2,1)S(1)} %get-tuple-element.126.refs_2_), channel_id=1, source_target_pairs={{0,2},{1,3},{2,0},{3,1},{4,6},{5,7},{6,4},{7,5},{8,10},{9,11},{10,... | collective-permute-start | bytes 1855496 | tf_op jit(solution)/shard_map/ppermute | solution.py:825
  26.8 4.8 %copy-start.5 = (bf16[1024,1024]{1,0:T(8,128)(2,1)S(1)}, bf16[1024,1024]{1,0:T(8,128)(2,1)}, u32[]{:S(2)}) copy-start(bf16[1024,1024]{1,0:T(8,128)(2,1)} %copy-done.4) | copy-start | bytes 6291460
  26.8 4.8 %copy-start.7 = (bf16[1024,1024]{1,0:T(8,128)(2,1)S(1)}, bf16[1024,1024]{1,0:T(8,128)(2,1)}, u32[]{:S(2)}) copy-start(bf16[1024,1024]{1,0:T(8,128)(2,1)} %copy-done.6) | copy-start | bytes 6291460
  29.5 11.7 %collective-permute-start.7 = (bf16[90,16,128]{2,1,0:T(8,128)(2,1)S(1)}, bf16[90,16,128]{2,1,0:T(8,128)(2,1)S(1)}, u32[]{:S(2)}, u32[]{:S(2)}) collective-permute-start(bf16[90,16,128]{2,1,0:T(8,128)(2,1)S(1)} %pack_panel.1.refs_6_), channel_id=1, source_target_pairs={{0,8},{4,12},{8,16},{12,20},{16,24},{20,28},{24,0},{28,4},{1,9},{5... | collective-permute-start | bytes 1105928 | tf_op jit(solution)/shard_map/ppermute | solution.py:825
  31.1 10.1 %collective-permute-start.14 = (bf16[9,16,128]{2,1,0:T(8,128)(2,1)S(1)}, bf16[9,16,128]{2,1,0:T(8,128)(2,1)S(1)}, u32[]{:S(2)}, u32[]{:S(2)}) collective-permute-start(bf16[9,16,128]{2,1,0:T(8,128)(2,1)S(1)} %collective-permute-done.11.refs_0_), channel_id=1, source_target_pairs={{0,1},{1,0},{2,3},{3,2},{4,5},{5,4},{6,7},{7,6},{8,9},{9,8},{10,11... | collective-permute-start | bytes 110600 | tf_op jit(solution)/shard_map/ppermute | solution.py:821
  31.1 22.4 %collective-permute-start.15 = (bf16[152,16,128]{2,1,0:T(8,128)(2,1)S(1)}, bf16[152,16,128]{2,1,0:T(8,128)(2,1)S(1)}, u32[]{:S(2)}, u32[]{:S(2)}) collective-permute-start(bf16[152,16,128]{2,1,0:T(8,128)(2,1)S(1)} %collective-permute-done.12.refs_1_), channel_id=1, source_target_pairs={{0,1},{1,0},{2,3},{3,2},{4,5},{5,4},{6,7},{7,6},{8,9},{9,8},{10,11... | collective-permute-start | bytes 1867784 | tf_op jit(solution)/shard_map/ppermute | solution.py:821
  37.1 26.5 %collective-permute-start.17 = (bf16[90,16,128]{2,1,0:T(8,128)(2,1)S(1)}, bf16[90,16,128]{2,1,0:T(8,128)(2,1)S(1)}, u32[]{:S(2)}, u32[]{:S(2)}) collective-permute-start(bf16[90,16,128]{2,1,0:T(8,128)(2,1)S(1)} %pack_panel.1.refs_6_), channel_id=1, source_target_pairs={{0,4},{4,0},{8,12},{12,8},{16,20},{20,16},{24,28},{28,24},{1,5},{5... | collective-permute-start | bytes 1105928 | tf_op jit(solution)/shard_map/ppermute | solution.py:821
  41.2 10.8 %collective-permute-start.8 = (bf16[90,16,128]{2,1,0:T(8,128)(2,1)S(1)}, bf16[90,16,128]{2,1,0:T(8,128)(2,1)S(1)}, u32[]{:S(2)}, u32[]{:S(2)}) collective-permute-start(bf16[90,16,128]{2,1,0:T(8,128)(2,1)S(1)} %collective-permute-done.7.refs_8_), channel_id=1, source_target_pairs={{0,8},{4,12},{8,16},{12,20},{16,24},{20,28},{24,0},{28,4},{1,9},{5... | collective-permute-start | bytes 1105928 | tf_op jit(solution)/shard_map/ppermute | solution.py:825
  41.2 24.2 %collective-permute-start.16 = (bf16[151,16,128]{2,1,0:T(8,128)(2,1)S(1)}, bf16[151,16,128]{2,1,0:T(8,128)(2,1)S(1)}, u32[]{:S(2)}, u32[]{:S(2)}) collective-permute-start(bf16[151,16,128]{2,1,0:T(8,128)(2,1)S(1)} %collective-permute-done.13.refs_2_), channel_id=1, source_target_pairs={{0,1},{1,0},{2,3},{3,2},{4,5},{5,4},{6,7},{7,6},{8,9},{9,8},{10,11... | collective-permute-start | bytes 1855496 | tf_op jit(solution)/shard_map/ppermute | solution.py:821
  46.0 17.7 %collective-permute-start.18 = (bf16[90,16,128]{2,1,0:T(8,128)(2,1)S(1)}, bf16[90,16,128]{2,1,0:T(8,128)(2,1)S(1)}, u32[]{:S(2)}, u32[]{:S(2)}) collective-permute-start(bf16[90,16,128]{2,1,0:T(8,128)(2,1)S(1)} %collective-permute-done.7.refs_8_), channel_id=1, source_target_pairs={{0,4},{4,0},{8,12},{12,8},{16,20},{20,16},{24,28},{28,24},{1,5},{5... | collective-permute-start | bytes 1105928 | tf_op jit(solution)/shard_map/ppermute | solution.py:821
  52.0 13.4 %collective-permute-start.19 = (bf16[90,16,128]{2,1,0:T(8,128)(2,1)S(1)}, bf16[90,16,128]{2,1,0:T(8,128)(2,1)S(1)}, u32[]{:S(2)}, u32[]{:S(2)}) collective-permute-start(bf16[90,16,128]{2,1,0:T(8,128)(2,1)S(1)} %collective-permute-done.8.refs_10_), channel_id=1, source_target_pairs={{0,4},{4,0},{8,12},{12,8},{16,20},{20,16},{24,28},{28,24},{1,5},{5... | collective-permute-start | bytes 1105928 | tf_op jit(solution)/shard_map/ppermute | solution.py:821
  53.5 9.7 %collective-permute-start.9 = (bf16[90,16,128]{2,1,0:T(8,128)(2,1)S(1)}, bf16[90,16,128]{2,1,0:T(8,128)(2,1)S(1)}, u32[]{:S(2)}, u32[]{:S(2)}) collective-permute-start(bf16[90,16,128]{2,1,0:T(8,128)(2,1)S(1)} %collective-permute-done.8.refs_10_), channel_id=1, source_target_pairs={{0,8},{4,12},{8,16},{12,20},{16,24},{20,28},{24,0},{28,4},{1,9},{5... | collective-permute-start | bytes 1105928 | tf_op jit(solution)/shard_map/ppermute | solution.py:825
  63.1 13.3 %collective-permute-start.10 = (bf16[90,16,128]{2,1,0:T(8,128)(2,1)S(1)}, bf16[90,16,128]{2,1,0:T(8,128)(2,1)S(1)}, u32[]{:S(2)}, u32[]{:S(2)}) collective-permute-start(bf16[90,16,128]{2,1,0:T(8,128)(2,1)S(1)} %collective-permute-done.9.refs_0_), channel_id=1, source_target_pairs={{0,4},{4,0},{8,12},{12,8},{16,20},{20,16},{24,28},{28,24},{1,5},{5... | collective-permute-start | bytes 1105928 | tf_op jit(solution)/shard_map/ppermute | solution.py:821
  80.3 2.0 %collective-permute-start.23 = (f32[72,128]{1,0:T(8,128)S(1)}, f32[72,128]{1,0:T(8,128)S(1)}, u32[]{:S(2)}, u32[]{:S(2)}) collective-permute-start(f32[72,128]{1,0:T(8,128)S(1)} %panel_last.1.refs_0_), channel_id=1, source_target_pairs={{0,1},{1,0},{2,3},{3,2},{4,5},{5,4},{6,7},{7,6},{8,9},{9,8},{10,11... | collective-permute-start | bytes 110600 | tf_op jit(solution)/shard_map/ppermute | solution.py:825
  80.4 4.0 %collective-permute-start.24 = (f32[72,128]{1,0:T(8,128)S(1)}, f32[72,128]{1,0:T(8,128)S(1)}, u32[]{:S(2)}, u32[]{:S(2)}) collective-permute-start(f32[72,128]{1,0:T(8,128)S(1)} %panel_last.1.refs_0_), channel_id=1, source_target_pairs={{0,2},{1,3},{2,0},{3,1},{4,6},{5,7},{6,4},{7,5},{8,10},{9,11},{10,... | collective-permute-start | bytes 110600 | tf_op jit(solution)/shard_map/ppermute | solution.py:825
  81.4 3.4 %collective-permute-start.25 = (f32[72,128]{1,0:T(8,128)S(1)}, f32[72,128]{1,0:T(8,128)S(1)}, u32[]{:S(2)}, u32[]{:S(2)}) collective-permute-start(f32[72,128]{1,0:T(8,128)S(1)} %panel_last.1.refs_0_), channel_id=1, source_target_pairs={{0,3},{1,2},{2,1},{3,0},{4,7},{5,6},{6,5},{7,4},{8,11},{9,10},{10,... | collective-permute-start | bytes 110600 | tf_op jit(solution)/shard_map/ppermute | solution.py:825
  (4 other events, 3.4 us)
